TPU v7x, 32 devices: a whole 2x2x4 slice. The times are simulated.
32 devices in a mesh: rep: 4 (over x, core), shard: 8 (over z, y).
Axes of the slice: x: 2, y: 2, z: 4, core: 2. Of those that a mesh axis runs over, the one named last changes fastest.
Arguments:
- tokens: bfloat16 [8192, 768], P(('rep', 'shard')), may hold values from -6 to 6
- letters: bfloat16 [8192, 8, 768], P(('rep', 'shard')), may hold values from -6 to 6
- lengths: int32 [32], P(('rep', 'shard')), may hold values from 64 to 256, as said below
- counts: int32 [8192], P(('rep', 'shard')), may hold values from 1 to 8, as said below
- cot_token: bfloat16 [8192, 768], P(('rep', 'shard')), may hold values from -6 to 6
- cot_letter: bfloat16 [8192, 768], P(('rep', 'shard')), may hold values from -6 to 6
- project_weight: bfloat16 [768, 2304], P('shard'), may hold values from -0.21875 to 0.21875
- project_bias: bfloat16 [1536], P('shard'), may hold values from -1.75 to 1.75
- output_weight: bfloat16 [768, 768], P('shard'), may hold values from -1.5 to 1.5
- output_bias: bfloat16 [768], P('shard'), may hold values from -1.75 to 1.75
- first_gain: bfloat16 [768], P('shard'), may hold values from 0.5 to 1.5
- first_shift: bfloat16 [768], P('shard'), may hold values from -1.75 to 1.75
- up_weight: bfloat16 [768, 3072], P('shard'), may hold values from -0.21875 to 0.21875
- up_bias: bfloat16 [3072], P('shard'), may hold values from -1.75 to 1.75
- down_weight: bfloat16 [3072, 768], P('shard'), may hold values from -0.109375 to 0.109375
- down_bias: bfloat16 [768], P('shard'), may hold values from -1.75 to 1.75
- second_gain: bfloat16 [768], P('shard'), may hold values from 0.5 to 1.5
- second_shift: bfloat16 [768], P('shard'), may hold values from -1.75 to 1.75
- gates_input: bfloat16 [2, 768, 1152], P(None, 'shard'), may hold values from -0.21875 to 0.21875
- gates_hidden: bfloat16 [2, 384, 1152], P(None, 'shard'), may hold values from -0.3125 to 0.3125
- shift_input: bfloat16 [2, 1152], P(None, 'shard'), may hold values from -1.75 to 1.75
- shift_hidden: bfloat16 [2, 1152], P(None, 'shard'), may hold values from -1.75 to 1.75
- token_mixer: bfloat16 [768, 768], P('shard'), may hold values from -0.21875 to 0.21875
- token_offset: bfloat16 [768], P('shard'), may hold values from -1.75 to 1.75
- letter_mixer: bfloat16 [768, 768], P('shard'), may hold values from -0.21875 to 0.21875
- letter_offset: bfloat16 [768], P('shard'), may hold values from -1.75 to 1.75
- window_kernel: bfloat16 [3, 1536, 1536], P(None, 'shard'), may hold values from -0.09375 to 0.09375
- window_offset: bfloat16 [1536], P('shard'), may hold values from -1.75 to 1.75
- third_gain: bfloat16 [768], P('shard'), may hold values from 0.5 to 1.5
- third_shift: bfloat16 [768], P('shard'), may hold values from -1.75 to 1.75
- fourth_gain: bfloat16 [768], P('shard'), may hold values from 0.5 to 1.5
- fourth_shift: bfloat16 [768], P('shard'), may hold values from -1.75 to 1.75
Outputs:
- token_out: bfloat16 [8192, 768], P(('rep', 'shard'))
- letter_out: bfloat16 [8192, 768], P(('rep', 'shard'))
- tokens_grad: bfloat16 [8192, 768], P(('rep', 'shard'))
- letters_grad: bfloat16 [8192, 8, 768], P(('rep', 'shard'))
- project_weight_grad: float32 [768, 2304], P('shard')
- project_bias_grad: float32 [1536], P('shard')
- output_weight_grad: float32 [768, 768], P('shard')
- output_bias_grad: float32 [768], P('shard')
- first_gain_grad: float32 [768], P('shard')
- first_shift_grad: float32 [768], P('shard')
- up_weight_grad: float32 [768, 3072], P('shard')
- up_bias_grad: float32 [3072], P('shard')
- down_weight_grad: float32 [3072, 768], P('shard')
- down_bias_grad: float32 [768], P('shard')
- second_gain_grad: float32 [768], P('shard')
- second_shift_grad: float32 [768], P('shard')
- gates_input_grad: float32 [2, 768, 1152], P(None, 'shard')
- gates_hidden_grad: float32 [2, 384, 1152], P(None, 'shard')
- shift_input_grad: float32 [2, 1152], P(None, 'shard')
- shift_hidden_grad: float32 [2, 1152], P(None, 'shard')
- token_mixer_grad: float32 [768, 768], P('shard')
- token_offset_grad: float32 [768], P('shard')
- letter_mixer_grad: float32 [768, 768], P('shard')
- letter_offset_grad: float32 [768], P('shard')
- window_kernel_grad: float32 [3, 1536, 1536], P(None, 'shard')
- window_offset_grad: float32 [1536], P('shard')
- third_gain_grad: float32 [768], P('shard')
- third_shift_grad: float32 [768], P('shard')
- fourth_gain_grad: float32 [768], P('shard')
- fourth_shift_grad: float32 [768], P('shard')
Inputs may be any that keep to these rules, and one draw needn't show every extreme that they name: `lengths`: each sequence has at least 64 valid tokens, the first ones of its slots; the first sequence is full. `counts`: A token's characters fill its first slots; the first token of all has 8. Counts are given for padded tokens too.
All inputs are finite; a program needn't handle non-finite values.
Results may differ from a plain program's by a relative error of at most 0.023.
Values may be sent and summed in bfloat16 or wider, within the bound.
No kernel may reach another device: no remote copies, remote signals or barrier semaphores. Data moves between devices by JAX's collectives and lax.ppermute only.
A program may use at most 256 MiB of HBM per device.

v0:
```python
import jax
import jax.numpy as jnp
from jax import lax
from jax.sharding import PartitionSpec as P

HEADS = 12


EPS = 1e-05


def shortened(value):
    return jax.tree.map(lambda a: a.astype(jnp.bfloat16) if a.dtype == jnp.float32 else a, value)


def product(left, right):
    return jnp.dot(left, right, preferred_element_type=jnp.float32)


def left_product(left, right):
    return lax.dot_general(
        left, right, (((0,), (0,)), ((), ())), preferred_element_type=jnp.float32
    )


def right_product(left, right):
    return lax.dot_general(
        left, right, (((1,), (1,)), ((), ())), preferred_element_type=jnp.float32
    )


def column_sum(values):
    return jnp.sum(values.astype(jnp.float32), axis=0)


def normalize(values, gain, shift):
    center = jnp.mean(values, axis=-1, keepdims=True)
    centered = values - center
    spread = jnp.mean(centered * centered, axis=-1, keepdims=True)
    return centered * lax.rsqrt(spread + EPS) * gain + shift


def exact_gelu(values):
    return jax.nn.gelu(values, approximate=False)


def recurrent_cell(inputs, hidden_gates, carried):
    hidden_width = carried.shape[-1]
    reset = jax.nn.sigmoid(inputs[:, :hidden_width] + hidden_gates[:, :hidden_width])
    update = jax.nn.sigmoid(
        inputs[:, hidden_width : 2 * hidden_width]
        + hidden_gates[:, hidden_width : 2 * hidden_width]
    )
    candidate = jnp.tanh(
        inputs[:, 2 * hidden_width :] + reset * hidden_gates[:, 2 * hidden_width :]
    )
    return (1.0 - update) * candidate + update * carried


def shards(
    tokens,
    letters,
    lengths,
    counts,
    cot_token,
    cot_letter,
    project_weight,
    project_bias,
    output_weight,
    output_bias,
    first_gain,
    first_shift,
    up_weight,
    up_bias,
    down_weight,
    down_bias,
    second_gain,
    second_shift,
    gates_input,
    gates_hidden,
    shift_input,
    shift_hidden,
    token_mixer,
    token_offset,
    letter_mixer,
    letter_offset,
    window_kernel,
    window_offset,
    third_gain,
    third_shift,
    fourth_gain,
    fourth_shift,
):
    seq_rows, model_width = tokens.shape
    letter_slots = letters.shape[1]
    head_width = model_width // HEADS
    score_scale = float(head_width) ** (-0.5)
    row_valid = jnp.arange(seq_rows) < lengths[0]
    row_mask = row_valid.astype(jnp.float32)[:, None]
    key_valid = row_valid[None, None, :]
    letter_flat = letters.reshape(seq_rows * letter_slots, model_width)
    attention_block = (
        lax.all_gather(project_weight, "shard", axis=0, tiled=True),
        lax.all_gather(project_bias, "shard", axis=0, tiled=True),
        lax.all_gather(output_weight, "shard", axis=0, tiled=True),
        lax.all_gather(output_bias, "shard", axis=0, tiled=True),
        lax.all_gather(first_gain, "shard", axis=0, tiled=True),
        lax.all_gather(first_shift, "shard", axis=0, tiled=True),
    )
    full_project, full_pbias, full_output, full_obias, gain_one, shift_one = attention_block
    bias_full = jnp.concatenate(
        [
            full_pbias[:model_width],
            jnp.zeros((model_width,), full_pbias.dtype),
            full_pbias[model_width:],
        ]
    ).astype(jnp.float32)
    mixed = (product(tokens, full_project) + bias_full).astype(jnp.bfloat16)
    queries = mixed[:, :model_width].reshape(seq_rows, HEADS, head_width)
    key_rows = mixed[:, model_width : 2 * model_width].reshape(seq_rows, HEADS, head_width)
    value_rows = mixed[:, 2 * model_width :].reshape(seq_rows, HEADS, head_width)

    def masked_scores_of(query_part, key_part):
        raw_scores = (
            jnp.einsum("qhd,khd->hqk", query_part, key_part, preferred_element_type=jnp.float32)
            * score_scale
        )
        return jnp.where(key_valid, raw_scores, -1e30)

    masked_scores = masked_scores_of(queries, key_rows)
    row_peak = jnp.max(masked_scores, axis=-1, keepdims=True)
    log_total = row_peak + jnp.log(
        jnp.sum(jnp.exp(masked_scores - row_peak), axis=-1, keepdims=True)
    )
    probs_low = jnp.exp(masked_scores - log_total).astype(jnp.bfloat16)
    context = (
        jnp.einsum("hqk,khd->qhd", probs_low, value_rows, preferred_element_type=jnp.float32)
        .astype(jnp.bfloat16)
        .reshape(seq_rows, model_width)
    )
    attended = product(context, full_output) + full_obias.astype(jnp.float32)
    residual_one = tokens.astype(jnp.float32) + attended
    first = normalize(residual_one, gain_one.astype(jnp.float32), shift_one.astype(jnp.float32))
    feed_block = (
        lax.all_gather(up_weight, "shard", axis=0, tiled=True),
        lax.all_gather(up_bias, "shard", axis=0, tiled=True),
        lax.all_gather(down_weight, "shard", axis=0, tiled=True),
        lax.all_gather(down_bias, "shard", axis=0, tiled=True),
        lax.all_gather(second_gain, "shard", axis=0, tiled=True),
        lax.all_gather(second_shift, "shard", axis=0, tiled=True),
    )
    full_up, full_ubias, full_down, full_dbias, gain_two, shift_two = feed_block
    first_low = first.astype(jnp.bfloat16)
    upper = product(first_low, full_up) + full_ubias.astype(jnp.float32)
    activated = exact_gelu(upper).astype(jnp.bfloat16)
    residual_two = first + product(activated, full_down) + full_dbias.astype(jnp.float32)
    second = normalize(residual_two, gain_two.astype(jnp.float32), shift_two.astype(jnp.float32))
    letter_block = (
        lax.all_gather(gates_input, "shard", axis=1, tiled=True),
        lax.all_gather(gates_hidden, "shard", axis=1, tiled=True),
        lax.all_gather(shift_input, "shard", axis=1, tiled=True),
        lax.all_gather(shift_hidden, "shard", axis=1, tiled=True),
        lax.all_gather(token_mixer, "shard", axis=0, tiled=True),
        lax.all_gather(token_offset, "shard", axis=0, tiled=True),
        lax.all_gather(letter_mixer, "shard", axis=0, tiled=True),
        lax.all_gather(letter_offset, "shard", axis=0, tiled=True),
        lax.all_gather(window_kernel, "shard", axis=1, tiled=True),
        lax.all_gather(window_offset, "shard", axis=0, tiled=True),
        lax.all_gather(third_gain, "shard", axis=0, tiled=True),
        lax.all_gather(third_shift, "shard", axis=0, tiled=True),
        lax.all_gather(fourth_gain, "shard", axis=0, tiled=True),
        lax.all_gather(fourth_shift, "shard", axis=0, tiled=True),
    )
    (
        full_gin,
        full_ghid,
        full_sin,
        full_shid,
        full_tmix,
        full_toff,
        full_lmix,
        full_loff,
        full_kernel,
        full_koff,
        gain_three,
        shift_three,
        gain_four,
        shift_four,
    ) = letter_block
    hidden_width = full_ghid.shape[1]
    forward_order = list(range(letter_slots))
    reverse_order = list(range(letter_slots - 1, -1, -1))

    def run_direction(direction, step_order):
        gate_inputs = (
            product(letter_flat, full_gin[direction]) + full_sin[direction].astype(jnp.float32)
        ).reshape(seq_rows, letter_slots, 3 * hidden_width)
        carried = jnp.zeros((seq_rows, hidden_width), jnp.float32)
        saved_states = []
        for position in step_order:
            saved_states.append(carried)
            hidden_gates = product(carried.astype(jnp.bfloat16), full_ghid[direction]) + full_shid[
                direction
            ].astype(jnp.float32)
            fresh = recurrent_cell(gate_inputs[:, position], hidden_gates, carried)
            carried = jnp.where((position < counts)[:, None], fresh, carried)
        return (carried, gate_inputs, saved_states)

    forth_state, forth_inputs, forth_saved = run_direction(0, forward_order)
    back_state, back_inputs, back_saved = run_direction(1, reverse_order)
    pooled = jnp.concatenate([forth_state, back_state], axis=-1)
    second_low = second.astype(jnp.bfloat16)
    pooled_low = pooled.astype(jnp.bfloat16)
    token_side = product(second_low, full_tmix) + full_toff.astype(jnp.float32)
    letter_side = product(pooled_low, full_lmix) + full_loff.astype(jnp.float32)
    joined = (jnp.concatenate([token_side, letter_side], axis=-1) * row_mask).astype(jnp.bfloat16)
    padded = jnp.pad(joined, ((1, 1), (0, 0)))
    convolved = (
        product(padded[:-2], full_kernel[0])
        + product(padded[1:-1], full_kernel[1])
        + product(padded[2:], full_kernel[2])
        + full_koff.astype(jnp.float32)
    )
    widened = exact_gelu(convolved)
    residual_three = second + widened[:, :model_width]
    residual_four = pooled + widened[:, model_width:]
    token_out = (
        normalize(residual_three, gain_three.astype(jnp.float32), shift_three.astype(jnp.float32))
        * row_mask
    )
    letter_out = (
        normalize(residual_four, gain_four.astype(jnp.float32), shift_four.astype(jnp.float32))
        * row_mask
    )
    letter_back = (
        lax.all_gather(gates_input, "shard", axis=1, tiled=True),
        lax.all_gather(gates_hidden, "shard", axis=1, tiled=True),
        lax.all_gather(shift_input, "shard", axis=1, tiled=True),
        lax.all_gather(shift_hidden, "shard", axis=1, tiled=True),
        lax.all_gather(token_mixer, "shard", axis=0, tiled=True),
        lax.all_gather(token_offset, "shard", axis=0, tiled=True),
        lax.all_gather(letter_mixer, "shard", axis=0, tiled=True),
        lax.all_gather(letter_offset, "shard", axis=0, tiled=True),
        lax.all_gather(window_kernel, "shard", axis=1, tiled=True),
        lax.all_gather(window_offset, "shard", axis=0, tiled=True),
        lax.all_gather(third_gain, "shard", axis=0, tiled=True),
        lax.all_gather(third_shift, "shard", axis=0, tiled=True),
        lax.all_gather(fourth_gain, "shard", axis=0, tiled=True),
        lax.all_gather(fourth_shift, "shard", axis=0, tiled=True),
    )
    (
        back_gin,
        back_ghid,
        unused_sin,
        back_shid,
        back_tmix,
        unused_toff,
        back_lmix,
        unused_loff,
        back_kernel,
        unused_koff,
        back_gain_three,
        back_shift_three,
        back_gain_four,
        back_shift_four,
    ) = letter_back
    out_token_delta = cot_token.astype(jnp.float32) * row_mask
    out_letter_delta = cot_letter.astype(jnp.float32) * row_mask
    unused_three, pull_three = jax.vjp(
        normalize,
        residual_three,
        back_gain_three.astype(jnp.float32),
        back_shift_three.astype(jnp.float32),
    )
    delta_three, delta_gain_three, delta_shift_three = pull_three(out_token_delta)
    unused_four, pull_four = jax.vjp(
        normalize,
        residual_four,
        back_gain_four.astype(jnp.float32),
        back_shift_four.astype(jnp.float32),
    )
    delta_four, delta_gain_four, delta_shift_four = pull_four(out_letter_delta)
    unused_gelu, pull_gelu = jax.vjp(exact_gelu, convolved)
    delta_conv = pull_gelu(jnp.concatenate([delta_three, delta_four], axis=-1))[0].astype(
        jnp.bfloat16
    )
    delta_koff = column_sum(delta_conv)
    back_terms = [right_product(delta_conv, back_kernel[kernel_tap]) for kernel_tap in range(3)]
    delta_joined = (
        jnp.pad(back_terms[0][1:], ((0, 1), (0, 0)))
        + back_terms[1]
        + jnp.pad(back_terms[2][:-1], ((1, 0), (0, 0)))
    ) * row_mask
    delta_tside = delta_joined[:, :model_width].astype(jnp.bfloat16)
    delta_lside = delta_joined[:, model_width:].astype(jnp.bfloat16)
    delta_tmix = left_product(second_low, delta_tside)
    delta_toff = column_sum(delta_tside)
    delta_lmix = left_product(pooled_low, delta_lside)
    delta_loff = column_sum(delta_lside)
    delta_second = delta_three + right_product(delta_tside, back_tmix)
    delta_pooled = delta_four + right_product(delta_lside, back_lmix)

    def back_direction(direction, step_order, gate_inputs, saved_states, delta_carried):
        delta_inputs = [None] * letter_slots
        delta_hidden = jnp.zeros(back_ghid.shape[1:], jnp.float32)
        delta_hshift = jnp.zeros((3 * hidden_width,), jnp.float32)
        for turn in range(letter_slots - 1, -1, -1):
            position = step_order[turn]
            carried = saved_states[turn]
            active = (position < counts)[:, None]
            carried_low = carried.astype(jnp.bfloat16)
            hidden_gates = product(carried_low, back_ghid[direction]) + back_shid[direction].astype(
                jnp.float32
            )
            unused_cell, pullback = jax.vjp(
                recurrent_cell, gate_inputs[:, position], hidden_gates, carried
            )
            delta_in, delta_gates, delta_direct = pullback(jnp.where(active, delta_carried, 0.0))
            gates_low = delta_gates.astype(jnp.bfloat16)
            delta_hidden = delta_hidden + left_product(carried_low, gates_low)
            delta_hshift = delta_hshift + column_sum(gates_low)
            delta_carried = (
                jnp.where(active, 0.0, delta_carried)
                + delta_direct
                + right_product(gates_low, back_ghid[direction])
            )
            delta_inputs[position] = delta_in
        inputs_low = (
            jnp.stack(delta_inputs, axis=1)
            .astype(jnp.bfloat16)
            .reshape(seq_rows * letter_slots, 3 * hidden_width)
        )
        return (
            left_product(letter_flat, inputs_low),
            column_sum(inputs_low),
            delta_hidden,
            delta_hshift,
            right_product(inputs_low, back_gin[direction]),
        )

    forth_back = back_direction(
        0, forward_order, forth_inputs, forth_saved, delta_pooled[:, :hidden_width]
    )
    back_back = back_direction(
        1, reverse_order, back_inputs, back_saved, delta_pooled[:, hidden_width:]
    )
    letters_grad = (
        (forth_back[4] + back_back[4])
        .astype(jnp.bfloat16)
        .reshape(seq_rows, letter_slots, model_width)
    )
    gin_delta = jnp.stack([forth_back[0], back_back[0]])
    ghid_delta = jnp.stack([forth_back[2], back_back[2]])
    sin_delta = jnp.stack([forth_back[1], back_back[1]])
    shid_delta = jnp.stack([forth_back[3], back_back[3]])
    group_size = lax.axis_size("shard")
    conv_all = lax.all_gather(delta_conv, "shard", axis=0, tiled=True)
    joined_own = lax.all_to_all(joined, "shard", split_axis=1, concat_axis=0, tiled=True)
    own_width = joined_own.shape[1]
    conv_blocks = conv_all.reshape(group_size, seq_rows, conv_all.shape[1])
    joined_blocks = jnp.pad(
        joined_own.reshape(group_size, seq_rows, own_width), ((0, 0), (1, 1), (0, 0))
    )
    kernel_own = jnp.stack(
        [
            jnp.einsum(
                "nsc,nse->ce",
                joined_blocks[:, kernel_tap : kernel_tap + seq_rows],
                conv_blocks,
                preferred_element_type=jnp.float32,
            )
            for kernel_tap in range(3)
        ]
    )
    rest_owned = (
        lax.psum_scatter(
            gin_delta.astype(jnp.bfloat16), "shard", scatter_dimension=1, tiled=True
        ).astype(jnp.float32),
        lax.psum_scatter(
            ghid_delta.astype(jnp.bfloat16), "shard", scatter_dimension=1, tiled=True
        ).astype(jnp.float32),
        lax.psum_scatter(
            sin_delta.astype(jnp.bfloat16), "shard", scatter_dimension=1, tiled=True
        ).astype(jnp.float32),
        lax.psum_scatter(
            shid_delta.astype(jnp.bfloat16), "shard", scatter_dimension=1, tiled=True
        ).astype(jnp.float32),
        lax.psum_scatter(
            delta_tmix.astype(jnp.bfloat16), "shard", scatter_dimension=0, tiled=True
        ).astype(jnp.float32),
        lax.psum_scatter(
            delta_toff.astype(jnp.bfloat16), "shard", scatter_dimension=0, tiled=True
        ).astype(jnp.float32),
        lax.psum_scatter(
            delta_lmix.astype(jnp.bfloat16), "shard", scatter_dimension=0, tiled=True
        ).astype(jnp.float32),
        lax.psum_scatter(
            delta_loff.astype(jnp.bfloat16), "shard", scatter_dimension=0, tiled=True
        ).astype(jnp.float32),
        lax.psum_scatter(
            delta_koff.astype(jnp.bfloat16), "shard", scatter_dimension=0, tiled=True
        ).astype(jnp.float32),
        lax.psum_scatter(
            delta_gain_three.astype(jnp.bfloat16), "shard", scatter_dimension=0, tiled=True
        ).astype(jnp.float32),
        lax.psum_scatter(
            delta_shift_three.astype(jnp.bfloat16), "shard", scatter_dimension=0, tiled=True
        ).astype(jnp.float32),
        lax.psum_scatter(
            delta_gain_four.astype(jnp.bfloat16), "shard", scatter_dimension=0, tiled=True
        ).astype(jnp.float32),
        lax.psum_scatter(
            delta_shift_four.astype(jnp.bfloat16), "shard", scatter_dimension=0, tiled=True
        ).astype(jnp.float32),
    )
    letter_owned = tuple(rest_owned[:8]) + (kernel_own,) + tuple(rest_owned[8:])
    letter_summed = jax.tree.map(
        lambda part: part.astype(jnp.float32), lax.psum(shortened(letter_owned), "rep")
    )
    feed_back = (
        lax.all_gather(up_weight, "shard", axis=0, tiled=True),
        lax.all_gather(up_bias, "shard", axis=0, tiled=True),
        lax.all_gather(down_weight, "shard", axis=0, tiled=True),
        lax.all_gather(down_bias, "shard", axis=0, tiled=True),
        lax.all_gather(second_gain, "shard", axis=0, tiled=True),
        lax.all_gather(second_shift, "shard", axis=0, tiled=True),
    )
    back_up, unused_ubias, back_down, unused_dbias, back_gain_two, back_shift_two = feed_back
    unused_two, pull_two = jax.vjp(
        normalize,
        residual_two,
        back_gain_two.astype(jnp.float32),
        back_shift_two.astype(jnp.float32),
    )
    delta_two, delta_gain_two, delta_shift_two = pull_two(delta_second)
    delta_lowered = delta_two.astype(jnp.bfloat16)
    delta_down = left_product(activated, delta_lowered)
    delta_dbias = column_sum(delta_lowered)
    unused_act, pull_act = jax.vjp(exact_gelu, upper)
    delta_upper = pull_act(right_product(delta_lowered, back_down))[0].astype(jnp.bfloat16)
    delta_up = left_product(first_low, delta_upper)
    delta_ubias = column_sum(delta_upper)
    delta_first = delta_two + right_product(delta_upper, back_up)
    attention_back = (
        lax.all_gather(project_weight, "shard", axis=0, tiled=True),
        lax.all_gather(project_bias, "shard", axis=0, tiled=True),
        lax.all_gather(output_weight, "shard", axis=0, tiled=True),
        lax.all_gather(output_bias, "shard", axis=0, tiled=True),
        lax.all_gather(first_gain, "shard", axis=0, tiled=True),
        lax.all_gather(first_shift, "shard", axis=0, tiled=True),
    )
    back_project, unused_pbias, back_output, unused_obias, back_gain_one, back_shift_one = (
        attention_back
    )
    unused_one, pull_one = jax.vjp(
        normalize,
        residual_one,
        back_gain_one.astype(jnp.float32),
        back_shift_one.astype(jnp.float32),
    )
    delta_one, delta_gain_one, delta_shift_one = pull_one(delta_first)
    delta_attended = delta_one.astype(jnp.bfloat16)
    delta_output = left_product(context, delta_attended)
    delta_obias = column_sum(delta_attended)
    delta_context = (
        right_product(delta_attended, back_output)
        .astype(jnp.bfloat16)
        .reshape(seq_rows, HEADS, head_width)
    )
    probabilities = jnp.exp(masked_scores_of(queries, key_rows) - log_total)
    delta_values = jnp.einsum(
        "hqk,qhd->khd",
        probabilities.astype(jnp.bfloat16),
        delta_context,
        preferred_element_type=jnp.float32,
    )
    delta_probs = jnp.einsum(
        "qhd,khd->hqk", delta_context, value_rows, preferred_element_type=jnp.float32
    )
    delta_scores = (
        probabilities * (delta_probs - jnp.sum(probabilities * delta_probs, axis=-1, keepdims=True))
    ).astype(jnp.bfloat16)
    delta_queries = (
        jnp.einsum("hqk,khd->qhd", delta_scores, key_rows, preferred_element_type=jnp.float32)
        * score_scale
    )
    delta_keys = (
        jnp.einsum("hqk,qhd->khd", delta_scores, queries, preferred_element_type=jnp.float32)
        * score_scale
    )
    delta_mixed = jnp.concatenate(
        [
            delta_queries.reshape(seq_rows, model_width),
            delta_keys.reshape(seq_rows, model_width),
            delta_values.reshape(seq_rows, model_width),
        ],
        axis=-1,
    ).astype(jnp.bfloat16)
    delta_project = left_product(tokens, delta_mixed)
    delta_mixed_sum = column_sum(delta_mixed)
    delta_pbias = jnp.concatenate(
        [delta_mixed_sum[:model_width], delta_mixed_sum[2 * model_width :]]
    )
    tokens_grad = (delta_one + right_product(delta_mixed, back_project)).astype(jnp.bfloat16)
    token_owned = (
        lax.psum_scatter(
            delta_project.astype(jnp.bfloat16), "shard", scatter_dimension=0, tiled=True
        ).astype(jnp.float32),
        lax.psum_scatter(
            delta_pbias.astype(jnp.bfloat16), "shard", scatter_dimension=0, tiled=True
        ).astype(jnp.float32),
        lax.psum_scatter(
            delta_output.astype(jnp.bfloat16), "shard", scatter_dimension=0, tiled=True
        ).astype(jnp.float32),
        lax.psum_scatter(
            delta_obias.astype(jnp.bfloat16), "shard", scatter_dimension=0, tiled=True
        ).astype(jnp.float32),
        lax.psum_scatter(
            delta_gain_one.astype(jnp.bfloat16), "shard", scatter_dimension=0, tiled=True
        ).astype(jnp.float32),
        lax.psum_scatter(
            delta_shift_one.astype(jnp.bfloat16), "shard", scatter_dimension=0, tiled=True
        ).astype(jnp.float32),
        lax.psum_scatter(
            delta_up.astype(jnp.bfloat16), "shard", scatter_dimension=0, tiled=True
        ).astype(jnp.float32),
        lax.psum_scatter(
            delta_ubias.astype(jnp.bfloat16), "shard", scatter_dimension=0, tiled=True
        ).astype(jnp.float32),
        lax.psum_scatter(
            delta_down.astype(jnp.bfloat16), "shard", scatter_dimension=0, tiled=True
        ).astype(jnp.float32),
        lax.psum_scatter(
            delta_dbias.astype(jnp.bfloat16), "shard", scatter_dimension=0, tiled=True
        ).astype(jnp.float32),
        lax.psum_scatter(
            delta_gain_two.astype(jnp.bfloat16), "shard", scatter_dimension=0, tiled=True
        ).astype(jnp.float32),
        lax.psum_scatter(
            delta_shift_two.astype(jnp.bfloat16), "shard", scatter_dimension=0, tiled=True
        ).astype(jnp.float32),
    )
    token_summed = (
        lax.psum(token_owned[0].astype(jnp.bfloat16), "rep").astype(jnp.float32),
        lax.psum(token_owned[1].astype(jnp.bfloat16), "rep").astype(jnp.float32),
        lax.psum(token_owned[2].astype(jnp.bfloat16), "rep").astype(jnp.float32),
        lax.psum(token_owned[3].astype(jnp.bfloat16), "rep").astype(jnp.float32),
        lax.psum(token_owned[4].astype(jnp.bfloat16), "rep").astype(jnp.float32),
        lax.psum(token_owned[5].astype(jnp.bfloat16), "rep").astype(jnp.float32),
        lax.psum(token_owned[6].astype(jnp.bfloat16), "rep").astype(jnp.float32),
        lax.psum(token_owned[7].astype(jnp.bfloat16), "rep").astype(jnp.float32),
        lax.psum(token_owned[8].astype(jnp.bfloat16), "rep").astype(jnp.float32),
        lax.psum(token_owned[9].astype(jnp.bfloat16), "rep").astype(jnp.float32),
        lax.psum(token_owned[10].astype(jnp.bfloat16), "rep").astype(jnp.float32),
        lax.psum(token_owned[11].astype(jnp.bfloat16), "rep").astype(jnp.float32),
    )
    return (
        token_out.astype(jnp.bfloat16),
        letter_out.astype(jnp.bfloat16),
        tokens_grad,
        letters_grad,
        token_summed[0],
        token_summed[1],
        token_summed[2],
        token_summed[3],
        token_summed[4],
        token_summed[5],
        token_summed[6],
        token_summed[7],
        token_summed[8],
        token_summed[9],
        token_summed[10],
        token_summed[11],
        letter_summed[0],
        letter_summed[1],
        letter_summed[2],
        letter_summed[3],
        letter_summed[4],
        letter_summed[5],
        letter_summed[6],
        letter_summed[7],
        letter_summed[8],
        letter_summed[9],
        letter_summed[10],
        letter_summed[11],
        letter_summed[12],
        letter_summed[13],
    )


def solution(mesh):
    placed = (
        P(("rep", "shard"), None),
        P(("rep", "shard"), None, None),
        P(("rep", "shard")),
        P(("rep", "shard")),
        P(("rep", "shard"), None),
        P(("rep", "shard"), None),
        P("shard", None),
        P("shard"),
        P("shard", None),
        P("shard"),
        P("shard"),
        P("shard"),
        P("shard", None),
        P("shard"),
        P("shard", None),
        P("shard"),
        P("shard"),
        P("shard"),
        P(None, "shard", None),
        P(None, "shard", None),
        P(None, "shard"),
        P(None, "shard"),
        P("shard", None),
        P("shard"),
        P("shard", None),
        P("shard"),
        P(None, "shard", None),
        P("shard"),
        P("shard"),
        P("shard"),
        P("shard"),
        P("shard"),
    )
    return jax.shard_map(
        shards,
        mesh=mesh,
        in_specs=placed,
        out_specs=(
            P(("rep", "shard"), None),
            P(("rep", "shard"), None),
            P(("rep", "shard"), None),
            P(("rep", "shard"), None, None),
            P("shard", None),
            P("shard"),
            P("shard", None),
            P("shard"),
            P("shard"),
            P("shard"),
            P("shard", None),
            P("shard"),
            P("shard", None),
            P("shard"),
            P("shard"),
            P("shard"),
            P(None, "shard", None),
            P(None, "shard", None),
            P(None, "shard"),
            P(None, "shard"),
            P("shard", None),
            P("shard"),
            P("shard", None),
            P("shard"),
            P(None, "shard", None),
            P("shard"),
            P("shard"),
            P("shard"),
            P("shard"),
            P("shard"),
        ),
        check_vma=False,
    )
```

profile of v0, /device:TPU:0, one launch (start us, length us, event | category | flops | bytes accessed | tf_op | source)
XLA Modules:
  0.0 1827.0 jit_solution(16758076236052966912)
XLA Ops:
  18.4 39.6 %all-reduce.99 = (bf16[768]{0:T(1024)(128)(2,1)S(1)}, bf16[768]{0:T(1024)(128)(2,1)S(1)}, bf16[1536]{0:T(1024)(128)(2,1)S(1)}, bf16[768]{0:T(1024)(128)(2,1)S(1)...) all-reduce(bf16[768]{0:T(1024)(128)(2,1)S(1)} %dynamic-update-slice, ...), channel_id=1, replica_groups=mesh['rep'=4,'shard'=8] {'shard'}, use_global_device_ids=true, to_apply=%add.76 | all-reduce | flops 10752 | bytes 43008
  59.8 16.4 all-gather.2
  76.4 18.7 %all-gather.1 = bf16[8,144,2]{1,2,0:T(2,128)(2,1)S(1)} all-gather(bf16[1,144,2]{1,2,0:T(2,128)(2,1)S(1)} %bitcast.437), channel_id=1, replica_groups=mesh['rep'=4,'shard'=8] {'shard'}, dimensions={0}, use_global_device_ids=true | all-gather | bytes 5184 | tf_op jit(solution)/shard_map/all_gather | solution.py:161
  96.4 27.3 %all-gather = bf16[8,1,384]{2,1,0:T(2,128)(2,1)S(1)} all-gather(bf16[1,1,384]{2,1,0:T(2,128)(2,1)S(1)} %reshape.493), channel_id=1, replica_groups=mesh['rep'=4,'shard'=8] {'shard'}, dimensions={0}, use_global_device_ids=true | all-gather | bytes 6912 | tf_op jit(solution)/shard_map/all_gather | solution.py:146
  130.9 2.8 convolution_add_fusion.31
  135.2 8.1 add_bitcast_fusion.1
  143.2 29.7 %fusion.507 = (f32[256,1,1152]{2,1,0:T(1,128)}, f32[256,1,1152]{2,1,0:T(1,128)}, f32[256,1,1152]{2,1,0:T(1,128)}, f32[256,1,1152]{2,1,0:T(1,128)}, f32[256,1,115...) fusion(f32[256,8,1152]{2,1,0:T(8,128)} %add_bitcast_fusion.1), kind=kLoop, calls=%fused_computation.844 | loop fusion | bytes 18874368 | tf_op jit(solution)/shard_map/slice | solution.py:205
  173.0 2.5 copy.221
  185.7 6.6 add_bitcast_fusion
  192.3 30.0 %fusion.508 = (f32[256,1,1152]{2,1,0:T(1,128)}, f32[256,1,1152]{2,1,0:T(1,128)}, f32[256,1,1152]{2,1,0:T(1,128)}, f32[256,1,1152]{2,1,0:T(1,128)}, f32[256,1,115...) fusion(f32[256,8,1152]{2,1,0:T(8,128)} %add_bitcast_fusion), kind=kLoop, calls=%fused_computation.845 | loop fusion | bytes 18874368 | tf_op jit(solution)/shard_map/slice | solution.py:205
  222.3 2.5 copy.213
  234.5 3.1 fusion.13
  289.4 2.9 convolution_add_fusion.34
  292.3 62.2 %all-gather.18.cloned.1.call-done = bf16[768,3072]{1,0:T(8,128)(2,1)} async-done(((bf16[96,3072]{1,0:T(8,128)(2,1)}), bf16[768,3072]{1,0:T(8,128)(2,1)}) %all-gather.18.cloned.1.call-update) | async-done | bytes 4718608 | tf_op jit(solution)/shard_map/all_gather | solution.py:145
  354.5 11.8 multiply_convert_fusion.1
  366.3 68.1 %all-gather.20.cloned.1.call-done = bf16[3072,768]{1,0:T(8,128)(2,1)} async-done(((bf16[384,768]{1,0:T(8,128)(2,1)}), bf16[3072,768]{1,0:T(8,128)(2,1)}) %all-gather.20.cloned.1.call-update) | async-done | bytes 4718608 | tf_op jit(solution)/shard_map/all_gather | solution.py:147
  434.4 4.5 fusion.514
  441.2 34.9 %all-gather.22.cloned.1.call-done = bf16[768,768]{1,0:T(8,128)(2,1)} async-done(((bf16[96,768]{1,0:T(8,128)(2,1)}), bf16[768,768]{1,0:T(8,128)(2,1)}) %all-gather.22.cloned.1.call-update) | async-done | bytes 1179664 | tf_op jit(solution)/shard_map/all_gather | solution.py:163
  480.9 191.4 %all-gather.30.cloned.1.call-done = bf16[3,1536,1536]{2,1,0:T(8,128)(2,1)} async-done(((bf16[3,192,1536]{2,1,0:T(8,128)(2,1)}), bf16[3,1536,1536]{2,1,0:T(8,128)(2,1)}) %all-gather.30.cloned.1.call-update) | async-done | bytes 14155792 | tf_op jit(solution)/shard_map/all_gather | solution.py:167
  672.3 4.0 fusion.8
  676.3 3.8 fusion.34
  680.2 7.0 multiply_multiply_fusion.10
  693.9 4.1 fusion.11
  697.9 3.8 fusion.7
  701.8 4.0 fusion.41
  760.4 4.4 fusion.27
  764.9 4.2 fusion.28
  771.2 10.6 copy.150
  784.0 7.9 fusion.467
  792.0 5.2 multiply_reduce_fusion.4
  803.1 3.5 multiply_reduce_fusion
  811.4 2.9 fusion.6
  814.3 5.8 copy.161
  820.7 2.6 convolution_convert_fusion.5
  823.4 2.8 convolution_convert_fusion.3
  826.2 2.9 convolution_convert_fusion.4
  829.1 2.9 fusion.338
  845.2 2.3 fusion.39
  856.2 5.5 convolution_convert_fusion.1
  861.8 5.2 convolution_convert_fusion
  871.1 2.3 copy.152
  873.4 2.3 copy.151
  875.7 2.5 fusion.52
  878.2 4.2 all-to-all-start
  903.6 48.2 %all-reduce.98 = (bf16[768]{0:T(1024)(128)(2,1)S(1)}, bf16[768]{0:T(1024)(128)(2,1)S(1)}, bf16[1536]{0:T(1024)(128)(2,1)}, bf16[768]{0:T(1024)(128)(2,1)}, bf16[...) all-reduce(bf16[768]{0:T(1024)(128)(2,1)} %copy-done.374, ...), channel_id=1, replica_groups=mesh['rep'=4,'shard'=8] {'shard'}, use_global_device_ids=true, to_apply=%add.79 | all-reduce | flops 16896 | bytes 67584
  971.6 4.4 fusion.60
  978.1 40.4 %reduce-scatter.28.cloned.1.call-done = bf16[96,2304]{1,0:T(8,128)(2,1)} async-done(((bf16[768,2304]{1,0:T(8,128)(2,1)}), bf16[96,2304]{1,0:T(8,128)(2,1)}) %reduce-scatter.28.cloned.1.call-update) | async-done | bytes 442384
  1020.6 98.3 %all-gather.32.cloned.1.call-done = bf16[2048,1536]{1,0:T(8,128)(2,1)} async-done(((bf16[256,1536]{1,0:T(8,128)(2,1)}), bf16[2048,1536]{1,0:T(8,128)(2,1)}) %all-gather.32.cloned.1.call-update) | async-done | bytes 6291472 | tf_op jit(solution)/shard_map/all_gather | solution.py:357
  1118.9 4.6 fusion.45
  1123.7 2.6 fusion.47
  1126.3 2.5 fusion.46
  1130.2 55.5 %reduce-scatter.16.cloned.1.call-done = bf16[96,768]{1,0:T(8,128)(2,1)} async-done(((bf16[768,768]{1,0:T(8,128)(2,1)}), bf16[96,768]{1,0:T(8,128)(2,1)}) %reduce-scatter.16.cloned.1.call-update) | async-done | bytes 147472 | tf_op jit(solution)/shard_map/reduce_scatter | solution.py:512
  1185.7 67.8 %reduce-scatter.24.cloned.1.call-done = bf16[96,768]{1,0:T(8,128)(2,1)} async-done(((bf16[768,768]{1,0:T(8,128)(2,1)}), bf16[96,768]{1,0:T(8,128)(2,1)}) %reduce-scatter.24.cloned.1.call-update) | async-done | bytes 147472 | tf_op jit(solution)/shard_map/reduce_scatter | solution.py:388
  1253.5 67.0 %reduce-scatter.26.cloned.1.call-done = bf16[96,768]{1,0:T(8,128)(2,1)} async-done(((bf16[768,768]{1,0:T(8,128)(2,1)}), bf16[96,768]{1,0:T(8,128)(2,1)}) %reduce-scatter.26.cloned.1.call-update) | async-done | bytes 147472 | tf_op jit(solution)/shard_map/reduce_scatter | solution.py:394
  1320.5 69.2 %reduce-scatter.22.cloned.1.call-done = bf16[2,48,1152]{2,1,0:T(8,128)(2,1)} async-done(((bf16[2,384,1152]{2,1,0:T(8,128)(2,1)}), bf16[2,48,1152]{2,1,0:T(8,128)(2,1)}) %reduce-scatter.22.cloned.1.call-update) | async-done | bytes 221200 | tf_op jit(solution)/shard_map/reduce_scatter | solution.py:379
  1389.7 97.9 %reduce-scatter.18.cloned.1.call-done = bf16[96,3072]{1,0:T(8,128)(2,1)} async-done(((bf16[768,3072]{1,0:T(8,128)(2,1)}), bf16[96,3072]{1,0:T(8,128)(2,1)}) %reduce-scatter.18.cloned.1.call-update) | async-done | bytes 589840 | tf_op jit(solution)/shard_map/reduce_scatter | solution.py:524
  1487.6 98.8 %reduce-scatter.20.cloned.1.call-done = bf16[384,768]{1,0:T(8,128)(2,1)} async-done(((bf16[3072,768]{1,0:T(8,128)(2,1)}), bf16[384,768]{1,0:T(8,128)(2,1)}) %reduce-scatter.20.cloned.1.call-update) | async-done | bytes 589840 | tf_op jit(solution)/shard_map/reduce_scatter | solution.py:530
  1587.2 2.6 multiply_convert_fusion.2
  1589.8 9.0 fusion
  1599.0 12.5 fusion.17
  1611.6 38.0 %reduce-scatter.30.cloned.1.call-done = bf16[144,2]{1,0:T(8,128)(2,1)} async-done(((bf16[1152,2]{1,0:T(8,128)(2,1)}), bf16[144,2]{1,0:T(8,128)(2,1)}) %reduce-scatter.30.cloned.1.call-update) | async-done | bytes 592
  1650.4 61.4 %reduce-scatter.32.cloned.1.call-done = bf16[144,2]{1,0:T(8,128)(2,1)} async-done(((bf16[1152,2]{1,0:T(8,128)(2,1)}), bf16[144,2]{1,0:T(8,128)(2,1)}) %reduce-scatter.32.cloned.1.call-update) | async-done | bytes 592
  1712.8 10.2 all-reduce.100
  1732.1 76.0 %all-reduce.107.cloned.1.call-done = (bf16[96,2304]{0,1:T(8,128)(2,1)}, bf16[2,96,1152]{2,0,1:T(2,128)(2,1)}, bf16[96,768]{1,0:T(8,128)(2,1)}, bf16[96,3072]{1,0...) async-done(((bf16[96,2304]{0,1:T(8,128)(2,1)}, ...) | async-done | bytes 4497424 | tf_op jit(solution)/shard_map/psum | solution.py:544
  (1200 shorter events, 267.3 us)
Async XLA Ops:
  7.2 127.9 %copy-start = (bf16[256,8,768]{2,1,0:T(8,128)(2,1)S(1)}, bf16[256,8,768]{2,1,0:T(8,128)(2,1)}, u32[]{:S(2)}) copy-start(bf16[256,8,768]{2,1,0:T(8,128)(2,1)} %param.33) | copy-start | bytes 9437188
  7.2 123.6 %all-gather.26.cloned.1.call-start = ((), (), s32[]{:S(2)}) async-start(), calls=%async_computation.16 | async-start | bytes 1990656 | tf_op jit(solution)/shard_map/all_gather | solution.py:160
  8.0 127.2 %all-gather.24.cloned.1.call-start = ((), (), s32[]{:S(2)}) async-start(), calls=%async_computation.15 | async-start | bytes 3981312 | tf_op jit(solution)/shard_map/all_gather | solution.py:159
  8.7 225.8 %all-gather.14.cloned.1.call-start = ((), (), s32[]{:S(2)}) async-start(), calls=%async_computation.10 | async-start | bytes 3981312 | tf_op jit(solution)/shard_map/all_gather | solution.py:103
  9.4 237.6 %all-gather.16.cloned.1.call-start = ((), (), s32[]{:S(2)}) async-start(), calls=%async_computation.11 | async-start | bytes 1327104 | tf_op jit(solution)/shard_map/all_gather | solution.py:105
  10.0 279.3 %all-gather.28.cloned.1.call-start = ((), (), s32[]{:S(2)}) async-start(), calls=%async_computation.17 | async-start | bytes 1327104 | tf_op jit(solution)/shard_map/all_gather | solution.py:165
  10.7 48.5 %copy-start.392 = (s32[256]{0:T(256)S(1)}, s32[256]{0:T(256)}, u32[]{:S(2)}) copy-start(s32[256]{0:T(256)} %param.35) | copy-start | bytes 3076
  10.8 49.0 %copy-start.393 = (bf16[2,144]{1,0:T(2,128)(2,1)S(1)}, bf16[2,144]{1,0:T(2,128)(2,1)}, u32[]{:S(2)}) copy-start(bf16[2,144]{1,0:T(2,128)(2,1)} %param.53) | copy-start | bytes 1732
  10.8 65.6 %copy-start.394 = (bf16[2,144]{1,0:T(2,128)(2,1)S(1)}, bf16[2,144]{1,0:T(2,128)(2,1)}, u32[]{:S(2)}) copy-start(bf16[2,144]{1,0:T(2,128)(2,1)} %param.52) | copy-start | bytes 1732
  10.8 85.6 %copy-start.395 = (bf16[384]{0:T(512)(128)(2,1)S(1)}, bf16[384]{0:T(512)(128)(2,1)}, u32[]{:S(2)}) copy-start(bf16[384]{0:T(512)(128)(2,1)} %param.45) | copy-start | bytes 2308
  10.8 343.7 %all-gather.18.cloned.1.call-start = ((), (), s32[]{:S(2)}) async-start(), calls=%async_computation.12 | async-start | bytes 5308416 | tf_op jit(solution)/shard_map/all_gather | solution.py:145
  11.4 423.0 %all-gather.20.cloned.1.call-start = ((), (), s32[]{:S(2)}) async-start(), calls=%async_computation.13 | async-start | bytes 5308416 | tf_op jit(solution)/shard_map/all_gather | solution.py:147
  12.1 464.0 %all-gather.22.cloned.1.call-start = ((), (), s32[]{:S(2)}) async-start(), calls=%async_computation.14 | async-start | bytes 1327104 | tf_op jit(solution)/shard_map/all_gather | solution.py:163
  12.9 659.4 %all-gather.30.cloned.1.call-start = ((), (), s32[]{:S(2)}) async-start(), calls=%async_computation.18 | async-start | bytes 15925248 | tf_op jit(solution)/shard_map/all_gather | solution.py:167
  13.6 962.4 %all-reduce.105.cloned.1.call-start = ((), (), s32[]{:S(2)}) async-start(), calls=%async_computation.29 | async-start | bytes 7077888
  289.3 65.1 %copy-start.318 = (f32[768]{0:T(1024)S(1)}, f32[768]{0:T(1024)}, u32[]{:S(2)}) copy-start(f32[768]{0:T(1024)} %convert_element_type.569) | copy-start | bytes 9220
  289.3 65.1 %copy-start.324 = (f32[768]{0:T(1024)S(1)}, f32[768]{0:T(1024)}, u32[]{:S(2)}) copy-start(f32[768]{0:T(1024)} %convert_element_type.570) | copy-start | bytes 9220
  289.3 65.1 %copy-start.353 = (f32[256]{0:T(256)S(1)}, f32[256]{0:T(256)}, u32[]{:S(2)}) copy-start(f32[256]{0:T(256)} %copy-done.352) | copy-start | bytes 3076
  434.4 41.7 %copy-start.326 = (f32[768]{0:T(1024)S(1)}, f32[768]{0:T(1024)}, u32[]{:S(2)}) copy-start(f32[768]{0:T(1024)} %convert_element_type.575) | copy-start | bytes 9220
  434.4 41.7 %copy-start.333 = (f32[768]{0:T(1024)S(1)}, f32[768]{0:T(1024)}, u32[]{:S(2)}) copy-start(f32[768]{0:T(1024)} %convert_element_type.576) | copy-start | bytes 9220
  438.9 248.2 %copy-start.334 = (f32[256]{0:T(256)}, f32[256]{0:T(256)S(1)}, u32[]{:S(2)}) copy-start(f32[256]{0:T(256)S(1)} %broadcast_multiply_fusion.2) | copy-start | bytes 3076
  711.5 48.7 %copy-start.167 = (f32[256,384]{1,0:T(8,128)}, f32[256,384]{1,0:T(8,128)S(1)}, u32[]{:S(2)}) copy-start(f32[256,384]{1,0:T(8,128)S(1)} %get-tuple-element.344) | copy-start | bytes 1179652
  711.5 48.7 %copy-start.171 = (f32[256,384]{1,0:T(8,128)}, f32[256,384]{1,0:T(8,128)S(1)}, u32[]{:S(2)}) copy-start(f32[256,384]{1,0:T(8,128)S(1)} %get-tuple-element.241) | copy-start | bytes 1179652
  713.3 46.9 %copy-start.140 = (f32[256,384]{1,0:T(8,128)}, f32[256,384]{1,0:T(8,128)S(1)}, u32[]{:S(2)}) copy-start(f32[256,384]{1,0:T(8,128)S(1)} %fusion.174) | copy-start | bytes 1179652
  716.6 43.5 %copy-start.194 = (f32[256,384]{1,0:T(8,128)}, f32[256,384]{1,0:T(8,128)S(1)}, u32[]{:S(2)}) copy-start(f32[256,384]{1,0:T(8,128)S(1)} %get-tuple-element.353) | copy-start | bytes 1179652
  716.6 43.5 %copy-start.215 = (f32[256,384]{1,0:T(8,128)}, f32[256,384]{1,0:T(8,128)S(1)}, u32[]{:S(2)}) copy-start(f32[256,384]{1,0:T(8,128)S(1)} %get-tuple-element.239) | copy-start | bytes 1179652
  716.8 43.2 %copy-start.138 = (f32[256,384]{1,0:T(8,128)}, f32[256,384]{1,0:T(8,128)S(1)}, u32[]{:S(2)}) copy-start(f32[256,384]{1,0:T(8,128)S(1)} %fusion.175) | copy-start | bytes 1179652
  719.9 40.0 %copy-start.196 = (f32[256,384]{1,0:T(8,128)}, f32[256,384]{1,0:T(8,128)S(1)}, u32[]{:S(2)}) copy-start(f32[256,384]{1,0:T(8,128)S(1)} %get-tuple-element.352) | copy-start | bytes 1179652
  719.9 40.0 %copy-start.217 = (f32[256,384]{1,0:T(8,128)}, f32[256,384]{1,0:T(8,128)S(1)}, u32[]{:S(2)}) copy-start(f32[256,384]{1,0:T(8,128)S(1)} %get-tuple-element.237) | copy-start | bytes 1179652
  720.2 39.8 %copy-start.142 = (f32[256,384]{1,0:T(8,128)}, f32[256,384]{1,0:T(8,128)S(1)}, u32[]{:S(2)}) copy-start(f32[256,384]{1,0:T(8,128)S(1)} %fusion.176) | copy-start | bytes 1179652
  723.3 36.5 %copy-start.198 = (f32[256,384]{1,0:T(8,128)}, f32[256,384]{1,0:T(8,128)S(1)}, u32[]{:S(2)}) copy-start(f32[256,384]{1,0:T(8,128)S(1)} %get-tuple-element.351) | copy-start | bytes 1179652
  723.3 36.5 %copy-start.219 = (f32[256,384]{1,0:T(8,128)}, f32[256,384]{1,0:T(8,128)S(1)}, u32[]{:S(2)}) copy-start(f32[256,384]{1,0:T(8,128)S(1)} %get-tuple-element.235) | copy-start | bytes 1179652
  723.6 36.3 %copy-start.145 = (f32[256,384]{1,0:T(8,128)}, f32[256,384]{1,0:T(8,128)S(1)}, u32[]{:S(2)}) copy-start(f32[256,384]{1,0:T(8,128)S(1)} %fusion.177) | copy-start | bytes 1179652
  726.8 32.9 %copy-start.200 = (f32[256,384]{1,0:T(8,128)}, f32[256,384]{1,0:T(8,128)S(1)}, u32[]{:S(2)}) copy-start(f32[256,384]{1,0:T(8,128)S(1)} %get-tuple-element.350) | copy-start | bytes 1179652
  726.8 32.9 %copy-start.221 = (f32[256,384]{1,0:T(8,128)}, f32[256,384]{1,0:T(8,128)S(1)}, u32[]{:S(2)}) copy-start(f32[256,384]{1,0:T(8,128)S(1)} %get-tuple-element.233) | copy-start | bytes 1179652
  727.1 32.6 %copy-start.147 = (f32[256,384]{1,0:T(8,128)}, f32[256,384]{1,0:T(8,128)S(1)}, u32[]{:S(2)}) copy-start(f32[256,384]{1,0:T(8,128)S(1)} %fusion.178) | copy-start | bytes 1179652
  730.2 29.3 %copy-start.202 = (f32[256,384]{1,0:T(8,128)}, f32[256,384]{1,0:T(8,128)S(1)}, u32[]{:S(2)}) copy-start(f32[256,384]{1,0:T(8,128)S(1)} %get-tuple-element.349) | copy-start | bytes 1179652
  730.2 29.3 %copy-start.223 = (f32[256,384]{1,0:T(8,128)}, f32[256,384]{1,0:T(8,128)S(1)}, u32[]{:S(2)}) copy-start(f32[256,384]{1,0:T(8,128)S(1)} %get-tuple-element.231) | copy-start | bytes 1179652
  781.8 236.7 %reduce-scatter.28.cloned.1.call-start = ((), (), s32[]{:S(2)}) async-start(), calls=%async_computation.26 | async-start | bytes 3981312
  820.1 298.8 %all-gather.32.cloned.1.call-start = ((), (), s32[]{:S(2)}) async-start(), calls=%async_computation.25 | async-start | bytes 7077888 | tf_op jit(solution)/shard_map/all_gather | solution.py:357
  820.7 365.0 %reduce-scatter.16.cloned.1.call-start = ((), (), s32[]{:S(2)}) async-start(), calls=%async_computation.19 | async-start | bytes 1327104 | tf_op jit(solution)/shard_map/reduce_scatter | solution.py:512
  823.3 430.1 %reduce-scatter.24.cloned.1.call-start = ((), (), s32[]{:S(2)}) async-start(), calls=%async_computation.23 | async-start | bytes 1327104 | tf_op jit(solution)/shard_map/reduce_scatter | solution.py:388
  833.8 486.7 %reduce-scatter.26.cloned.1.call-start = ((), (), s32[]{:S(2)}) async-start(), calls=%async_computation.24 | async-start | bytes 1327104 | tf_op jit(solution)/shard_map/reduce_scatter | solution.py:394
  845.1 544.6 %reduce-scatter.22.cloned.1.call-start = ((), (), s32[]{:S(2)}) async-start(), calls=%async_computation.22 | async-start | bytes 1990656 | tf_op jit(solution)/shard_map/reduce_scatter | solution.py:379
  855.5 632.1 %reduce-scatter.18.cloned.1.call-start = ((), (), s32[]{:S(2)}) async-start(), calls=%async_computation.20 | async-start | bytes 5308416 | tf_op jit(solution)/shard_map/reduce_scatter | solution.py:524
  861.7 724.8 %reduce-scatter.20.cloned.1.call-start = ((), (), s32[]{:S(2)}) async-start(), calls=%async_computation.21 | async-start | bytes 5308416 | tf_op jit(solution)/shard_map/reduce_scatter | solution.py:530
  878.2 142.4 %all-to-all-start = ((bf16[256,8,192]{0,2,1:T(8,128)(2,1)}), bf16[256,8,192]{0,2,1:T(8,128)(2,1)}, u32[]{:S(2)}, u32[]{:S(2)}) async-start(bf16[256,8,192]{0,2,1:T(8,128)(2,1)} %fusion.52), calls=%async_computation.6 | async-start | bytes 1572864 | tf_op jit(solution)/shard_map/all_to_all | solution.py:358
  882.4 767.1 %reduce-scatter.30.cloned.1.call-start = ((), (), s32[]{:S(2)}) async-start(), calls=%async_computation.27 | async-start | bytes 331776
  899.3 72.3 %copy-start.280 = (bf16[12,64,256]{2,1,0:T(8,128)(2,1)S(1)}, bf16[12,64,256]{2,1,0:T(8,128)(2,1)}, u32[]{:S(2)}) copy-start(bf16[12,64,256]{2,1,0:T(8,128)(2,1)} %copy-done.278) | copy-start | bytes 1179652
  900.4 811.4 %reduce-scatter.32.cloned.1.call-start = ((), (), s32[]{:S(2)}) async-start(), calls=%async_computation.28 | async-start | bytes 331776
  971.3 836.8 %all-reduce.107.cloned.1.call-start = ((), (), s32[]{:S(2)}) async-start(), calls=%async_computation.30 | async-start | bytes 9289728 | tf_op jit(solution)/shard_map/psum | solution.py:544
  1598.9 113.8 %copy-start.396 = (bf16[96]{0:T(256)(128)(2,1)S(1)}, bf16[96]{0:T(256)(128)(2,1)}, u32[]{:S(2)}) copy-start(bf16[96]{0:T(256)(128)(2,1)} %dynamic-slice.19) | copy-start | bytes 580
  1598.9 113.8 %copy-start.397 = (bf16[96]{0:T(256)(128)(2,1)S(1)}, bf16[96]{0:T(256)(128)(2,1)}, u32[]{:S(2)}) copy-start(bf16[96]{0:T(256)(128)(2,1)} %dynamic-slice.21) | copy-start | bytes 580
  1598.9 113.8 %copy-start.398 = (bf16[96]{0:T(256)(128)(2,1)S(1)}, bf16[96]{0:T(256)(128)(2,1)}, u32[]{:S(2)}) copy-start(bf16[96]{0:T(256)(128)(2,1)} %dynamic-slice.25) | copy-start | bytes 580
  1598.9 113.8 %copy-start.399 = (bf16[96]{0:T(256)(128)(2,1)S(1)}, bf16[96]{0:T(256)(128)(2,1)}, u32[]{:S(2)}) copy-start(bf16[96]{0:T(256)(128)(2,1)} %dynamic-slice.27) | copy-start | bytes 580
  1598.9 113.8 %copy-start.400 = (bf16[96]{0:T(256)(128)(2,1)S(1)}, bf16[96]{0:T(256)(128)(2,1)}, u32[]{:S(2)}) copy-start(bf16[96]{0:T(256)(128)(2,1)} %dynamic-slice.29) | copy-start | bytes 580
  1598.9 113.8 %copy-start.401 = (bf16[96]{0:T(256)(128)(2,1)S(1)}, bf16[96]{0:T(256)(128)(2,1)}, u32[]{:S(2)}) copy-start(bf16[96]{0:T(256)(128)(2,1)} %dynamic-slice.33) | copy-start | bytes 580
  1599.0 113.8 %copy-start.402 = (bf16[96]{0:T(256)(128)(2,1)S(1)}, bf16[96]{0:T(256)(128)(2,1)}, u32[]{:S(2)}) copy-start(bf16[96]{0:T(256)(128)(2,1)} %dynamic-slice.35) | copy-start | bytes 580
  1599.0 113.8 %copy-start.403 = (bf16[192]{0:T(256)(128)(2,1)S(1)}, bf16[192]{0:T(256)(128)(2,1)}, u32[]{:S(2)}) copy-start(bf16[192]{0:T(256)(128)(2,1)} %dynamic-slice.15) | copy-start | bytes 1156
  1599.0 113.8 %copy-start.404 = (bf16[192]{0:T(256)(128)(2,1)S(1)}, bf16[192]{0:T(256)(128)(2,1)}, u32[]{:S(2)}) copy-start(bf16[192]{0:T(256)(128)(2,1)} %dynamic-slice.37) | copy-start | bytes 1156
  1599.0 113.8 %copy-start.405 = (bf16[96]{0:T(256)(128)(2,1)S(1)}, bf16[96]{0:T(256)(128)(2,1)}, u32[]{:S(2)}) copy-start(bf16[96]{0:T(256)(128)(2,1)} %dynamic-slice.39) | copy-start | bytes 580
  1599.0 113.8 %copy-start.406 = (bf16[96]{0:T(256)(128)(2,1)S(1)}, bf16[96]{0:T(256)(128)(2,1)}, u32[]{:S(2)}) copy-start(bf16[96]{0:T(256)(128)(2,1)} %dynamic-slice.41) | copy-start | bytes 580
  1599.0 113.8 %copy-start.407 = (bf16[96]{0:T(256)(128)(2,1)S(1)}, bf16[96]{0:T(256)(128)(2,1)}, u32[]{:S(2)}) copy-start(bf16[96]{0:T(256)(128)(2,1)} %dynamic-slice.43) | copy-start | bytes 580
  1599.0 113.8 %copy-start.408 = (bf16[96]{0:T(256)(128)(2,1)S(1)}, bf16[96]{0:T(256)(128)(2,1)}, u32[]{:S(2)}) copy-start(bf16[96]{0:T(256)(128)(2,1)} %dynamic-slice.45) | copy-start | bytes 580
  (384 other events, 991.3 us)
Sparse Core Ops, SparseCore 0:
  10.3 49.1 all-gather.25
  61.6 63.3 all-gather.23
  127.2 63.3 all-gather.13
  192.6 39.8 all-gather.15
  234.6 39.7 all-gather.27
  276.4 78.0 all-gather.17
  356.7 77.6 all-gather.19
  436.6 39.4 all-gather.21
  478.3 193.9 all-gather.29
  781.9 154.4 all-reduce.104
  940.0 78.4 reduce-scatter.27
  1020.5 98.3 all-gather.31
  1122.8 62.8 reduce-scatter.15
  1189.5 63.9 reduce-scatter.23
  1256.7 63.7 reduce-scatter.25
  1324.4 65.2 reduce-scatter.21
  1393.2 94.3 reduce-scatter.17
  1491.1 95.2 reduce-scatter.19
  1590.3 59.1 reduce-scatter.29
  1653.3 58.5 reduce-scatter.31
  1716.1 91.9 all-reduce.106
where the time goes:
time: 1830 us
  waiting for transfers between devices  1130 us (62%)
  local copies, waits for them, and re-layouts  210 us (11%)
  matrix products  198 us (11%)
  blocking collectives  160 us (9%)
  other arithmetic  95.8 us (5%)
  between operations  22.8 us (1%)
    all_gather x1, waiting for transfers between devices, shards(): lax.all_gather(window_kernel, 'shard', axis=1, tiled=True)  191 us
    unnamed x25, waiting for transfers between devices  146 us
    unnamed x912, local copies, waits for them, and re-layouts  127 us
    reduce_scatter x1, waiting for transfers between devices, shards(): lax.psum_scatter(delta_down.astype(jnp.bfloat16), 'shard', scatter_dimens...  98.8 us
    all_gather x1, waiting for transfers between devices, shards(): conv_all = lax.all_gather(delta_conv, 'shard', axis=0, tiled=True)  98.3 us
    reduce_scatter x1, waiting for transfers between devices, shards(): lax.psum_scatter(delta_up.astype(jnp.bfloat16), 'shard', scatter_dimensio...  97.9 us
    unnamed x2, blocking collectives  87.8 us
    psum x1, waiting for transfers between devices, shards(): lax.psum(token_owned[0].astype(jnp.bfloat16), 'rep').astype(jnp.float32)  76 us
  transfers between devices with their start and end apart: 22, of which 15 were waited for; matrix products, arithmetic and copies ran while one was open for 19% of the time, Pallas kernels for 0%

commit v1 on v0

v1 whole, which is shorter than its diff:
```python
import jax
import jax.numpy as jnp
from jax import lax
from jax.experimental import pallas as pl
from jax.experimental.pallas import tpu as pltpu
from jax.sharding import PartitionSpec as P

HEADS = 12


EPS = 1e-05


def shortened(value):
    return jax.tree.map(lambda a: a.astype(jnp.bfloat16) if a.dtype == jnp.float32 else a, value)


def product(left, right):
    return jnp.dot(left, right, preferred_element_type=jnp.float32)


def left_product(left, right):
    return lax.dot_general(
        left, right, (((0,), (0,)), ((), ())), preferred_element_type=jnp.float32
    )


def right_product(left, right):
    return lax.dot_general(
        left, right, (((1,), (1,)), ((), ())), preferred_element_type=jnp.float32
    )


def column_sum(values):
    return jnp.sum(values.astype(jnp.float32), axis=0)


def normalize(values, gain, shift):
    center = jnp.mean(values, axis=-1, keepdims=True)
    centered = values - center
    spread = jnp.mean(centered * centered, axis=-1, keepdims=True)
    return centered * lax.rsqrt(spread + EPS) * gain + shift


def exact_gelu(values):
    return jax.nn.gelu(values, approximate=False)


def recurrent_cell(inputs, hidden_gates, carried):
    hidden_width = carried.shape[-1]
    reset = jax.nn.sigmoid(inputs[:, :hidden_width] + hidden_gates[:, :hidden_width])
    update = jax.nn.sigmoid(
        inputs[:, hidden_width : 2 * hidden_width]
        + hidden_gates[:, hidden_width : 2 * hidden_width]
    )
    candidate = jnp.tanh(
        inputs[:, 2 * hidden_width :] + reset * hidden_gates[:, 2 * hidden_width :]
    )
    return (1.0 - update) * candidate + update * carried


DEPTH_SIZE = 4


class Place:
    def __init__(self):
        self.rep_size = lax.axis_size("rep")
        self.shard_size = lax.axis_size("shard")
        self.depth = DEPTH_SIZE
        self.height = self.shard_size // DEPTH_SIZE
        rep_at = lax.axis_index("rep")
        shard_at = lax.axis_index("shard")
        self.shard_at = shard_at
        self.core = rep_at % 2
        self.side = (rep_at // 2) % 2
        self.row = shard_at % self.height
        self.layer = shard_at // self.height
        self.coords = jnp.stack([self.layer, self.row, self.side, self.core]).astype(jnp.int32)

    def over_core(self, value):
        return lax.ppermute(value, "rep", [(i, i ^ 1) for i in range(self.rep_size)])

    def over_side(self, value):
        return lax.ppermute(value, "rep", [(i, i ^ 2) for i in range(self.rep_size)])

    def over_far(self, value, step):
        return lax.ppermute(
            value, "rep", [(i, (i + 4 * step) % self.rep_size) for i in range(self.rep_size)]
        )

    def over_row(self, value, step):
        return lax.ppermute(value, "shard", [(i, i ^ step) for i in range(self.shard_size)])

    def over_layer(self, value, step):
        return lax.ppermute(
            value, "shard", [(i, i ^ (step * self.height)) for i in range(self.shard_size)]
        )


def put_together(place, parts, rows, columns, split):
    depth, part_rows, half = parts[0][0][0].shape
    flat = [part for group in parts for inner in group for part in inner]
    slots = [
        (core_slot, side_slot, row_slot)
        for core_slot in range(2)
        for side_slot in range(len(parts[0]))
        for row_slot in range(len(parts[0][0]))
    ]
    height = place.height
    pieces = 2 if split else 1

    def body(coords_ref, *refs):
        ins, out_ref, sems = refs[: len(flat)], refs[len(flat)], refs[len(flat) + 1]
        layer, row, side, core = (coords_ref[i] for i in range(4))
        copies = []
        for at, (core_slot, side_slot, row_slot) in enumerate(slots):
            for layer_slot in range(depth):
                block = (layer ^ layer_slot) * height + (row ^ row_slot)
                if split:
                    block = block * 2 + (side ^ side_slot)
                column = pl.multiple_of((core ^ core_slot) * half, 128)
                copies.append(
                    pltpu.make_async_copy(
                        ins[at].at[layer_slot],
                        out_ref.at[block, :, pl.ds(column, half)],
                        sems.at[at * depth + layer_slot],
                    )
                )
        for copy in copies:
            copy.start()
        for copy in copies:
            copy.wait()

    blocks = depth * height * pieces
    whole = pl.pallas_call(
        body,
        out_shape=jax.ShapeDtypeStruct((blocks, part_rows, columns), flat[0].dtype),
        in_specs=[pl.BlockSpec(memory_space=pltpu.SMEM)]
        + [pl.BlockSpec(memory_space=pl.ANY)] * len(flat),
        out_specs=pl.BlockSpec(memory_space=pl.ANY),
        scratch_shapes=[pltpu.SemaphoreType.DMA((len(flat) * depth,))],
        name="put_together",
    )(place.coords, *flat)
    return whole.reshape(rows * place.shard_size, columns)


def gathered(place, shard, split):
    rows, columns = shard.shape
    half = columns // 2
    part_rows = rows // 2 if split else rows
    top = place.side * part_rows if split else 0
    piece = lax.dynamic_slice(shard, (top, place.core * half), (part_rows, half))
    layers = jnp.stack(
        [piece] + [place.over_layer(piece, step) for step in range(1, place.depth)]
    )
    column = [layers] + [place.over_row(layers, step) for step in range(1, place.height)]
    sides = [column]
    if split:
        sides.append([place.over_side(part) for part in column])
    cores = [sides, [[place.over_core(part) for part in group] for group in sides]]
    return put_together(place, cores, rows, columns, split)


def pick(value, at, axis):
    return lax.dynamic_index_in_dim(value, at, axis, keepdims=False)


def widen(value):
    return value.astype(jnp.float32)


def narrow(value):
    return value.astype(jnp.bfloat16)


def owned_gradient(place, inputs, delta, split):
    half = delta.shape[1] // 2

    def half_of(at):
        return left_product(inputs, lax.dynamic_slice_in_dim(delta, at * half, half, axis=1))

    return owned_sum(place, half_of, split)


def owned_hidden(place, states, deltas):
    def half_of(at):
        state = jnp.where(at == 0, states[0], states[1])
        return left_product(state, jnp.where(at == 0, deltas[0], deltas[1]))

    both = owned_sum(place, half_of, False)
    half = both.shape[1] // 2
    return jnp.stack([both[:, :half], both[:, half:]])


def owned_sum(place, half_of, split):
    sent = narrow(half_of(1 - place.core))
    other = place.over_core(sent)
    held = narrow(half_of(place.core) + widen(other))
    full_rows, half = held.shape
    rows = full_rows // place.shard_size
    part_rows = rows // 2 if split else rows
    if split:
        held = held.reshape(place.shard_size, 2, part_rows, half)
        other = place.over_side(pick(held, 1 - place.side, 1))
        held = narrow(widen(pick(held, place.side, 1)) + widen(other))
    held = held.reshape(place.depth, place.height, part_rows, half)
    total = widen(pick(held, place.row, 1))
    for step in range(1, place.height):
        total = total + widen(place.over_row(pick(held, place.row ^ step, 1), step))
    held = narrow(total)
    total = widen(pick(held, place.layer, 0))
    for step in range(1, place.depth):
        total = total + widen(place.over_layer(pick(held, place.layer ^ step, 0), step))
    held = narrow(total)
    for step in range(1, place.rep_size // 4):
        total = total + widen(place.over_far(held, step))
    held = narrow(total)
    other = place.over_side(held)
    if split:
        first = jnp.where(place.side == 0, held, other)
        last = jnp.where(place.side == 0, other, held)
        held = jnp.concatenate([first, last], axis=0)
    else:
        held = narrow(widen(held) + widen(other))
    other = place.over_core(held)
    first = jnp.where(place.core == 0, held, other)
    last = jnp.where(place.core == 0, other, held)
    return widen(jnp.concatenate([first, last], axis=1))


def gathered_vectors(place, vectors):
    flat = [v.reshape(-1) for v in vectors]
    packed = jnp.concatenate(flat)[None, :]
    layers = jnp.concatenate(
        [packed] + [place.over_layer(packed, step) for step in range(1, place.depth)], axis=0
    )
    slots = jnp.stack(
        [layers] + [place.over_row(layers, step) for step in range(1, place.height)], axis=1
    ).reshape(place.shard_size, -1)
    order = jnp.arange(place.shard_size)
    slot_of = ((order // place.height) ^ place.layer) * place.height + (
        (order % place.height) ^ place.row
    )
    ordered = jnp.take(slots, slot_of, axis=0, mode="clip").astype(jnp.float32)
    whole, start = [], 0
    for v in vectors:
        width = v.size
        part = ordered[:, start : start + width]
        if v.ndim == 1:
            whole.append(part.reshape(-1))
        else:
            lead, inner = v.shape
            whole.append(
                part.reshape(place.shard_size, lead, inner).transpose(1, 0, 2).reshape(lead, -1)
            )
        start += width
    return whole


def owned_vectors(place, vectors):
    count = place.shard_size
    rows = []
    for v in vectors:
        if v.ndim == 1:
            rows.append(v.reshape(count, -1))
        else:
            lead = v.shape[0]
            rows.append(v.reshape(lead, count, -1).transpose(1, 0, 2).reshape(count, -1))
    total = jnp.concatenate(rows, axis=1)
    total = total + place.over_core(total)
    total = total + place.over_side(total)
    base = total
    for step in range(1, place.rep_size // 4):
        total = total + place.over_far(base, step)
    span = 1
    while span < place.height:
        total = total + place.over_row(total, span)
        span *= 2
    span = 1
    while span < place.depth:
        total = total + place.over_layer(total, span)
        span *= 2
    own = lax.dynamic_index_in_dim(total, place.shard_at, 0, keepdims=False)
    parts, start = [], 0
    for v in vectors:
        width = v.size // count
        part = own[start : start + width]
        parts.append(part if v.ndim == 1 else part.reshape(v.shape[0], -1))
        start += width
    return parts


def shards(
    tokens,
    letters,
    lengths,
    counts,
    cot_token,
    cot_letter,
    project_weight,
    project_bias,
    output_weight,
    output_bias,
    first_gain,
    first_shift,
    up_weight,
    up_bias,
    down_weight,
    down_bias,
    second_gain,
    second_shift,
    gates_input,
    gates_hidden,
    shift_input,
    shift_hidden,
    token_mixer,
    token_offset,
    letter_mixer,
    letter_offset,
    window_kernel,
    window_offset,
    third_gain,
    third_shift,
    fourth_gain,
    fourth_shift,
):
    place = Place()
    seq_rows, model_width = tokens.shape
    letter_slots = letters.shape[1]
    head_width = model_width // HEADS
    score_scale = float(head_width) ** (-0.5)
    row_valid = jnp.arange(seq_rows) < lengths[0]
    row_mask = row_valid.astype(jnp.float32)[:, None]
    key_valid = row_valid[None, None, :]
    letter_flat = letters.transpose(1, 0, 2).reshape(letter_slots * seq_rows, model_width)

    (
        full_pbias,
        full_obias,
        gain_one,
        shift_one,
        full_ubias,
        full_dbias,
        gain_two,
        shift_two,
        full_sin,
        full_shid,
        full_toff,
        full_loff,
        full_koff,
        gain_three,
        shift_three,
        gain_four,
        shift_four,
    ) = gathered_vectors(
        place,
        (
            project_bias,
            output_bias,
            first_gain,
            first_shift,
            up_bias,
            down_bias,
            second_gain,
            second_shift,
            shift_input,
            shift_hidden,
            token_offset,
            letter_offset,
            window_offset,
            third_gain,
            third_shift,
            fourth_gain,
            fourth_shift,
        ),
    )
    side_by_side = lambda w: jnp.concatenate([w[i] for i in range(w.shape[0])], axis=1)
    full_project = gathered(place, project_weight, True)
    full_gin = gathered(place, side_by_side(gates_input), True)
    full_ghid = gathered(place, side_by_side(gates_hidden), False)
    full_output = gathered(place, output_weight, False)
    full_up = gathered(place, up_weight, False)
    full_down = gathered(place, down_weight, False)
    full_tmix = gathered(place, token_mixer, False)
    full_lmix = gathered(place, letter_mixer, False)
    full_kernel = gathered(place, side_by_side(window_kernel), True)

    bias_full = jnp.concatenate(
        [full_pbias[:model_width], jnp.zeros((model_width,), jnp.float32), full_pbias[model_width:]]
    )
    mixed = (product(tokens, full_project) + bias_full).astype(jnp.bfloat16)
    queries = mixed[:, :model_width].reshape(seq_rows, HEADS, head_width)
    key_rows = mixed[:, model_width : 2 * model_width].reshape(seq_rows, HEADS, head_width)
    value_rows = mixed[:, 2 * model_width :].reshape(seq_rows, HEADS, head_width)

    def masked_scores_of(query_part, key_part):
        raw_scores = (
            jnp.einsum("qhd,khd->hqk", query_part, key_part, preferred_element_type=jnp.float32)
            * score_scale
        )
        return jnp.where(key_valid, raw_scores, -1e30)

    masked_scores = masked_scores_of(queries, key_rows)
    row_peak = jnp.max(masked_scores, axis=-1, keepdims=True)
    log_total = row_peak + jnp.log(
        jnp.sum(jnp.exp(masked_scores - row_peak), axis=-1, keepdims=True)
    )
    probs_low = jnp.exp(masked_scores - log_total).astype(jnp.bfloat16)
    context = (
        jnp.einsum("hqk,khd->qhd", probs_low, value_rows, preferred_element_type=jnp.float32)
        .astype(jnp.bfloat16)
        .reshape(seq_rows, model_width)
    )
    attended = product(context, full_output) + full_obias
    residual_one = tokens.astype(jnp.float32) + attended
    first = normalize(residual_one, gain_one, shift_one)
    first_low = first.astype(jnp.bfloat16)
    upper = product(first_low, full_up) + full_ubias
    activated = exact_gelu(upper).astype(jnp.bfloat16)
    residual_two = first + product(activated, full_down) + full_dbias
    second = normalize(residual_two, gain_two, shift_two)
    hidden_width = full_ghid.shape[0]
    gates_width = 3 * hidden_width
    forward_order = list(range(letter_slots))
    reverse_order = list(range(letter_slots - 1, -1, -1))
    ghid_of = [full_ghid[:, d * gates_width : (d + 1) * gates_width] for d in range(2)]
    gin_of = [full_gin[:, d * gates_width : (d + 1) * gates_width] for d in range(2)]

    def run_direction(direction, step_order):
        gate_inputs = (product(letter_flat, gin_of[direction]) + full_sin[direction]).reshape(
            letter_slots, seq_rows, gates_width
        )
        carried = jnp.zeros((seq_rows, hidden_width), jnp.float32)
        saved_states = []
        for position in step_order:
            saved_states.append(carried)
            hidden_gates = product(carried.astype(jnp.bfloat16), ghid_of[direction]) + full_shid[
                direction
            ]
            fresh = recurrent_cell(gate_inputs[position], hidden_gates, carried)
            carried = jnp.where((position < counts)[:, None], fresh, carried)
        return (carried, gate_inputs, saved_states)

    forth_state, forth_inputs, forth_saved = run_direction(0, forward_order)
    back_state, back_inputs, back_saved = run_direction(1, reverse_order)
    pooled = jnp.concatenate([forth_state, back_state], axis=-1)
    second_low = second.astype(jnp.bfloat16)
    pooled_low = pooled.astype(jnp.bfloat16)
    token_side = product(second_low, full_tmix) + full_toff
    letter_side = product(pooled_low, full_lmix) + full_loff
    joined = (jnp.concatenate([token_side, letter_side], axis=-1) * row_mask).astype(jnp.bfloat16)
    joined_width = joined.shape[1]
    taps = product(joined, full_kernel)
    convolved = (
        jnp.pad(taps[:-1, :joined_width], ((1, 0), (0, 0)))
        + taps[:, joined_width : 2 * joined_width]
        + jnp.pad(taps[1:, 2 * joined_width :], ((0, 1), (0, 0)))
        + full_koff
    )
    widened = exact_gelu(convolved)
    residual_three = second + widened[:, :model_width]
    residual_four = pooled + widened[:, model_width:]
    token_out = normalize(residual_three, gain_three, shift_three) * row_mask
    letter_out = normalize(residual_four, gain_four, shift_four) * row_mask

    out_token_delta = cot_token.astype(jnp.float32) * row_mask
    out_letter_delta = cot_letter.astype(jnp.float32) * row_mask
    unused_three, pull_three = jax.vjp(normalize, residual_three, gain_three, shift_three)
    delta_three, delta_gain_three, delta_shift_three = pull_three(out_token_delta)
    unused_four, pull_four = jax.vjp(normalize, residual_four, gain_four, shift_four)
    delta_four, delta_gain_four, delta_shift_four = pull_four(out_letter_delta)
    unused_gelu, pull_gelu = jax.vjp(exact_gelu, convolved)
    delta_conv = pull_gelu(jnp.concatenate([delta_three, delta_four], axis=-1))[0].astype(
        jnp.bfloat16
    )
    delta_koff = column_sum(delta_conv)
    delta_taps = jnp.concatenate(
        [
            jnp.pad(delta_conv[1:], ((0, 1), (0, 0))),
            delta_conv,
            jnp.pad(delta_conv[:-1], ((1, 0), (0, 0))),
        ],
        axis=1,
    )
    kernel_grad = owned_gradient(place, joined, delta_taps, True)
    delta_joined = right_product(delta_taps, full_kernel) * row_mask
    delta_tside = delta_joined[:, :model_width].astype(jnp.bfloat16)
    delta_lside = delta_joined[:, model_width:].astype(jnp.bfloat16)
    tmix_grad = owned_gradient(place, second_low, delta_tside, False)
    delta_toff = column_sum(delta_tside)
    lmix_grad = owned_gradient(place, pooled_low, delta_lside, False)
    delta_loff = column_sum(delta_lside)
    delta_second = delta_three + right_product(delta_tside, full_tmix)
    delta_pooled = delta_four + right_product(delta_lside, full_lmix)

    def back_direction(direction, step_order, gate_inputs, saved_states, delta_carried):
        delta_inputs = [None] * letter_slots
        delta_gate_list = [None] * letter_slots
        state_list = [None] * letter_slots
        delta_hshift = jnp.zeros((gates_width,), jnp.float32)
        for turn in range(letter_slots - 1, -1, -1):
            position = step_order[turn]
            carried = saved_states[turn]
            active = (position < counts)[:, None]
            carried_low = carried.astype(jnp.bfloat16)
            hidden_gates = product(carried_low, ghid_of[direction]) + full_shid[direction]
            unused_cell, pullback = jax.vjp(
                recurrent_cell, gate_inputs[position], hidden_gates, carried
            )
            delta_in, delta_gates, delta_direct = pullback(jnp.where(active, delta_carried, 0.0))
            gates_low = delta_gates.astype(jnp.bfloat16)
            delta_hshift = delta_hshift + column_sum(gates_low)
            delta_carried = (
                jnp.where(active, 0.0, delta_carried)
                + delta_direct
                + right_product(gates_low, ghid_of[direction])
            )
            delta_inputs[position] = delta_in.astype(jnp.bfloat16)
            delta_gate_list[turn] = gates_low
            state_list[turn] = carried_low
        inputs_low = jnp.concatenate(delta_inputs, axis=0)
        return (
            inputs_low,
            column_sum(inputs_low),
            jnp.concatenate(state_list, axis=0),
            jnp.concatenate(delta_gate_list, axis=0),
            delta_hshift,
        )

    forth_back = back_direction(
        0, forward_order, forth_inputs, forth_saved, delta_pooled[:, :hidden_width]
    )
    back_back = back_direction(
        1, reverse_order, back_inputs, back_saved, delta_pooled[:, hidden_width:]
    )
    gates_low = jnp.concatenate([forth_back[0], back_back[0]], axis=1)
    letters_grad = (
        right_product(gates_low, full_gin)
        .astype(jnp.bfloat16)
        .reshape(letter_slots, seq_rows, model_width)
        .transpose(1, 0, 2)
    )
    gin_grad = owned_gradient(place, letter_flat, gates_low, True)
    gin_grad = jnp.stack([gin_grad[:, :gates_width], gin_grad[:, gates_width:]])
    sin_delta = jnp.stack([forth_back[1], back_back[1]])
    shid_delta = jnp.stack([forth_back[4], back_back[4]])
    ghid_grad = owned_hidden(
        place, (forth_back[2], back_back[2]), (forth_back[3], back_back[3])
    )

    unused_two, pull_two = jax.vjp(normalize, residual_two, gain_two, shift_two)
    delta_two, delta_gain_two, delta_shift_two = pull_two(delta_second)
    delta_lowered = delta_two.astype(jnp.bfloat16)
    down_grad = owned_gradient(place, activated, delta_lowered, False)
    delta_dbias = column_sum(delta_lowered)
    unused_act, pull_act = jax.vjp(exact_gelu, upper)
    delta_upper = pull_act(right_product(delta_lowered, full_down))[0].astype(jnp.bfloat16)
    up_grad = owned_gradient(place, first_low, delta_upper, False)
    delta_ubias = column_sum(delta_upper)
    delta_first = delta_two + right_product(delta_upper, full_up)
    unused_one, pull_one = jax.vjp(normalize, residual_one, gain_one, shift_one)
    delta_one, delta_gain_one, delta_shift_one = pull_one(delta_first)
    delta_attended = delta_one.astype(jnp.bfloat16)
    output_grad = owned_gradient(place, context, delta_attended, False)
    delta_obias = column_sum(delta_attended)
    delta_context = (
        right_product(delta_attended, full_output)
        .astype(jnp.bfloat16)
        .reshape(seq_rows, HEADS, head_width)
    )
    probabilities = jnp.exp(masked_scores_of(queries, key_rows) - log_total)
    delta_values = jnp.einsum(
        "hqk,qhd->khd",
        probabilities.astype(jnp.bfloat16),
        delta_context,
        preferred_element_type=jnp.float32,
    )
    delta_probs = jnp.einsum(
        "qhd,khd->hqk", delta_context, value_rows, preferred_element_type=jnp.float32
    )
    delta_scores = (
        probabilities * (delta_probs - jnp.sum(probabilities * delta_probs, axis=-1, keepdims=True))
    ).astype(jnp.bfloat16)
    delta_queries = (
        jnp.einsum("hqk,khd->qhd", delta_scores, key_rows, preferred_element_type=jnp.float32)
        * score_scale
    )
    delta_keys = (
        jnp.einsum("hqk,qhd->khd", delta_scores, queries, preferred_element_type=jnp.float32)
        * score_scale
    )
    delta_mixed = jnp.concatenate(
        [
            delta_queries.reshape(seq_rows, model_width),
            delta_keys.reshape(seq_rows, model_width),
            delta_values.reshape(seq_rows, model_width),
        ],
        axis=-1,
    ).astype(jnp.bfloat16)
    project_grad = owned_gradient(place, tokens, delta_mixed, True)
    delta_mixed_sum = column_sum(delta_mixed)
    delta_pbias = jnp.concatenate(
        [delta_mixed_sum[:model_width], delta_mixed_sum[2 * model_width :]]
    )
    tokens_grad = (delta_one + right_product(delta_mixed, full_project)).astype(jnp.bfloat16)
    (
        pbias_grad,
        obias_grad,
        gain_one_grad,
        shift_one_grad,
        ubias_grad,
        dbias_grad,
        gain_two_grad,
        shift_two_grad,
        sin_grad,
        shid_grad,
        toff_grad,
        loff_grad,
        koff_grad,
        gain_three_grad,
        shift_three_grad,
        gain_four_grad,
        shift_four_grad,
    ) = owned_vectors(
        place,
        (
            delta_pbias,
            delta_obias,
            delta_gain_one,
            delta_shift_one,
            delta_ubias,
            delta_dbias,
            delta_gain_two,
            delta_shift_two,
            sin_delta,
            shid_delta,
            delta_toff,
            delta_loff,
            delta_koff,
            delta_gain_three,
            delta_shift_three,
            delta_gain_four,
            delta_shift_four,
        ),
    )
    taps_grad = jnp.stack(
        [kernel_grad[:, t * joined_width : (t + 1) * joined_width] for t in range(3)]
    )
    return (
        token_out.astype(jnp.bfloat16),
        letter_out.astype(jnp.bfloat16),
        tokens_grad,
        letters_grad,
        project_grad,
        pbias_grad,
        output_grad,
        obias_grad,
        gain_one_grad,
        shift_one_grad,
        up_grad,
        ubias_grad,
        down_grad,
        dbias_grad,
        gain_two_grad,
        shift_two_grad,
        gin_grad,
        ghid_grad,
        sin_grad,
        shid_grad,
        tmix_grad,
        toff_grad,
        lmix_grad,
        loff_grad,
        taps_grad,
        koff_grad,
        gain_three_grad,
        shift_three_grad,
        gain_four_grad,
        shift_four_grad,
    )


def solution(mesh):
    placed = (
        P(("rep", "shard"), None),
        P(("rep", "shard"), None, None),
        P(("rep", "shard")),
        P(("rep", "shard")),
        P(("rep", "shard"), None),
        P(("rep", "shard"), None),
        P("shard", None),
        P("shard"),
        P("shard", None),
        P("shard"),
        P("shard"),
        P("shard"),
        P("shard", None),
        P("shard"),
        P("shard", None),
        P("shard"),
        P("shard"),
        P("shard"),
        P(None, "shard", None),
        P(None, "shard", None),
        P(None, "shard"),
        P(None, "shard"),
        P("shard", None),
        P("shard"),
        P("shard", None),
        P("shard"),
        P(None, "shard", None),
        P("shard"),
        P("shard"),
        P("shard"),
        P("shard"),
        P("shard"),
    )
    return jax.shard_map(
        shards,
        mesh=mesh,
        in_specs=placed,
        out_specs=(
            P(("rep", "shard"), None),
            P(("rep", "shard"), None),
            P(("rep", "shard"), None),
            P(("rep", "shard"), None, None),
            P("shard", None),
            P("shard"),
            P("shard", None),
            P("shard"),
            P("shard"),
            P("shard"),
            P("shard", None),
            P("shard"),
            P("shard", None),
            P("shard"),
            P("shard"),
            P("shard"),
            P(None, "shard", None),
            P(None, "shard", None),
            P(None, "shard"),
            P(None, "shard"),
            P("shard", None),
            P("shard"),
            P("shard", None),
            P("shard"),
            P(None, "shard", None),
            P("shard"),
            P("shard"),
            P("shard"),
            P("shard"),
            P("shard"),
        ),
        check_vma=False,
    )
```

time: 1830 us -> 1930 us (1.055)
  Pallas kernels: 0 us -> 1110 us
  waiting for transfers between devices: 1130 us -> 303 us
  blocking collectives: 160 us -> 0 us
  starting transfers between devices: 5.84 us -> 150 us
  local copies, waits for them, and re-layouts: 210 us -> 118 us
  matrix products: 198 us -> 152 us
    pallas_call x0 -> x9, Pallas kernels: none -> 1110 us  [put_together(): pl.pallas_call(body, out_shape=jax.ShapeDtypeStruct((blocks, part_rows, c...]
    reduce_scatter x6 -> x0, waiting for transfers between devices: 456 us -> none  [the longest x1 98.8 us: shards(): lax.psum_scatter(delta_down.astype(jnp.bfloat16), 'shard', scatter_dimens...]
    all_gather x10 -> x0, waiting for transfers between devices: 455 us -> none  [the longest x1 191 us: shards(): lax.all_gather(window_kernel, 'shard', axis=1, tiled=True)]
    ppermute x0 -> x141, waiting for transfers between devices: none -> 303 us  [the longest x59 146 us: over_layer(): lax.ppermute(value, 'shard', [(i, i ^ step * self.height) for i in range(...]
    ppermute x0 -> x141, starting transfers between devices: none -> 150 us  [the longest x59 100 us: over_layer(): lax.ppermute(value, 'shard', [(i, i ^ step * self.height) for i in range(...]
    unnamed x25 -> x0, waiting for transfers between devices: 146 us -> none
    unnamed x2 -> x0, blocking collectives: 87.8 us -> none
    psum x1 -> x0, waiting for transfers between devices: 76 us -> none  [shards(): lax.psum(token_owned[0].astype(jnp.bfloat16), 'rep').astype(jnp.float32)]
  transfers between devices with their start and end apart: 22 -> 141, of which waited for: 15 -> 50; matrix products, arithmetic and copies ran while one was open for 19% -> 10% of each run, Pallas kernels for 0% -> 35%
where the time goes in v1:
time: 1930 us; the launch traced here: 1920 us
  Pallas kernels  1110 us (58%)
  waiting for transfers between devices  303 us (16%)
  matrix products  152 us (8%)
  starting transfers between devices  150 us (8%)
  local copies, waits for them, and re-layouts  118 us (6%)
  other arithmetic  86.9 us (5%)
    pallas_call x9, Pallas kernels, put_together(): pl.pallas_call(body, out_shape=jax.ShapeDtypeStruct((blocks, part_rows, c...  1110 us
    ppermute x59, waiting for transfers between devices, over_layer(): lax.ppermute(value, 'shard', [(i, i ^ step * self.height) for i in range(...  146 us
    ppermute x19, waiting for transfers between devices, over_side(): lax.ppermute(value, 'rep', [(i, i ^ 2) for i in range(self.rep_size)])  116 us
    ppermute x59, starting transfers between devices, over_layer(): lax.ppermute(value, 'shard', [(i, i ^ step * self.height) for i in range(...  100 us
    unnamed x669, local copies, waits for them, and re-layouts  58.9 us
    dot_general x18, matrix products, left_product(): lax.dot_general(left, right, (((0,), (0,)), ((), ())), preferred_element_...  56.7 us
    dot_general x25, matrix products, product(): return jnp.dot(left, right, preferred_element_type=jnp.float32)  49.1 us
  transfers between devices with their start and end apart: 141, of which 50 were waited for; matrix products, arithmetic and copies ran while one was open for 10% of the time, Pallas kernels for 35%

profile of v1, /device:TPU:0, one launch (start us, length us, event | category | flops | bytes accessed | tf_op | source)
XLA Modules:
  0.0 1923.1 jit_solution(9722099359376398067)
XLA Ops:
  2.3 10.1 concatenate.104
  12.5 5.1 collective-permute-start.12
  40.5 4.2 copy.82
  50.1 2.9 collective-permute-start.32
  55.3 2.9 collective-permute-start.14
  65.7 4.6 collective-permute-start.48
  70.3 5.9 collective-permute-done.1
  77.9 2.8 collective-permute-start.38
  83.2 10.8 collective-permute-start.26
  94.0 3.9 collective-permute-done.39
  103.4 15.3 collective-permute-done.27
  123.0 14.7 collective-permute-done.21
  166.0 9.3 collective-permute-done.62
  180.0 5.6 collective-permute-done.3.refs_1_
  192.0 37.6 %put_together.10 = bf16[8,96,768]{2,1,0:T(8,128)(2,1)} custom-call(s32[4]{0:T(128)} %pad_add_fusion.64.coords_ref, bf16[4,96,384]{2,1,0:T(8,128)(2,1)} %copy-done.206, bf16[4,96,384]{2,1,0:T(8,128)(2,1)} %copy-done.228, bf16[4,96,384]{2,1,0:T(8,128)(2,1)} %copy-done.225, bf16[4,96,384]{2,1,0:T(8,128)(2,1)} %copy-done.236), custom_call_target="tpu_custom_call" | custom-call | tf_op jit(solution)/shard_map/put_together/pallas_call | solution.py:135
  229.7 37.7 %put_together.13 = bf16[8,96,768]{2,1,0:T(8,128)(2,1)} custom-call(s32[4]{0:T(128)} %pad_add_fusion.64.coords_ref, bf16[4,96,384]{2,1,0:T(8,128)(2,1)} %copy-done.205, bf16[4,96,384]{2,1,0:T(8,128)(2,1)} %copy-done.232, bf16[4,96,384]{2,1,0:T(8,128)(2,1)} %copy-done.229, bf16[4,96,384]{2,1,0:T(8,128)(2,1)} %copy-done.237), custom_call_target="tpu_custom_call" | custom-call | tf_op jit(solution)/shard_map/put_together/pallas_call | solution.py:135
  267.3 37.7 %put_together.16 = bf16[8,96,768]{2,1,0:T(8,128)(2,1)} custom-call(s32[4]{0:T(128)} %pad_add_fusion.64.coords_ref, bf16[4,96,384]{2,1,0:T(8,128)(2,1)} %copy-done.207, bf16[4,96,384]{2,1,0:T(8,128)(2,1)} %collective-permute-done.57.refs_1_, bf16[4,96,384]{2,1,0:T(8,128)(2,1)} %copy-done.233, bf16[4,96,384]{2,1,0:T(8,128)(2,1)} %copy-done.238), custom_call_target="tpu_custom_call" | custom-call | tf_op jit(solution)/shard_map/put_together/pallas_call | solution.py:135
  305.8 55.5 %put_together.15 = bf16[8,48,2304]{2,1,0:T(8,128)(2,1)} custom-call(s32[4]{0:T(128)} %pad_add_fusion.64.coords_ref, bf16[4,48,1152]{2,1,0:T(8,128)(2,1)} %copy-done.159, bf16[4,48,1152]{2,1,0:T(8,128)(2,1)} %collective-permute-done.51.refs_1_, bf16[4,48,1152]{2,1,0:T(8,128)(2,1)} %collective-permute-done.52.refs_2_, bf16[4,48,1152]{2,1,0:T(8,128)(2,1)} %copy-done.215), custom_call_target="tpu_custom_call" | custom-call | tf_op jit(solution)/shard_map/put_together/pallas_call | solution.py:135
  363.7 2.7 convolution_add_fusion.9
  368.0 6.3 collective-permute-done.43.refs_3_
  375.3 109.3 %put_together.9 = bf16[16,48,2304]{2,1,0:T(8,128)(2,1)} custom-call(s32[4]{0:T(128)} %pad_add_fusion.64.coords_ref, bf16[4,48,1152]{2,1,0:T(8,128)(2,1)} %copy-done.155, bf16[4,48,1152]{2,1,0:T(8,128)(2,1)} %collective-permute-done.3.refs_1_, bf16[4,48,1152]{2,1,0:T(8,128)(2,1)} %collective-permute-done.4.refs_2_, ...), custom_call_target="tpu_custom_call" | custom-call | tf_op jit(solution)/shard_map/put_together/pallas_call | solution.py:135
  484.6 3.7 fusion.20
  498.0 109.3 %put_together.14 = bf16[16,48,2304]{2,1,0:T(8,128)(2,1)} custom-call(s32[4]{0:T(128)} %pad_add_fusion.64.coords_ref, bf16[4,48,1152]{2,1,0:T(8,128)(2,1)} %copy-done.154, bf16[4,48,1152]{2,1,0:T(8,128)(2,1)} %collective-permute-done.41.refs_1_, bf16[4,48,1152]{2,1,0:T(8,128)(2,1)} %collective-permute-done.42.refs_2_, ...), custom_call_target="tpu_custom_call" | custom-call | tf_op jit(solution)/shard_map/put_together/pallas_call | solution.py:135
  607.3 6.8 add_bitcast_fusion.1
  627.9 4.3 add_bitcast_fusion
  651.8 144.8 %put_together.11 = bf16[8,96,3072]{2,1,0:T(8,128)(2,1)} custom-call(s32[4]{0:T(128)} %pad_add_fusion.64.coords_ref, bf16[4,96,1536]{2,1,0:T(8,128)(2,1)} %pad_maximum_fusion.7.refs_0_, bf16[4,96,1536]{2,1,0:T(8,128)(2,1)} %collective-permute-done.23.refs_1_, bf16[4,96,1536]{2,1,0:T(8,128)(2,1)} %collective-permute-done.24.refs_2_, ...), custom_call_target="tpu_custom_call" | custom-call | tf_op jit(solution)/shard_map/put_together/pallas_call | solution.py:135
  797.9 144.8 %put_together.12 = bf16[8,384,768]{2,1,0:T(8,128)(2,1)} custom-call(s32[4]{0:T(128)} %pad_add_fusion.64.coords_ref, bf16[4,384,384]{2,1,0:T(8,128)(2,1)} %pad_maximum_fusion.8.refs_0_, bf16[4,384,384]{2,1,0:T(8,128)(2,1)} %collective-permute-done.29.refs_1_, bf16[4,384,384]{2,1,0:T(8,128)(2,1)} %collective-permute-done.30.refs_2_, ...), custom_call_target="tpu_custom_call" | custom-call | tf_op jit(solution)/shard_map/put_together/pallas_call | solution.py:135
  942.8 11.5 multiply_convert_fusion.1
  959.7 430.9 %put_together.17 = bf16[16,96,4608]{2,1,0:T(8,128)(2,1)} custom-call(s32[4]{0:T(128)} %pad_add_fusion.64.coords_ref, bf16[4,96,2304]{2,1,0:T(8,128)(2,1)} %pad_maximum_fusion.5.refs_0_, bf16[4,96,2304]{2,1,0:T(8,128)(2,1)} %collective-permute-done.63.refs_1_, bf16[4,96,2304]{2,1,0:T(8,128)(2,1)} %collective-permute-done.64.refs_2_, ...), custom_call_target="tpu_custom_call" | custom-call | tf_op jit(solution)/shard_map/put_together/pallas_call | solution.py:135
  1390.6 7.3 fusion.625
  1398.6 3.6 multiply_multiply_fusion.10
  1409.7 9.4 fusion.39
  1419.1 3.0 convolution_add_fusion.18
  1428.3 2.7 convert_reduce_fusion.2
  1436.8 3.6 convolution_convert_fusion.7
  1495.5 8.9 fusion.22
  1511.2 6.6 fusion.32
  1539.3 6.2 fusion.36
  1558.7 3.1 convolution_convert_fusion.2
  1563.7 5.0 convolution_convert_fusion
  1568.7 3.4 copy.121
  1583.7 3.9 collective-permute-done.120
  1589.3 4.7 collective-permute-done.127
  1596.6 4.7 add_convert_fusion.6
  1606.1 3.5 collective-permute-done.122
  1618.8 2.9 collective-permute-done.86
  1634.2 5.1 collective-permute-done.116
  1639.4 3.7 collective-permute-done.115
  1644.4 3.5 collective-permute-done.117
  1654.6 9.4 add_convert_fusion.3
  1666.5 2.8 add_convert_fusion.2
  1671.0 2.7 add_convert_fusion.1
  1678.5 16.2 collective-permute-done.105
  1695.6 13.4 collective-permute-done.72
  1713.2 2.8 collective-permute-done.106
  1730.3 2.7 collective-permute-done.108
  1735.2 72.6 %collective-permute-done.110 = bf16[48,1152]{1,0:T(8,128)(2,1)S(1)} collective-permute-done((bf16[48,1152]{1,0:T(8,128)(2,1)S(1)}, bf16[48,1152]{1,0:T(8,128)(2,1)S(1)}, u32[]{:S(2)}, u32[]{:S(2)}) %collective-permute-start.110) | collective-permute-done | bytes 110624 | tf_op jit(solution)/shard_map/ppermute | solution.py:84
  1813.5 2.8 collective-permute-start.101
  1822.3 13.5 collective-permute-done.99
  1837.8 18.5 collective-permute-done.100
  1864.0 5.5 collective-permute-done.93
  1870.8 14.7 collective-permute-done.136
  1885.6 20.2 %collective-permute-done.137 = bf16[96,2304]{1,0:T(8,128)(2,1)S(1)} collective-permute-done((bf16[96,2304]{1,0:T(8,128)(2,1)S(1)}, bf16[96,2304]{1,0:T(8,128)(2,1)S(1)}, u32[]{:S(2)}, u32[]{:S(2)}) %collective-permute-start.137) | collective-permute-done | bytes 442400 | tf_op jit(solution)/shard_map/ppermute | solution.py:95
  1907.4 9.9 collective-permute-done.139
  (1290 shorter events, 373.9 us)
Async XLA Ops:
  12.5 32.3 %collective-permute-start.12 = (bf16[1,2496]{1,0:T(2,128)(2,1)S(1)}, bf16[1,2496]{1,0:T(2,128)(2,1)S(1)}, u32[]{:S(2)}, u32[]{:S(2)}) collective-permute-start(bf16[1,2496]{1,0:T(2,128)(2,1)S(1)} %broadcast_in_dim.297), channel_id=1, source_target_pairs={{0,6},{1,7},{2,4},{3,5},{4,2},{5,3},{6,0},{7,1},{8,14},{9,15},{10,... | collective-permute-start | bytes 14984 | tf_op jit(solution)/shard_map/ppermute | solution.py:95
  17.6 27.2 %collective-permute-start.11 = (bf16[1,2496]{1,0:T(2,128)(2,1)S(1)}, bf16[1,2496]{1,0:T(2,128)(2,1)S(1)}, u32[]{:S(2)}, u32[]{:S(2)}) collective-permute-start(bf16[1,2496]{1,0:T(2,128)(2,1)S(1)} %broadcast_in_dim.297), channel_id=1, source_target_pairs={{0,4},{1,5},{2,6},{3,7},{4,0},{5,1},{6,2},{7,3},{8,12},{9,13},{10,... | collective-permute-start | bytes 14984 | tf_op jit(solution)/shard_map/ppermute | solution.py:95
  17.6 28.6 %collective-permute-start.10 = (bf16[1,2496]{1,0:T(2,128)(2,1)S(1)}, bf16[1,2496]{1,0:T(2,128)(2,1)S(1)}, u32[]{:S(2)}, u32[]{:S(2)}) collective-permute-start(bf16[1,2496]{1,0:T(2,128)(2,1)S(1)} %broadcast_in_dim.297), channel_id=1, source_target_pairs={{0,2},{1,3},{2,0},{3,1},{4,6},{5,7},{6,4},{7,5},{8,10},{9,11},{10,... | collective-permute-start | bytes 14984 | tf_op jit(solution)/shard_map/ppermute | solution.py:95
  19.1 34.6 %collective-permute-start.55 = (bf16[96,384]{1,0:T(8,128)(2,1)S(1)}, bf16[96,384]{1,0:T(8,128)(2,1)S(1)}, u32[]{:S(2)}, u32[]{:S(2)}) collective-permute-start(bf16[96,384]{1,0:T(8,128)(2,1)S(1)} %constant_dynamic-slice_fusion.1), channel_id=1, source_target_pairs={{0,4},{1,5},{2,6},{3,7},{4,0},{5,1},{6,2},{7,3},{8,12},{9,13},{10,... | collective-permute-start | bytes 221192 | tf_op jit(solution)/shard_map/ppermute | solution.py:95
  21.4 32.5 %collective-permute-start.54 = (bf16[96,384]{1,0:T(8,128)(2,1)S(1)}, bf16[96,384]{1,0:T(8,128)(2,1)S(1)}, u32[]{:S(2)}, u32[]{:S(2)}) collective-permute-start(bf16[96,384]{1,0:T(8,128)(2,1)S(1)} %constant_dynamic-slice_fusion.1), channel_id=1, source_target_pairs={{0,2},{1,3},{2,0},{3,1},{4,6},{5,7},{6,4},{7,5},{8,10},{9,11},{10,... | collective-permute-start | bytes 221192 | tf_op jit(solution)/shard_map/ppermute | solution.py:95
  77.9 22.2 %collective-permute-start.38 = (bf16[48,1152]{1,0:T(8,128)(2,1)S(1)}, bf16[48,1152]{1,0:T(8,128)(2,1)S(1)}, u32[]{:S(2)}, u32[]{:S(2)}) collective-permute-start(bf16[48,1152]{1,0:T(8,128)(2,1)S(1)} %fusion.423), channel_id=1, source_target_pairs={{0,2},{1,3},{2,0},{3,1},{4,6},{5,7},{6,4},{7,5},{8,10},{9,11},{10,... | collective-permute-start | bytes 331784 | tf_op jit(solution)/shard_map/ppermute | solution.py:95
  83.0 35.7 %collective-permute-start.27 = (bf16[384,384]{1,0:T(8,128)(2,1)}, bf16[384,384]{1,0:T(8,128)(2,1)S(1)}, u32[]{:S(2)}, u32[]{:S(2)}) collective-permute-start(bf16[384,384]{1,0:T(8,128)(2,1)} %constant_dynamic-slice_fusion.4), channel_id=1, source_target_pairs={{0,4},{1,5},{2,6},{3,7},{4,0},{5,1},{6,2},{7,3},{8,12},{9,13},{10,... | collective-permute-start | bytes 884744 | tf_op jit(solution)/shard_map/ppermute | solution.py:95
  83.2 38.1 %collective-permute-start.26 = (bf16[384,384]{1,0:T(8,128)(2,1)}, bf16[384,384]{1,0:T(8,128)(2,1)S(1)}, u32[]{:S(2)}, u32[]{:S(2)}) collective-permute-start(bf16[384,384]{1,0:T(8,128)(2,1)} %constant_dynamic-slice_fusion.4), channel_id=1, source_target_pairs={{0,2},{1,3},{2,0},{3,1},{4,6},{5,7},{6,4},{7,5},{8,10},{9,11},{10,... | collective-permute-start | bytes 884744 | tf_op jit(solution)/shard_map/ppermute | solution.py:95
  97.9 23.6 %collective-permute-start.28 = (bf16[384,384]{1,0:T(8,128)(2,1)}, bf16[384,384]{1,0:T(8,128)(2,1)S(1)}, u32[]{:S(2)}, u32[]{:S(2)}) collective-permute-start(bf16[384,384]{1,0:T(8,128)(2,1)} %constant_dynamic-slice_fusion.4), channel_id=1, source_target_pairs={{0,6},{1,7},{2,4},{3,5},{4,2},{5,3},{6,0},{7,1},{8,14},{9,15},{10,... | collective-permute-start | bytes 884744 | tf_op jit(solution)/shard_map/ppermute | solution.py:95
  100.0 37.6 %collective-permute-start.21 = (bf16[96,1536]{1,0:T(8,128)(2,1)}, bf16[96,1536]{1,0:T(8,128)(2,1)S(1)}, u32[]{:S(2)}, u32[]{:S(2)}) collective-permute-start(bf16[96,1536]{1,0:T(8,128)(2,1)} %constant_dynamic-slice_fusion.5), channel_id=1, source_target_pairs={{0,4},{1,5},{2,6},{3,7},{4,0},{5,1},{6,2},{7,3},{8,12},{9,13},{10,... | collective-permute-start | bytes 884744 | tf_op jit(solution)/shard_map/ppermute | solution.py:95
  100.7 37.0 %collective-permute-start.20 = (bf16[96,1536]{1,0:T(8,128)(2,1)}, bf16[96,1536]{1,0:T(8,128)(2,1)S(1)}, u32[]{:S(2)}, u32[]{:S(2)}) collective-permute-start(bf16[96,1536]{1,0:T(8,128)(2,1)} %constant_dynamic-slice_fusion.5), channel_id=1, source_target_pairs={{0,2},{1,3},{2,0},{3,1},{4,6},{5,7},{6,4},{7,5},{8,10},{9,11},{10,... | collective-permute-start | bytes 884744 | tf_op jit(solution)/shard_map/ppermute | solution.py:95
  118.7 21.8 %collective-permute-start.22 = (bf16[96,1536]{1,0:T(8,128)(2,1)}, bf16[96,1536]{1,0:T(8,128)(2,1)S(1)}, u32[]{:S(2)}, u32[]{:S(2)}) collective-permute-start(bf16[96,1536]{1,0:T(8,128)(2,1)} %constant_dynamic-slice_fusion.5), channel_id=1, source_target_pairs={{0,6},{1,7},{2,4},{3,5},{4,2},{5,3},{6,0},{7,1},{8,14},{9,15},{10,... | collective-permute-start | bytes 884744 | tf_op jit(solution)/shard_map/ppermute | solution.py:95
  121.5 22.5 %collective-permute-start.17 = (bf16[4,96,384]{2,1,0:T(8,128)(2,1)S(1)}, bf16[4,96,384]{2,1,0:T(8,128)(2,1)S(1)}, u32[]{:S(2)}, u32[]{:S(2)}) collective-permute-start(bf16[4,96,384]{2,1,0:T(8,128)(2,1)S(1)} %pad_maximum_fusion.17.refs_0_), channel_id=1, source_target_pairs={{0,1},{1,0},{2,3},{3,2},{4,5},{5,4},{6,7},{7,6},{8,9},{9,8},{10,11... | collective-permute-start | bytes 884744 | tf_op jit(solution)/shard_map/ppermute | solution.py:92
  141.4 23.8 %collective-permute-start.61 = (bf16[96,2304]{1,0:T(8,128)(2,1)S(1)}, bf16[96,2304]{1,0:T(8,128)(2,1)S(1)}, u32[]{:S(2)}, u32[]{:S(2)}) collective-permute-start(bf16[96,2304]{1,0:T(8,128)(2,1)S(1)} %fusion.159), channel_id=1, source_target_pairs={{0,4},{1,5},{2,6},{3,7},{4,0},{5,1},{6,2},{7,3},{8,12},{9,13},{10,... | collective-permute-start | bytes 1327112 | tf_op jit(solution)/shard_map/ppermute | solution.py:95
  144.0 22.0 %collective-permute-start.60 = (bf16[96,2304]{1,0:T(8,128)(2,1)S(1)}, bf16[96,2304]{1,0:T(8,128)(2,1)}, u32[]{:S(2)}, u32[]{:S(2)}) collective-permute-start(bf16[96,2304]{1,0:T(8,128)(2,1)S(1)} %fusion.159), channel_id=1, source_target_pairs={{0,2},{1,3},{2,0},{3,1},{4,6},{5,7},{6,4},{7,5},{8,10},{9,11},{10,... | collective-permute-start | bytes 1327112 | tf_op jit(solution)/shard_map/ppermute | solution.py:95
  144.0 31.3 %collective-permute-start.62 = (bf16[96,2304]{1,0:T(8,128)(2,1)S(1)}, bf16[96,2304]{1,0:T(8,128)(2,1)}, u32[]{:S(2)}, u32[]{:S(2)}) collective-permute-start(bf16[96,2304]{1,0:T(8,128)(2,1)S(1)} %fusion.159), channel_id=1, source_target_pairs={{0,6},{1,7},{2,4},{3,5},{4,2},{5,3},{6,0},{7,1},{8,14},{9,15},{10,... | collective-permute-start | bytes 1327112 | tf_op jit(solution)/shard_map/ppermute | solution.py:95
  147.1 28.2 %collective-permute-start.52 = (bf16[4,48,1152]{2,1,0:T(8,128)(2,1)S(1)}, bf16[4,48,1152]{2,1,0:T(8,128)(2,1)}, u32[]{:S(2)}, u32[]{:S(2)}) collective-permute-start(bf16[4,48,1152]{2,1,0:T(8,128)(2,1)S(1)} %pad_maximum_fusion.15.refs_0_), channel_id=1, source_target_pairs={{0,8},{8,0},{16,24},{24,16},{1,9},{9,1},{17,25},{25,17},{2,10},{10... | collective-permute-start | bytes 1327112 | tf_op jit(solution)/shard_map/ppermute | solution.py:81
  178.3 183.0 %collective-permute-start.42 = (bf16[4,48,1152]{2,1,0:T(8,128)(2,1)S(1)}, bf16[4,48,1152]{2,1,0:T(8,128)(2,1)}, u32[]{:S(2)}, u32[]{:S(2)}) collective-permute-start(bf16[4,48,1152]{2,1,0:T(8,128)(2,1)S(1)} %pad_maximum_fusion.14.refs_0_), channel_id=1, source_target_pairs={{0,16},{8,24},{16,0},{24,8},{1,17},{9,25},{17,1},{25,9},{2,18},{10... | collective-permute-start | bytes 1327112 | tf_op jit(solution)/shard_map/ppermute | solution.py:84
  185.6 175.9 %collective-permute-start.41 = (bf16[4,48,1152]{2,1,0:T(8,128)(2,1)S(1)}, bf16[4,48,1152]{2,1,0:T(8,128)(2,1)}, u32[]{:S(2)}, u32[]{:S(2)}) collective-permute-start(bf16[4,48,1152]{2,1,0:T(8,128)(2,1)S(1)} %pad_maximum_fusion.14.refs_0_), channel_id=1, source_target_pairs={{0,1},{1,0},{2,3},{3,2},{4,5},{5,4},{6,7},{7,6},{8,9},{9,8},{10,11... | collective-permute-start | bytes 1327112 | tf_op jit(solution)/shard_map/ppermute | solution.py:92
  186.0 177.2 %collective-permute-start.4 = (bf16[4,48,1152]{2,1,0:T(8,128)(2,1)S(1)}, bf16[4,48,1152]{2,1,0:T(8,128)(2,1)}, u32[]{:S(2)}, u32[]{:S(2)}) collective-permute-start(bf16[4,48,1152]{2,1,0:T(8,128)(2,1)S(1)} %pad_maximum_fusion.13.refs_0_), channel_id=1, source_target_pairs={{0,16},{8,24},{16,0},{24,8},{1,17},{9,25},{17,1},{25,9},{2,18},{10... | collective-permute-start | bytes 1327112 | tf_op jit(solution)/shard_map/ppermute | solution.py:84
  187.6 117.4 %collective-permute-start.53 = (bf16[4,48,1152]{2,1,0:T(8,128)(2,1)}, bf16[4,48,1152]{2,1,0:T(8,128)(2,1)S(1)}, u32[]{:S(2)}, u32[]{:S(2)}) collective-permute-start(bf16[4,48,1152]{2,1,0:T(8,128)(2,1)} %collective-permute-done.51.refs_1_), channel_id=1, source_target_pairs={{0,8},{8,0},{16,24},{24,16},{1,9},{9,1},{17,25},{25,17},{2,10},{10... | collective-permute-start | bytes 1327112 | tf_op jit(solution)/shard_map/ppermute | solution.py:81
  187.7 175.6 %collective-permute-start.5 = (bf16[4,48,1152]{2,1,0:T(8,128)(2,1)}, bf16[4,48,1152]{2,1,0:T(8,128)(2,1)}, u32[]{:S(2)}, u32[]{:S(2)}) collective-permute-start(bf16[4,48,1152]{2,1,0:T(8,128)(2,1)} %collective-permute-done.3.refs_1_), channel_id=1, source_target_pairs={{0,16},{8,24},{16,0},{24,8},{1,17},{9,25},{17,1},{25,9},{2,18},{10... | collective-permute-start | bytes 1327112 | tf_op jit(solution)/shard_map/ppermute | solution.py:84
  305.0 62.8 %collective-permute-start.6 = (bf16[4,48,1152]{2,1,0:T(8,128)(2,1)S(1)}, bf16[4,48,1152]{2,1,0:T(8,128)(2,1)}, u32[]{:S(2)}, u32[]{:S(2)}) collective-permute-start(bf16[4,48,1152]{2,1,0:T(8,128)(2,1)S(1)} %pad_maximum_fusion.13.refs_0_), channel_id=1, source_target_pairs={{0,8},{8,0},{16,24},{24,16},{1,9},{9,1},{17,25},{25,17},{2,10},{10... | collective-permute-start | bytes 1327112 | tf_op jit(solution)/shard_map/ppermute | solution.py:81
  367.9 124.8 %collective-permute-start.44 = (bf16[4,48,1152]{2,1,0:T(8,128)(2,1)S(1)}, bf16[4,48,1152]{2,1,0:T(8,128)(2,1)}, u32[]{:S(2)}, u32[]{:S(2)}) collective-permute-start(bf16[4,48,1152]{2,1,0:T(8,128)(2,1)S(1)} %pad_maximum_fusion.14.refs_0_), channel_id=1, source_target_pairs={{0,8},{8,0},{16,24},{24,16},{1,9},{9,1},{17,25},{25,17},{2,10},{10... | collective-permute-start | bytes 1327112 | tf_op jit(solution)/shard_map/ppermute | solution.py:81
  374.3 272.2 %collective-permute-start.24 = (bf16[4,96,1536]{2,1,0:T(8,128)(2,1)}, bf16[4,96,1536]{2,1,0:T(8,128)(2,1)}, u32[]{:S(2)}, u32[]{:S(2)}) collective-permute-start(bf16[4,96,1536]{2,1,0:T(8,128)(2,1)} %pad_maximum_fusion.7.refs_0_), channel_id=1, source_target_pairs={{0,8},{8,0},{16,24},{24,16},{1,9},{9,1},{17,25},{25,17},{2,10},{10... | collective-permute-start | bytes 3538952 | tf_op jit(solution)/shard_map/ppermute | solution.py:81
  374.3 120.5 %collective-permute-start.45 = (bf16[4,48,1152]{2,1,0:T(8,128)(2,1)}, bf16[4,48,1152]{2,1,0:T(8,128)(2,1)}, u32[]{:S(2)}, u32[]{:S(2)}) collective-permute-start(bf16[4,48,1152]{2,1,0:T(8,128)(2,1)} %collective-permute-done.41.refs_1_), channel_id=1, source_target_pairs={{0,8},{8,0},{16,24},{24,16},{1,9},{9,1},{17,25},{25,17},{2,10},{10... | collective-permute-start | bytes 1327112 | tf_op jit(solution)/shard_map/ppermute | solution.py:81
  374.8 119.6 %collective-permute-start.46 = (bf16[4,48,1152]{2,1,0:T(8,128)(2,1)}, bf16[4,48,1152]{2,1,0:T(8,128)(2,1)}, u32[]{:S(2)}, u32[]{:S(2)}) collective-permute-start(bf16[4,48,1152]{2,1,0:T(8,128)(2,1)} %collective-permute-done.42.refs_2_), channel_id=1, source_target_pairs={{0,8},{8,0},{16,24},{24,16},{1,9},{9,1},{17,25},{25,17},{2,10},{10... | collective-permute-start | bytes 1327112 | tf_op jit(solution)/shard_map/ppermute | solution.py:81
  374.9 121.6 %collective-permute-start.47 = (bf16[4,48,1152]{2,1,0:T(8,128)(2,1)}, bf16[4,48,1152]{2,1,0:T(8,128)(2,1)}, u32[]{:S(2)}, u32[]{:S(2)}) collective-permute-start(bf16[4,48,1152]{2,1,0:T(8,128)(2,1)} %collective-permute-done.43.refs_3_), channel_id=1, source_target_pairs={{0,8},{8,0},{16,24},{24,16},{1,9},{9,1},{17,25},{25,17},{2,10},{10... | collective-permute-start | bytes 1327112 | tf_op jit(solution)/shard_map/ppermute | solution.py:81
  492.7 153.9 %collective-permute-start.23 = (bf16[4,96,1536]{2,1,0:T(8,128)(2,1)}, bf16[4,96,1536]{2,1,0:T(8,128)(2,1)}, u32[]{:S(2)}, u32[]{:S(2)}) collective-permute-start(bf16[4,96,1536]{2,1,0:T(8,128)(2,1)} %pad_maximum_fusion.7.refs_0_), channel_id=1, source_target_pairs={{0,1},{1,0},{2,3},{3,2},{4,5},{5,4},{6,7},{7,6},{8,9},{9,8},{10,11... | collective-permute-start | bytes 3538952 | tf_op jit(solution)/shard_map/ppermute | solution.py:92
  494.5 152.6 %collective-permute-start.29 = (bf16[4,384,384]{2,1,0:T(8,128)(2,1)}, bf16[4,384,384]{2,1,0:T(8,128)(2,1)}, u32[]{:S(2)}, u32[]{:S(2)}) collective-permute-start(bf16[4,384,384]{2,1,0:T(8,128)(2,1)} %pad_maximum_fusion.8.refs_0_), channel_id=1, source_target_pairs={{0,1},{1,0},{2,3},{3,2},{4,5},{5,4},{6,7},{7,6},{8,9},{9,8},{10,11... | collective-permute-start | bytes 3538952 | tf_op jit(solution)/shard_map/ppermute | solution.py:92
  494.8 302.9 %collective-permute-start.64 = (bf16[4,96,2304]{2,1,0:T(8,128)(2,1)}, bf16[4,96,2304]{2,1,0:T(8,128)(2,1)}, u32[]{:S(2)}, u32[]{:S(2)}) collective-permute-start(bf16[4,96,2304]{2,1,0:T(8,128)(2,1)} %pad_maximum_fusion.5.refs_0_), channel_id=1, source_target_pairs={{0,16},{8,24},{16,0},{24,8},{1,17},{9,25},{17,1},{25,9},{2,18},{10... | collective-permute-start | bytes 5308424 | tf_op jit(solution)/shard_map/ppermute | solution.py:84
  496.5 154.8 %collective-permute-start.63 = (bf16[4,96,2304]{2,1,0:T(8,128)(2,1)}, bf16[4,96,2304]{2,1,0:T(8,128)(2,1)}, u32[]{:S(2)}, u32[]{:S(2)}) collective-permute-start(bf16[4,96,2304]{2,1,0:T(8,128)(2,1)} %pad_maximum_fusion.5.refs_0_), channel_id=1, source_target_pairs={{0,1},{1,0},{2,3},{3,2},{4,5},{5,4},{6,7},{7,6},{8,9},{9,8},{10,11... | collective-permute-start | bytes 5308424 | tf_op jit(solution)/shard_map/ppermute | solution.py:92
  646.5 150.2 %collective-permute-start.30 = (bf16[4,384,384]{2,1,0:T(8,128)(2,1)}, bf16[4,384,384]{2,1,0:T(8,128)(2,1)}, u32[]{:S(2)}, u32[]{:S(2)}) collective-permute-start(bf16[4,384,384]{2,1,0:T(8,128)(2,1)} %pad_maximum_fusion.8.refs_0_), channel_id=1, source_target_pairs={{0,8},{8,0},{16,24},{24,16},{1,9},{9,1},{17,25},{25,17},{2,10},{10... | collective-permute-start | bytes 3538952 | tf_op jit(solution)/shard_map/ppermute | solution.py:81
  647.1 150.8 %collective-permute-start.31 = (bf16[4,384,384]{2,1,0:T(8,128)(2,1)}, bf16[4,384,384]{2,1,0:T(8,128)(2,1)}, u32[]{:S(2)}, u32[]{:S(2)}) collective-permute-start(bf16[4,384,384]{2,1,0:T(8,128)(2,1)} %collective-permute-done.29.refs_1_), channel_id=1, source_target_pairs={{0,8},{8,0},{16,24},{24,16},{1,9},{9,1},{17,25},{25,17},{2,10},{10... | collective-permute-start | bytes 3538952 | tf_op jit(solution)/shard_map/ppermute | solution.py:81
  651.2 308.5 %collective-permute-start.66 = (bf16[4,96,2304]{2,1,0:T(8,128)(2,1)}, bf16[4,96,2304]{2,1,0:T(8,128)(2,1)}, u32[]{:S(2)}, u32[]{:S(2)}) collective-permute-start(bf16[4,96,2304]{2,1,0:T(8,128)(2,1)} %pad_maximum_fusion.5.refs_0_), channel_id=1, source_target_pairs={{0,8},{8,0},{16,24},{24,16},{1,9},{9,1},{17,25},{25,17},{2,10},{10... | collective-permute-start | bytes 5308424 | tf_op jit(solution)/shard_map/ppermute | solution.py:81
  651.7 308.0 %collective-permute-start.67 = (bf16[4,96,2304]{2,1,0:T(8,128)(2,1)}, bf16[4,96,2304]{2,1,0:T(8,128)(2,1)}, u32[]{:S(2)}, u32[]{:S(2)}) collective-permute-start(bf16[4,96,2304]{2,1,0:T(8,128)(2,1)} %collective-permute-done.63.refs_1_), channel_id=1, source_target_pairs={{0,8},{8,0},{16,24},{24,16},{1,9},{9,1},{17,25},{25,17},{2,10},{10... | collective-permute-start | bytes 5308424 | tf_op jit(solution)/shard_map/ppermute | solution.py:81
  796.7 157.6 %collective-permute-start.65 = (bf16[4,96,2304]{2,1,0:T(8,128)(2,1)}, bf16[4,96,2304]{2,1,0:T(8,128)(2,1)}, u32[]{:S(2)}, u32[]{:S(2)}) collective-permute-start(bf16[4,96,2304]{2,1,0:T(8,128)(2,1)} %collective-permute-done.63.refs_1_), channel_id=1, source_target_pairs={{0,16},{8,24},{16,0},{24,8},{1,17},{9,25},{17,1},{25,9},{2,18},{10... | collective-permute-start | bytes 5308424 | tf_op jit(solution)/shard_map/ppermute | solution.py:84
  797.7 162.0 %collective-permute-start.68 = (bf16[4,96,2304]{2,1,0:T(8,128)(2,1)}, bf16[4,96,2304]{2,1,0:T(8,128)(2,1)}, u32[]{:S(2)}, u32[]{:S(2)}) collective-permute-start(bf16[4,96,2304]{2,1,0:T(8,128)(2,1)} %collective-permute-done.64.refs_2_), channel_id=1, source_target_pairs={{0,8},{8,0},{16,24},{24,16},{1,9},{9,1},{17,25},{25,17},{2,10},{10... | collective-permute-start | bytes 5308424 | tf_op jit(solution)/shard_map/ppermute | solution.py:81
  1549.5 26.0 %collective-permute-start.119 = (bf16[768,384]{1,0:T(8,128)(2,1)}, bf16[768,384]{1,0:T(8,128)(2,1)}, u32[]{:S(2)}, u32[]{:S(2)}) collective-permute-start(bf16[768,384]{1,0:T(8,128)(2,1)} %convolution_convert_fusion.5), channel_id=1, source_target_pairs={{0,8},{8,0},{16,24},{24,16},{1,9},{9,1},{17,25},{25,17},{2,10},{10... | collective-permute-start | bytes 1769480 | tf_op jit(solution)/shard_map/ppermute | solution.py:81
  1553.2 24.5 %collective-permute-start.126 = (bf16[768,384]{1,0:T(8,128)(2,1)}, bf16[768,384]{1,0:T(8,128)(2,1)}, u32[]{:S(2)}, u32[]{:S(2)}) collective-permute-start(bf16[768,384]{1,0:T(8,128)(2,1)} %convolution_convert_fusion.4), channel_id=1, source_target_pairs={{0,8},{8,0},{16,24},{24,16},{1,9},{9,1},{17,25},{25,17},{2,10},{10... | collective-permute-start | bytes 1769480 | tf_op jit(solution)/shard_map/ppermute | solution.py:81
  1553.2 28.3 %collective-permute-start.83 = (bf16[768,384]{1,0:T(8,128)(2,1)}, bf16[768,384]{1,0:T(8,128)(2,1)}, u32[]{:S(2)}, u32[]{:S(2)}) collective-permute-start(bf16[768,384]{1,0:T(8,128)(2,1)} %convolution_convert_fusion.6), channel_id=1, source_target_pairs={{0,8},{8,0},{16,24},{24,16},{1,9},{9,1},{17,25},{25,17},{2,10},{10... | collective-permute-start | bytes 1769480 | tf_op jit(solution)/shard_map/ppermute | solution.py:81
  1561.7 104.8 %collective-permute-start.90 = (bf16[768,1536]{1,0:T(8,128)(2,1)}, bf16[768,1536]{1,0:T(8,128)(2,1)}, u32[]{:S(2)}, u32[]{:S(2)}) collective-permute-start(bf16[768,1536]{1,0:T(8,128)(2,1)} %convolution_convert_fusion.2), channel_id=1, source_target_pairs={{0,8},{8,0},{16,24},{24,16},{1,9},{9,1},{17,25},{25,17},{2,10},{10... | collective-permute-start | bytes 7077896 | tf_op jit(solution)/shard_map/ppermute | solution.py:81
  1572.2 98.9 %collective-permute-start.97 = (bf16[3072,384]{1,0:T(8,128)(2,1)}, bf16[3072,384]{1,0:T(8,128)(2,1)}, u32[]{:S(2)}, u32[]{:S(2)}) collective-permute-start(bf16[3072,384]{1,0:T(8,128)(2,1)} %convolution_convert_fusion.1), channel_id=1, source_target_pairs={{0,8},{8,0},{16,24},{24,16},{1,9},{9,1},{17,25},{25,17},{2,10},{10... | collective-permute-start | bytes 7077896 | tf_op jit(solution)/shard_map/ppermute | solution.py:81
  1639.4 84.1 %collective-permute-start.133 = (bf16[1536,2304]{1,0:T(8,128)(2,1)S(1)}, bf16[1536,2304]{1,0:T(8,128)(2,1)S(1)}, u32[]{:S(2)}, u32[]{:S(2)}) collective-permute-start(bf16[1536,2304]{1,0:T(8,128)(2,1)S(1)} %bitcast.446), channel_id=1, source_target_pairs={{0,8},{8,0},{16,24},{24,16},{1,9},{9,1},{17,25},{25,17},{2,10},{10... | collective-permute-start | bytes 21233672 | tf_op jit(solution)/shard_map/ppermute | solution.py:81
  1653.6 22.8 %collective-permute-start.71 = (bf16[8,48,1152]{2,1,0:T(8,128)(2,1)}, bf16[8,48,1152]{2,1,0:T(8,128)(2,1)}, u32[]{:S(2)}, u32[]{:S(2)}) collective-permute-start(bf16[8,48,1152]{2,1,0:T(8,128)(2,1)} %dynamic-slice_bitcast_fusion.5), channel_id=1, source_target_pairs={{0,16},{8,24},{16,0},{24,8},{1,17},{9,25},{17,1},{25,9},{2,18},{10... | collective-permute-start | bytes 2654216 | tf_op jit(solution)/shard_map/ppermute | solution.py:84
  1665.4 29.3 %collective-permute-start.105 = (bf16[8,48,1152]{2,1,0:T(8,128)(2,1)S(1)}, bf16[8,48,1152]{2,1,0:T(8,128)(2,1)S(1)}, u32[]{:S(2)}, u32[]{:S(2)}) collective-permute-start(bf16[8,48,1152]{2,1,0:T(8,128)(2,1)S(1)} %dynamic-slice_bitcast_fusion.4), channel_id=1, source_target_pairs={{0,16},{8,24},{16,0},{24,8},{1,17},{9,25},{17,1},{25,9},{2,18},{10... | collective-permute-start | bytes 2654216 | tf_op jit(solution)/shard_map/ppermute | solution.py:84
  1670.5 137.5 %collective-permute-start.91 = (bf16[4,96,1536]{2,1,0:T(8,128)(2,1)}, bf16[4,96,1536]{2,1,0:T(8,128)(2,1)}, u32[]{:S(2)}, u32[]{:S(2)}) collective-permute-start(bf16[4,96,1536]{2,1,0:T(8,128)(2,1)} %dynamic-slice_bitcast_fusion.3), channel_id=1, source_target_pairs={{0,1},{1,0},{2,3},{3,2},{4,5},{5,4},{6,7},{7,6},{8,9},{9,8},{10,11... | collective-permute-start | bytes 3538952 | tf_op jit(solution)/shard_map/ppermute | solution.py:92
  1677.9 31.1 %collective-permute-start.72 = (bf16[4,48,1152]{2,1,0:T(8,128)(2,1)S(1)}, bf16[4,48,1152]{2,1,0:T(8,128)(2,1)S(1)}, u32[]{:S(2)}, u32[]{:S(2)}) collective-permute-start(bf16[4,48,1152]{2,1,0:T(8,128)(2,1)S(1)} %dynamic-slice_bitcast_fusion.11), channel_id=1, source_target_pairs={{0,1},{1,0},{2,3},{3,2},{4,5},{5,4},{6,7},{7,6},{8,9},{9,8},{10,11... | collective-permute-start | bytes 1327112 | tf_op jit(solution)/shard_map/ppermute | solution.py:92
  1719.4 92.1 %collective-permute-start.98 = (bf16[4,384,384]{2,1,0:T(8,128)(2,1)}, bf16[4,384,384]{2,1,0:T(8,128)(2,1)}, u32[]{:S(2)}, u32[]{:S(2)}) collective-permute-start(bf16[4,384,384]{2,1,0:T(8,128)(2,1)} %dynamic-slice_bitcast_fusion.2), channel_id=1, source_target_pairs={{0,1},{1,0},{2,3},{3,2},{4,5},{5,4},{6,7},{7,6},{8,9},{9,8},{10,11... | collective-permute-start | bytes 3538952 | tf_op jit(solution)/shard_map/ppermute | solution.py:92
  1729.2 87.1 %collective-permute-start.134 = (bf16[8,96,2304]{2,1,0:T(8,128)(2,1)S(1)}, bf16[8,96,2304]{2,1,0:T(8,128)(2,1)S(1)}, u32[]{:S(2)}, u32[]{:S(2)}) collective-permute-start(bf16[8,96,2304]{2,1,0:T(8,128)(2,1)S(1)} %dynamic-slice_bitcast_fusion), channel_id=1, source_target_pairs={{0,16},{8,24},{16,0},{24,8},{1,17},{9,25},{17,1},{25,9},{2,18},{10... | collective-permute-start | bytes 10616840 | tf_op jit(solution)/shard_map/ppermute | solution.py:84
  1734.1 73.8 %collective-permute-start.110 = (bf16[48,1152]{1,0:T(8,128)(2,1)S(1)}, bf16[48,1152]{1,0:T(8,128)(2,1)S(1)}, u32[]{:S(2)}, u32[]{:S(2)}) collective-permute-start(bf16[48,1152]{1,0:T(8,128)(2,1)S(1)} %fusion.389), channel_id=1, source_target_pairs={{0,16},{8,24},{16,0},{24,8},{1,17},{9,25},{17,1},{25,9},{2,18},{10... | collective-permute-start | bytes 331784 | tf_op jit(solution)/shard_map/ppermute | solution.py:84
  1735.1 78.3 %collective-permute-start.77 = (bf16[96,1152]{1,0:T(8,128)(2,1)S(1)}, bf16[96,1152]{1,0:T(8,128)(2,1)S(1)}, u32[]{:S(2)}, u32[]{:S(2)}) collective-permute-start(bf16[96,1152]{1,0:T(8,128)(2,1)S(1)} %pad_maximum_fusion.20), channel_id=1, source_target_pairs={{0,8},{8,0},{16,24},{24,16},{1,9},{9,1},{17,25},{25,17},{2,10},{10... | collective-permute-start | bytes 663560 | tf_op jit(solution)/shard_map/ppermute | solution.py:81
  1809.7 50.5 %collective-permute-start.92 = (bf16[96,1536]{1,0:T(8,128)(2,1)S(1)}, bf16[96,1536]{1,0:T(8,128)(2,1)S(1)}, u32[]{:S(2)}, u32[]{:S(2)}) collective-permute-start(bf16[96,1536]{1,0:T(8,128)(2,1)S(1)} %get-tuple-element.234), channel_id=1, source_target_pairs={{0,2},{1,3},{2,0},{3,1},{4,6},{5,7},{6,4},{7,5},{8,10},{9,11},{10,... | collective-permute-start | bytes 884744 | tf_op jit(solution)/shard_map/ppermute | solution.py:95
  1813.2 22.6 %collective-permute-start.99 = (bf16[384,384]{1,0:T(8,128)(2,1)S(1)}, bf16[384,384]{1,0:T(8,128)(2,1)S(1)}, u32[]{:S(2)}, u32[]{:S(2)}) collective-permute-start(bf16[384,384]{1,0:T(8,128)(2,1)S(1)} %get-tuple-element.231), channel_id=1, source_target_pairs={{0,2},{1,3},{2,0},{3,1},{4,6},{5,7},{6,4},{7,5},{8,10},{9,11},{10,... | collective-permute-start | bytes 884744 | tf_op jit(solution)/shard_map/ppermute | solution.py:95
  1813.5 24.3 %collective-permute-start.101 = (bf16[384,384]{1,0:T(8,128)(2,1)S(1)}, bf16[384,384]{1,0:T(8,128)(2,1)S(1)}, u32[]{:S(2)}, u32[]{:S(2)}) collective-permute-start(bf16[384,384]{1,0:T(8,128)(2,1)S(1)} %get-tuple-element.232), channel_id=1, source_target_pairs={{0,6},{1,7},{2,4},{3,5},{4,2},{5,3},{6,0},{7,1},{8,14},{9,15},{10,... | collective-permute-start | bytes 884744 | tf_op jit(solution)/shard_map/ppermute | solution.py:95
  1816.4 39.9 %collective-permute-start.100 = (bf16[384,384]{1,0:T(8,128)(2,1)S(1)}, bf16[384,384]{1,0:T(8,128)(2,1)S(1)}, u32[]{:S(2)}, u32[]{:S(2)}) collective-permute-start(bf16[384,384]{1,0:T(8,128)(2,1)S(1)} %get-tuple-element.233), channel_id=1, source_target_pairs={{0,4},{1,5},{2,6},{3,7},{4,0},{5,1},{6,2},{7,3},{8,12},{9,13},{10,... | collective-permute-start | bytes 884744 | tf_op jit(solution)/shard_map/ppermute | solution.py:95
  1817.9 40.4 %collective-permute-start.135 = (bf16[4,96,2304]{2,1,0:T(8,128)(2,1)S(1)}, bf16[4,96,2304]{2,1,0:T(8,128)(2,1)S(1)}, u32[]{:S(2)}, u32[]{:S(2)}) collective-permute-start(bf16[4,96,2304]{2,1,0:T(8,128)(2,1)S(1)} %dynamic-slice_bitcast_fusion.1), channel_id=1, source_target_pairs={{0,1},{1,0},{2,3},{3,2},{4,5},{5,4},{6,7},{7,6},{8,9},{9,8},{10,11... | collective-permute-start | bytes 5308424 | tf_op jit(solution)/shard_map/ppermute | solution.py:92
  1835.8 26.6 %collective-permute-start.94 = (bf16[96,1536]{1,0:T(8,128)(2,1)S(1)}, bf16[96,1536]{1,0:T(8,128)(2,1)S(1)}, u32[]{:S(2)}, u32[]{:S(2)}) collective-permute-start(bf16[96,1536]{1,0:T(8,128)(2,1)S(1)} %get-tuple-element.235), channel_id=1, source_target_pairs={{0,6},{1,7},{2,4},{3,5},{4,2},{5,3},{6,0},{7,1},{8,14},{9,15},{10,... | collective-permute-start | bytes 884744 | tf_op jit(solution)/shard_map/ppermute | solution.py:95
  1837.8 31.7 %collective-permute-start.93 = (bf16[96,1536]{1,0:T(8,128)(2,1)S(1)}, bf16[96,1536]{1,0:T(8,128)(2,1)S(1)}, u32[]{:S(2)}, u32[]{:S(2)}) collective-permute-start(bf16[96,1536]{1,0:T(8,128)(2,1)S(1)} %get-tuple-element.236), channel_id=1, source_target_pairs={{0,4},{1,5},{2,6},{3,7},{4,0},{5,1},{6,2},{7,3},{8,12},{9,13},{10,... | collective-permute-start | bytes 884744 | tf_op jit(solution)/shard_map/ppermute | solution.py:95
  1858.9 26.7 %collective-permute-start.136 = (bf16[96,2304]{1,0:T(8,128)(2,1)S(1)}, bf16[96,2304]{1,0:T(8,128)(2,1)S(1)}, u32[]{:S(2)}, u32[]{:S(2)}) collective-permute-start(bf16[96,2304]{1,0:T(8,128)(2,1)S(1)} %get-tuple-element.209), channel_id=1, source_target_pairs={{0,2},{1,3},{2,0},{3,1},{4,6},{5,7},{6,4},{7,5},{8,10},{9,11},{10,... | collective-permute-start | bytes 1327112 | tf_op jit(solution)/shard_map/ppermute | solution.py:95
  1860.2 25.4 %collective-permute-start.138 = (bf16[96,2304]{1,0:T(8,128)(2,1)S(1)}, bf16[96,2304]{1,0:T(8,128)(2,1)S(1)}, u32[]{:S(2)}, u32[]{:S(2)}) collective-permute-start(bf16[96,2304]{1,0:T(8,128)(2,1)S(1)} %get-tuple-element.210), channel_id=1, source_target_pairs={{0,6},{1,7},{2,4},{3,5},{4,2},{5,3},{6,0},{7,1},{8,14},{9,15},{10,... | collective-permute-start | bytes 1327112 | tf_op jit(solution)/shard_map/ppermute | solution.py:95
  1862.4 43.5 %collective-permute-start.137 = (bf16[96,2304]{1,0:T(8,128)(2,1)S(1)}, bf16[96,2304]{1,0:T(8,128)(2,1)S(1)}, u32[]{:S(2)}, u32[]{:S(2)}) collective-permute-start(bf16[96,2304]{1,0:T(8,128)(2,1)S(1)} %get-tuple-element.211), channel_id=1, source_target_pairs={{0,4},{1,5},{2,6},{3,7},{4,0},{5,1},{6,2},{7,3},{8,12},{9,13},{10,... | collective-permute-start | bytes 1327112 | tf_op jit(solution)/shard_map/ppermute | solution.py:95
  1869.6 37.5 %collective-permute-start.95 = (bf16[96,1536]{1,0:T(8,128)(2,1)S(1)}, bf16[96,1536]{1,0:T(8,128)(2,1)S(1)}, u32[]{:S(2)}, u32[]{:S(2)}) collective-permute-start(bf16[96,1536]{1,0:T(8,128)(2,1)S(1)} %fusion.152), channel_id=1, source_target_pairs={{0,16},{8,24},{16,0},{24,8},{1,17},{9,25},{17,1},{25,9},{2,18},{10... | collective-permute-start | bytes 884744 | tf_op jit(solution)/shard_map/ppermute | solution.py:84
  1870.8 36.5 %collective-permute-start.103 = (bf16[384,384]{1,0:T(8,128)(2,1)S(1)}, bf16[384,384]{1,0:T(8,128)(2,1)S(1)}, u32[]{:S(2)}, u32[]{:S(2)}) collective-permute-start(bf16[384,384]{1,0:T(8,128)(2,1)S(1)} %add_convert_fusion.13), channel_id=1, source_target_pairs={{0,8},{8,0},{16,24},{24,16},{1,9},{9,1},{17,25},{25,17},{2,10},{10... | collective-permute-start | bytes 884744 | tf_op jit(solution)/shard_map/ppermute | solution.py:81
  (404 other events, 4574.6 us)

commit v2 on v1

--- a/solution.py
+++ b/solution.py
@@ -137,7 +137,7 @@
         out_shape=jax.ShapeDtypeStruct((blocks, part_rows, columns), flat[0].dtype),
         in_specs=[pl.BlockSpec(memory_space=pltpu.SMEM)]
         + [pl.BlockSpec(memory_space=pl.ANY)] * len(flat),
-        out_specs=pl.BlockSpec(memory_space=pl.ANY),
+        out_specs=pl.BlockSpec(memory_space=pltpu.VMEM),
         scratch_shapes=[pltpu.SemaphoreType.DMA((len(flat) * depth,))],
         name="put_together",
     )(place.coords, *flat)

time: 1930 us -> 937 us (0.49)
  Pallas kernels: 1110 us -> 44.1 us
  waiting for transfers between devices: 303 us -> 356 us
    pallas_call x9, Pallas kernels: 1110 us -> 44.1 us  [put_together(): pl.pallas_call(body, out_shape=jax.ShapeDtypeStruct((blocks, part_rows, c...]
    ppermute x20, waiting for transfers between devices: 36.5 us -> 72.9 us  [over_row(): lax.ppermute(value, 'shard', [(i, i ^ step) for i in range(self.shard_siz...]
    ppermute x19, waiting for transfers between devices: 116 us -> 136 us  [over_side(): lax.ppermute(value, 'rep', [(i, i ^ 2) for i in range(self.rep_size)])]
  transfers between devices with their start and end apart: 141 -> 141, of which waited for: 50 -> 50; matrix products, arithmetic and copies ran while one was open for 10% -> 20% of each run, Pallas kernels for 35% -> 4%
where the time goes in v2:
time: 937 us; the launch traced here: 926 us
  waiting for transfers between devices  356 us (38%)
  starting transfers between devices  163 us (17%)
  matrix products  152 us (16%)
  local copies, waits for them, and re-layouts  118 us (13%)
  other arithmetic  86.9 us (9%)
  Pallas kernels  44.1 us (5%)
    ppermute x59, waiting for transfers between devices, over_layer(): lax.ppermute(value, 'shard', [(i, i ^ step * self.height) for i in range(...  144 us
    ppermute x19, waiting for transfers between devices, over_side(): lax.ppermute(value, 'rep', [(i, i ^ 2) for i in range(self.rep_size)])  136 us
    ppermute x59, starting transfers between devices, over_layer(): lax.ppermute(value, 'shard', [(i, i ^ step * self.height) for i in range(...  105 us
    ppermute x20, waiting for transfers between devices, over_row(): lax.ppermute(value, 'shard', [(i, i ^ step) for i in range(self.shard_siz...  72.9 us
    unnamed x669, local copies, waits for them, and re-layouts  59.1 us
    dot_general x18, matrix products, left_product(): lax.dot_general(left, right, (((0,), (0,)), ((), ())), preferred_element_...  56.6 us
    dot_general x25, matrix products, product(): return jnp.dot(left, right, preferred_element_type=jnp.float32)  49 us
    pallas_call x9, Pallas kernels, put_together(): pl.pallas_call(body, out_shape=jax.ShapeDtypeStruct((blocks, part_rows, c...  44.1 us
  transfers between devices with their start and end apart: 141, of which 50 were waited for; matrix products, arithmetic and copies ran while one was open for 20% of the time, Pallas kernels for 4%

profile of v2, /device:TPU:0, one launch (start us, length us, event | category | flops | bytes accessed | tf_op | source)
XLA Modules:
  0.0 925.9 jit_solution(6103763570271689697)
XLA Ops:
  2.3 10.1 %concatenate.104 = bf16[2496]{0:T(1024)(128)(2,1)S(1)} concatenate(bf16[192]{0:T(256)(128)(2,1)} %param.39, bf16[96]{0:T(256)(128)(2,1)} %param.41, bf16[96]{0:T(256)(128)(2,1)} %param.42, bf16[96]{0:T(256)(128)(2,1)} %param.43, bf16[384]{0:T(512)(128)(2,1)} %param.45, bf16[96]{0:T(256)(128)(2,1)} %param.47, bf16[96]{0:T(256)(128)(2,1)} %param.48, bf16[96]{0:T(256)(128)(2,1)} %param.49, ...), dimensions={0} | concatenate | bytes 9984 | tf_op jit(solution)/shard_map/concatenate | solution.py:233
  12.5 5.1 collective-permute-start.12
  40.5 4.2 copy.82
  50.1 2.9 collective-permute-start.32
  55.3 2.9 collective-permute-start.14
  65.7 4.6 collective-permute-start.48
  70.3 5.9 collective-permute-done.1
  77.9 2.8 collective-permute-start.38
  83.2 10.8 %collective-permute-start.26 = (bf16[384,384]{1,0:T(8,128)(2,1)}, bf16[384,384]{1,0:T(8,128)(2,1)S(1)}, u32[]{:S(2)}, u32[]{:S(2)}) collective-permute-start(bf16[384,384]{1,0:T(8,128)(2,1)} %constant_dynamic-slice_fusion.4), channel_id=1, source_target_pairs={{0,2},{1,3},{2,0},{3,1},{4,6},{5,7},{6,4},{7,5},{8,10},{9,11},{10,... | collective-permute-start | bytes 884744 | tf_op jit(solution)/shard_map/ppermute | solution.py:95
  94.0 3.9 collective-permute-done.39
  103.4 15.3 %collective-permute-done.27 = bf16[384,384]{1,0:T(8,128)(2,1)S(1)} collective-permute-done((bf16[384,384]{1,0:T(8,128)(2,1)}, bf16[384,384]{1,0:T(8,128)(2,1)S(1)}, u32[]{:S(2)}, u32[]{:S(2)}) %collective-permute-start.27) | collective-permute-done | bytes 294944 | tf_op jit(solution)/shard_map/ppermute | solution.py:95
  123.0 14.7 %collective-permute-done.21 = bf16[96,1536]{1,0:T(8,128)(2,1)S(1)} collective-permute-done((bf16[96,1536]{1,0:T(8,128)(2,1)}, bf16[96,1536]{1,0:T(8,128)(2,1)S(1)}, u32[]{:S(2)}, u32[]{:S(2)}) %collective-permute-start.21) | collective-permute-done | bytes 294944 | tf_op jit(solution)/shard_map/ppermute | solution.py:95
  166.0 9.3 %collective-permute-done.62 = bf16[96,2304]{1,0:T(8,128)(2,1)} collective-permute-done((bf16[96,2304]{1,0:T(8,128)(2,1)S(1)}, bf16[96,2304]{1,0:T(8,128)(2,1)}, u32[]{:S(2)}, u32[]{:S(2)}) %collective-permute-start.62) | collective-permute-done | bytes 442400 | tf_op jit(solution)/shard_map/ppermute | solution.py:95
  180.0 5.6 collective-permute-done.3.refs_1_
  192.0 3.2 put_together.10
  195.2 3.2 put_together.13
  198.4 3.2 put_together.16
  202.4 3.5 put_together.15
  214.4 4.6 collective-permute-done.43.refs_3_
  220.0 4.7 put_together.9
  224.8 3.7 fusion.20
  238.1 4.8 put_together.14
  243.0 6.8 add_bitcast_fusion.1
  263.8 4.3 add_bitcast_fusion
  282.9 4.4 collective-permute-done.29.refs_1_
  291.4 33.0 %collective-permute-done.63.refs_1_ = bf16[4,96,2304]{2,1,0:T(8,128)(2,1)} collective-permute-done((bf16[4,96,2304]{2,1,0:T(8,128)(2,1)}, bf16[4,96,2304]{2,1,0:T(8,128)(2,1)}, u32[]{:S(2)}, u32[]{:S(2)}) %collective-permute-start.63) | collective-permute-done | bytes 1769504 | tf_op jit(solution)/shard_map/ppermute | solution.py:92
  324.9 5.3 put_together.11
  331.9 5.3 put_together.12
  337.3 11.5 %multiply_convert_fusion.1 = (bf16[256,3072]{1,0:T(8,128)(2,1)S(1)}, f32[256,3072]{1,0:T(8,128)}, f32[256,3072]{1,0:T(8,128)}) fusion(f32[3072]{0:T(1024)S(1)} %copy-done.290, bf16[768,3072]{1,0:T(8,128)(2,1)} %bitcast.455, f32[256,768]{1,0:T(8,128)S(1)} %get-tuple-element.354, f32[768]{0:T(1024)} %add.1564, f32[768]{0:T(1024)S(1)} %mul.1162, ...), kind=kOutput, calls=%fused_computation.55 | convolution fusion | flops 1260847104 | bytes 13389824 | tf_op jit(solution)/shard_map/dot_general | solution.py:19
  348.8 22.4 %collective-permute-done.65.refs_3_ = bf16[4,96,2304]{2,1,0:T(8,128)(2,1)} collective-permute-done((bf16[4,96,2304]{2,1,0:T(8,128)(2,1)}, bf16[4,96,2304]{2,1,0:T(8,128)(2,1)}, u32[]{:S(2)}, u32[]{:S(2)}) %collective-permute-start.65) | collective-permute-done | bytes 1769504 | tf_op jit(solution)/shard_map/ppermute | solution.py:84
  376.2 10.9 %put_together.17 = bf16[16,96,4608]{2,1,0:T(8,128)(2,1)} custom-call(s32[4]{0:T(128)} %pad_add_fusion.64.coords_ref, bf16[4,96,2304]{2,1,0:T(8,128)(2,1)} %pad_maximum_fusion.5.refs_0_, bf16[4,96,2304]{2,1,0:T(8,128)(2,1)} %collective-permute-done.63.refs_1_, bf16[4,96,2304]{2,1,0:T(8,128)(2,1)} %collective-permute-done.64.refs_2_, ...), custom_call_target="tpu_custom_call" | custom-call | tf_op jit(solution)/shard_map/put_together/pallas_call | solution.py:135
  387.1 7.3 fusion.625
  395.1 3.6 multiply_multiply_fusion.10
  406.2 9.4 %fusion.39 = bf16[256,1536]{1,0:T(8,128)(2,1)S(1)} fusion(bf16[1536,4608]{1,0:T(8,128)(2,1)} %bitcast.436, f32[256]{0:T(256)S(1)} %copy-done.293, bf16[255,1536]{1,0:T(8,128)(2,1)} %get-tuple-element.256, bf16[255,1536]{1,0:T(8,128)(2,1)} %get-tuple-element.255, bf16[256,1536]{1,0:T(8,128)(2,1)S(1)} %get-tuple-element.108), kind=kOutput, calls=%fused_computation.92 | convolution fusion | flops 3636461568 | bytes 17296384 | tf_op jit(solution)/shard_map/dot_general | solution.py:29
  415.6 3.0 convolution_add_fusion.18
  424.9 2.7 convert_reduce_fusion.2
  433.4 3.6 convolution_convert_fusion.7
  492.0 8.9 fusion.22
  507.7 6.6 fusion.32
  536.1 6.2 fusion.36
  552.6 8.4 collective-permute-start.81
  561.1 3.1 convolution_convert_fusion.2
  566.0 5.0 convolution_convert_fusion
  571.0 3.4 copy.121
  586.0 3.9 collective-permute-done.120
  591.7 4.5 collective-permute-done.127
  599.1 4.6 add_convert_fusion.6
  608.4 3.3 collective-permute-done.122
  637.1 4.6 collective-permute-done.116
  641.7 3.7 collective-permute-done.115
  657.5 9.4 %add_convert_fusion.3 = bf16[768,1152]{1,0:T(8,128)(2,1)} fusion(bf16[768,1152]{1,0:T(8,128)(2,1)} %collective-permute-done.104, bf16[2048,768]{1,0:T(8,128)(2,1)} %bitcast.480, s32[]{:T(128)S(6)} %select_n.493, bf16[2048,1152]{1,0:T(8,128)(2,1)} %copy-done.89, bf16[2048,1152]{1,0:T(8,128)(2,1)S(1)} %bitcast.454), kind=kOutput, calls=%fused_computation.43 | convolution fusion | flops 3635970048 | bytes 16121860 | tf_op jit(solution)/shard_map/dot_general | solution.py:23
  669.3 2.8 add_convert_fusion.2
  681.2 15.9 %collective-permute-done.105 = bf16[8,48,1152]{2,1,0:T(8,128)(2,1)S(1)} collective-permute-done((bf16[8,48,1152]{2,1,0:T(8,128)(2,1)S(1)}, bf16[8,48,1152]{2,1,0:T(8,128)(2,1)S(1)}, u32[]{:S(2)}, u32[]{:S(2)}) %collective-permute-start.105) | collective-permute-done | bytes 884768 | tf_op jit(solution)/shard_map/ppermute | solution.py:84
  698.1 13.7 %collective-permute-done.72 = bf16[4,48,1152]{2,1,0:T(8,128)(2,1)S(1)} collective-permute-done((bf16[4,48,1152]{2,1,0:T(8,128)(2,1)S(1)}, bf16[4,48,1152]{2,1,0:T(8,128)(2,1)S(1)}, u32[]{:S(2)}, u32[]{:S(2)}) %collective-permute-start.72) | collective-permute-done | bytes 442400 | tf_op jit(solution)/shard_map/ppermute | solution.py:92
  716.0 2.8 collective-permute-done.106
  733.0 2.8 collective-permute-done.108
  738.1 72.6 %collective-permute-done.110 = bf16[48,1152]{1,0:T(8,128)(2,1)S(1)} collective-permute-done((bf16[48,1152]{1,0:T(8,128)(2,1)S(1)}, bf16[48,1152]{1,0:T(8,128)(2,1)S(1)}, u32[]{:S(2)}, u32[]{:S(2)}) %collective-permute-start.110) | collective-permute-done | bytes 110624 | tf_op jit(solution)/shard_map/ppermute | solution.py:84
  816.3 2.8 collective-permute-start.101
  825.3 13.3 %collective-permute-done.99 = bf16[384,384]{1,0:T(8,128)(2,1)S(1)} collective-permute-done((bf16[384,384]{1,0:T(8,128)(2,1)S(1)}, bf16[384,384]{1,0:T(8,128)(2,1)S(1)}, u32[]{:S(2)}, u32[]{:S(2)}) %collective-permute-start.99) | collective-permute-done | bytes 294944 | tf_op jit(solution)/shard_map/ppermute | solution.py:95
  840.7 18.4 %collective-permute-done.100 = bf16[384,384]{1,0:T(8,128)(2,1)S(1)} collective-permute-done((bf16[384,384]{1,0:T(8,128)(2,1)S(1)}, bf16[384,384]{1,0:T(8,128)(2,1)S(1)}, u32[]{:S(2)}, u32[]{:S(2)}) %collective-permute-start.100) | collective-permute-done | bytes 294944 | tf_op jit(solution)/shard_map/ppermute | solution.py:95
  866.8 5.5 collective-permute-done.93
  873.6 14.9 %collective-permute-done.136 = bf16[96,2304]{1,0:T(8,128)(2,1)S(1)} collective-permute-done((bf16[96,2304]{1,0:T(8,128)(2,1)S(1)}, bf16[96,2304]{1,0:T(8,128)(2,1)S(1)}, u32[]{:S(2)}, u32[]{:S(2)}) %collective-permute-start.136) | collective-permute-done | bytes 442400 | tf_op jit(solution)/shard_map/ppermute | solution.py:95
  888.5 20.1 %collective-permute-done.137 = bf16[96,2304]{1,0:T(8,128)(2,1)S(1)} collective-permute-done((bf16[96,2304]{1,0:T(8,128)(2,1)S(1)}, bf16[96,2304]{1,0:T(8,128)(2,1)S(1)}, u32[]{:S(2)}, u32[]{:S(2)}) %collective-permute-start.137) | collective-permute-done | bytes 442400 | tf_op jit(solution)/shard_map/ppermute | solution.py:95
  910.2 9.9 %collective-permute-done.139 = bf16[96,2304]{1,0:T(8,128)(2,1)S(1)} collective-permute-done((bf16[96,2304]{1,0:T(8,128)(2,1)S(1)}, bf16[96,2304]{1,0:T(8,128)(2,1)S(1)}, u32[]{:S(2)}, u32[]{:S(2)}) %collective-permute-start.139) | collective-permute-done | bytes 442400 | tf_op jit(solution)/shard_map/ppermute | solution.py:84
  (1290 shorter events, 386.2 us)
Async XLA Ops:
  12.5 32.3 %collective-permute-start.12 = (bf16[1,2496]{1,0:T(2,128)(2,1)S(1)}, bf16[1,2496]{1,0:T(2,128)(2,1)S(1)}, u32[]{:S(2)}, u32[]{:S(2)}) collective-permute-start(bf16[1,2496]{1,0:T(2,128)(2,1)S(1)} %broadcast_in_dim.297), channel_id=1, source_target_pairs={{0,6},{1,7},{2,4},{3,5},{4,2},{5,3},{6,0},{7,1},{8,14},{9,15},{10,... | collective-permute-start | bytes 14984 | tf_op jit(solution)/shard_map/ppermute | solution.py:95
  17.6 27.2 %collective-permute-start.11 = (bf16[1,2496]{1,0:T(2,128)(2,1)S(1)}, bf16[1,2496]{1,0:T(2,128)(2,1)S(1)}, u32[]{:S(2)}, u32[]{:S(2)}) collective-permute-start(bf16[1,2496]{1,0:T(2,128)(2,1)S(1)} %broadcast_in_dim.297), channel_id=1, source_target_pairs={{0,4},{1,5},{2,6},{3,7},{4,0},{5,1},{6,2},{7,3},{8,12},{9,13},{10,... | collective-permute-start | bytes 14984 | tf_op jit(solution)/shard_map/ppermute | solution.py:95
  17.6 28.6 %collective-permute-start.10 = (bf16[1,2496]{1,0:T(2,128)(2,1)S(1)}, bf16[1,2496]{1,0:T(2,128)(2,1)S(1)}, u32[]{:S(2)}, u32[]{:S(2)}) collective-permute-start(bf16[1,2496]{1,0:T(2,128)(2,1)S(1)} %broadcast_in_dim.297), channel_id=1, source_target_pairs={{0,2},{1,3},{2,0},{3,1},{4,6},{5,7},{6,4},{7,5},{8,10},{9,11},{10,... | collective-permute-start | bytes 14984 | tf_op jit(solution)/shard_map/ppermute | solution.py:95
  19.1 34.6 %collective-permute-start.55 = (bf16[96,384]{1,0:T(8,128)(2,1)S(1)}, bf16[96,384]{1,0:T(8,128)(2,1)S(1)}, u32[]{:S(2)}, u32[]{:S(2)}) collective-permute-start(bf16[96,384]{1,0:T(8,128)(2,1)S(1)} %constant_dynamic-slice_fusion.1), channel_id=1, source_target_pairs={{0,4},{1,5},{2,6},{3,7},{4,0},{5,1},{6,2},{7,3},{8,12},{9,13},{10,... | collective-permute-start | bytes 221192 | tf_op jit(solution)/shard_map/ppermute | solution.py:95
  21.4 32.5 %collective-permute-start.54 = (bf16[96,384]{1,0:T(8,128)(2,1)S(1)}, bf16[96,384]{1,0:T(8,128)(2,1)S(1)}, u32[]{:S(2)}, u32[]{:S(2)}) collective-permute-start(bf16[96,384]{1,0:T(8,128)(2,1)S(1)} %constant_dynamic-slice_fusion.1), channel_id=1, source_target_pairs={{0,2},{1,3},{2,0},{3,1},{4,6},{5,7},{6,4},{7,5},{8,10},{9,11},{10,... | collective-permute-start | bytes 221192 | tf_op jit(solution)/shard_map/ppermute | solution.py:95
  77.8 20.0 %collective-permute-start.39 = (bf16[48,1152]{1,0:T(8,128)(2,1)S(1)}, bf16[48,1152]{1,0:T(8,128)(2,1)S(1)}, u32[]{:S(2)}, u32[]{:S(2)}) collective-permute-start(bf16[48,1152]{1,0:T(8,128)(2,1)S(1)} %fusion.423), channel_id=1, source_target_pairs={{0,4},{1,5},{2,6},{3,7},{4,0},{5,1},{6,2},{7,3},{8,12},{9,13},{10,... | collective-permute-start | bytes 331784 | tf_op jit(solution)/shard_map/ppermute | solution.py:95
  77.9 22.2 %collective-permute-start.38 = (bf16[48,1152]{1,0:T(8,128)(2,1)S(1)}, bf16[48,1152]{1,0:T(8,128)(2,1)S(1)}, u32[]{:S(2)}, u32[]{:S(2)}) collective-permute-start(bf16[48,1152]{1,0:T(8,128)(2,1)S(1)} %fusion.423), channel_id=1, source_target_pairs={{0,2},{1,3},{2,0},{3,1},{4,6},{5,7},{6,4},{7,5},{8,10},{9,11},{10,... | collective-permute-start | bytes 331784 | tf_op jit(solution)/shard_map/ppermute | solution.py:95
  83.0 35.7 %collective-permute-start.27 = (bf16[384,384]{1,0:T(8,128)(2,1)}, bf16[384,384]{1,0:T(8,128)(2,1)S(1)}, u32[]{:S(2)}, u32[]{:S(2)}) collective-permute-start(bf16[384,384]{1,0:T(8,128)(2,1)} %constant_dynamic-slice_fusion.4), channel_id=1, source_target_pairs={{0,4},{1,5},{2,6},{3,7},{4,0},{5,1},{6,2},{7,3},{8,12},{9,13},{10,... | collective-permute-start | bytes 884744 | tf_op jit(solution)/shard_map/ppermute | solution.py:95
  83.2 38.1 %collective-permute-start.26 = (bf16[384,384]{1,0:T(8,128)(2,1)}, bf16[384,384]{1,0:T(8,128)(2,1)S(1)}, u32[]{:S(2)}, u32[]{:S(2)}) collective-permute-start(bf16[384,384]{1,0:T(8,128)(2,1)} %constant_dynamic-slice_fusion.4), channel_id=1, source_target_pairs={{0,2},{1,3},{2,0},{3,1},{4,6},{5,7},{6,4},{7,5},{8,10},{9,11},{10,... | collective-permute-start | bytes 884744 | tf_op jit(solution)/shard_map/ppermute | solution.py:95
  97.9 23.6 %collective-permute-start.28 = (bf16[384,384]{1,0:T(8,128)(2,1)}, bf16[384,384]{1,0:T(8,128)(2,1)S(1)}, u32[]{:S(2)}, u32[]{:S(2)}) collective-permute-start(bf16[384,384]{1,0:T(8,128)(2,1)} %constant_dynamic-slice_fusion.4), channel_id=1, source_target_pairs={{0,6},{1,7},{2,4},{3,5},{4,2},{5,3},{6,0},{7,1},{8,14},{9,15},{10,... | collective-permute-start | bytes 884744 | tf_op jit(solution)/shard_map/ppermute | solution.py:95
  100.0 37.6 %collective-permute-start.21 = (bf16[96,1536]{1,0:T(8,128)(2,1)}, bf16[96,1536]{1,0:T(8,128)(2,1)S(1)}, u32[]{:S(2)}, u32[]{:S(2)}) collective-permute-start(bf16[96,1536]{1,0:T(8,128)(2,1)} %constant_dynamic-slice_fusion.5), channel_id=1, source_target_pairs={{0,4},{1,5},{2,6},{3,7},{4,0},{5,1},{6,2},{7,3},{8,12},{9,13},{10,... | collective-permute-start | bytes 884744 | tf_op jit(solution)/shard_map/ppermute | solution.py:95
  100.7 37.0 %collective-permute-start.20 = (bf16[96,1536]{1,0:T(8,128)(2,1)}, bf16[96,1536]{1,0:T(8,128)(2,1)S(1)}, u32[]{:S(2)}, u32[]{:S(2)}) collective-permute-start(bf16[96,1536]{1,0:T(8,128)(2,1)} %constant_dynamic-slice_fusion.5), channel_id=1, source_target_pairs={{0,2},{1,3},{2,0},{3,1},{4,6},{5,7},{6,4},{7,5},{8,10},{9,11},{10,... | collective-permute-start | bytes 884744 | tf_op jit(solution)/shard_map/ppermute | solution.py:95
  118.7 21.8 %collective-permute-start.22 = (bf16[96,1536]{1,0:T(8,128)(2,1)}, bf16[96,1536]{1,0:T(8,128)(2,1)S(1)}, u32[]{:S(2)}, u32[]{:S(2)}) collective-permute-start(bf16[96,1536]{1,0:T(8,128)(2,1)} %constant_dynamic-slice_fusion.5), channel_id=1, source_target_pairs={{0,6},{1,7},{2,4},{3,5},{4,2},{5,3},{6,0},{7,1},{8,14},{9,15},{10,... | collective-permute-start | bytes 884744 | tf_op jit(solution)/shard_map/ppermute | solution.py:95
  121.4 20.0 %collective-permute-start.18 = (bf16[4,96,384]{2,1,0:T(8,128)(2,1)S(1)}, bf16[4,96,384]{2,1,0:T(8,128)(2,1)S(1)}, u32[]{:S(2)}, u32[]{:S(2)}) collective-permute-start(bf16[4,96,384]{2,1,0:T(8,128)(2,1)S(1)} %pad_maximum_fusion.17.refs_0_), channel_id=1, source_target_pairs={{0,8},{8,0},{16,24},{24,16},{1,9},{9,1},{17,25},{25,17},{2,10},{10... | collective-permute-start | bytes 884744 | tf_op jit(solution)/shard_map/ppermute | solution.py:81
  121.5 22.5 %collective-permute-start.17 = (bf16[4,96,384]{2,1,0:T(8,128)(2,1)S(1)}, bf16[4,96,384]{2,1,0:T(8,128)(2,1)S(1)}, u32[]{:S(2)}, u32[]{:S(2)}) collective-permute-start(bf16[4,96,384]{2,1,0:T(8,128)(2,1)S(1)} %pad_maximum_fusion.17.refs_0_), channel_id=1, source_target_pairs={{0,1},{1,0},{2,3},{3,2},{4,5},{5,4},{6,7},{7,6},{8,9},{9,8},{10,11... | collective-permute-start | bytes 884744 | tf_op jit(solution)/shard_map/ppermute | solution.py:92
  141.4 23.8 %collective-permute-start.61 = (bf16[96,2304]{1,0:T(8,128)(2,1)S(1)}, bf16[96,2304]{1,0:T(8,128)(2,1)S(1)}, u32[]{:S(2)}, u32[]{:S(2)}) collective-permute-start(bf16[96,2304]{1,0:T(8,128)(2,1)S(1)} %fusion.159), channel_id=1, source_target_pairs={{0,4},{1,5},{2,6},{3,7},{4,0},{5,1},{6,2},{7,3},{8,12},{9,13},{10,... | collective-permute-start | bytes 1327112 | tf_op jit(solution)/shard_map/ppermute | solution.py:95
  144.0 22.0 %collective-permute-start.60 = (bf16[96,2304]{1,0:T(8,128)(2,1)S(1)}, bf16[96,2304]{1,0:T(8,128)(2,1)}, u32[]{:S(2)}, u32[]{:S(2)}) collective-permute-start(bf16[96,2304]{1,0:T(8,128)(2,1)S(1)} %fusion.159), channel_id=1, source_target_pairs={{0,2},{1,3},{2,0},{3,1},{4,6},{5,7},{6,4},{7,5},{8,10},{9,11},{10,... | collective-permute-start | bytes 1327112 | tf_op jit(solution)/shard_map/ppermute | solution.py:95
  144.0 31.3 %collective-permute-start.62 = (bf16[96,2304]{1,0:T(8,128)(2,1)S(1)}, bf16[96,2304]{1,0:T(8,128)(2,1)}, u32[]{:S(2)}, u32[]{:S(2)}) collective-permute-start(bf16[96,2304]{1,0:T(8,128)(2,1)S(1)} %fusion.159), channel_id=1, source_target_pairs={{0,6},{1,7},{2,4},{3,5},{4,2},{5,3},{6,0},{7,1},{8,14},{9,15},{10,... | collective-permute-start | bytes 1327112 | tf_op jit(solution)/shard_map/ppermute | solution.py:95
  147.1 28.2 %collective-permute-start.52 = (bf16[4,48,1152]{2,1,0:T(8,128)(2,1)S(1)}, bf16[4,48,1152]{2,1,0:T(8,128)(2,1)}, u32[]{:S(2)}, u32[]{:S(2)}) collective-permute-start(bf16[4,48,1152]{2,1,0:T(8,128)(2,1)S(1)} %pad_maximum_fusion.15.refs_0_), channel_id=1, source_target_pairs={{0,8},{8,0},{16,24},{24,16},{1,9},{9,1},{17,25},{25,17},{2,10},{10... | collective-permute-start | bytes 1327112 | tf_op jit(solution)/shard_map/ppermute | solution.py:81
  165.2 20.4 %collective-permute-start.3 = (bf16[4,48,1152]{2,1,0:T(8,128)(2,1)S(1)}, bf16[4,48,1152]{2,1,0:T(8,128)(2,1)}, u32[]{:S(2)}, u32[]{:S(2)}) collective-permute-start(bf16[4,48,1152]{2,1,0:T(8,128)(2,1)S(1)} %pad_maximum_fusion.13.refs_0_), channel_id=1, source_target_pairs={{0,1},{1,0},{2,3},{3,2},{4,5},{5,4},{6,7},{7,6},{8,9},{9,8},{10,11... | collective-permute-start | bytes 1327112 | tf_op jit(solution)/shard_map/ppermute | solution.py:92
  166.0 20.0 %collective-permute-start.19 = (bf16[4,96,384]{2,1,0:T(8,128)(2,1)}, bf16[4,96,384]{2,1,0:T(8,128)(2,1)S(1)}, u32[]{:S(2)}, u32[]{:S(2)}) collective-permute-start(bf16[4,96,384]{2,1,0:T(8,128)(2,1)} %copy-done.228), channel_id=1, source_target_pairs={{0,8},{8,0},{16,24},{24,16},{1,9},{9,1},{17,25},{25,17},{2,10},{10... | collective-permute-start | bytes 884744 | tf_op jit(solution)/shard_map/ppermute | solution.py:81
  178.3 27.6 %collective-permute-start.42 = (bf16[4,48,1152]{2,1,0:T(8,128)(2,1)S(1)}, bf16[4,48,1152]{2,1,0:T(8,128)(2,1)}, u32[]{:S(2)}, u32[]{:S(2)}) collective-permute-start(bf16[4,48,1152]{2,1,0:T(8,128)(2,1)S(1)} %pad_maximum_fusion.14.refs_0_), channel_id=1, source_target_pairs={{0,16},{8,24},{16,0},{24,8},{1,17},{9,25},{17,1},{25,9},{2,18},{10... | collective-permute-start | bytes 1327112 | tf_op jit(solution)/shard_map/ppermute | solution.py:84
  185.6 20.5 %collective-permute-start.41 = (bf16[4,48,1152]{2,1,0:T(8,128)(2,1)S(1)}, bf16[4,48,1152]{2,1,0:T(8,128)(2,1)}, u32[]{:S(2)}, u32[]{:S(2)}) collective-permute-start(bf16[4,48,1152]{2,1,0:T(8,128)(2,1)S(1)} %pad_maximum_fusion.14.refs_0_), channel_id=1, source_target_pairs={{0,1},{1,0},{2,3},{3,2},{4,5},{5,4},{6,7},{7,6},{8,9},{9,8},{10,11... | collective-permute-start | bytes 1327112 | tf_op jit(solution)/shard_map/ppermute | solution.py:92
  186.0 21.8 %collective-permute-start.4 = (bf16[4,48,1152]{2,1,0:T(8,128)(2,1)S(1)}, bf16[4,48,1152]{2,1,0:T(8,128)(2,1)}, u32[]{:S(2)}, u32[]{:S(2)}) collective-permute-start(bf16[4,48,1152]{2,1,0:T(8,128)(2,1)S(1)} %pad_maximum_fusion.13.refs_0_), channel_id=1, source_target_pairs={{0,16},{8,24},{16,0},{24,8},{1,17},{9,25},{17,1},{25,9},{2,18},{10... | collective-permute-start | bytes 1327112 | tf_op jit(solution)/shard_map/ppermute | solution.py:84
  187.7 21.9 %collective-permute-start.5 = (bf16[4,48,1152]{2,1,0:T(8,128)(2,1)}, bf16[4,48,1152]{2,1,0:T(8,128)(2,1)}, u32[]{:S(2)}, u32[]{:S(2)}) collective-permute-start(bf16[4,48,1152]{2,1,0:T(8,128)(2,1)} %collective-permute-done.3.refs_1_), channel_id=1, source_target_pairs={{0,16},{8,24},{16,0},{24,8},{1,17},{9,25},{17,1},{25,9},{2,18},{10... | collective-permute-start | bytes 1327112 | tf_op jit(solution)/shard_map/ppermute | solution.py:84
  219.0 63.4 %collective-permute-start.24 = (bf16[4,96,1536]{2,1,0:T(8,128)(2,1)}, bf16[4,96,1536]{2,1,0:T(8,128)(2,1)}, u32[]{:S(2)}, u32[]{:S(2)}) collective-permute-start(bf16[4,96,1536]{2,1,0:T(8,128)(2,1)} %pad_maximum_fusion.7.refs_0_), channel_id=1, source_target_pairs={{0,8},{8,0},{16,24},{24,16},{1,9},{9,1},{17,25},{25,17},{2,10},{10... | collective-permute-start | bytes 3538952 | tf_op jit(solution)/shard_map/ppermute | solution.py:81
  232.9 49.6 %collective-permute-start.23 = (bf16[4,96,1536]{2,1,0:T(8,128)(2,1)}, bf16[4,96,1536]{2,1,0:T(8,128)(2,1)}, u32[]{:S(2)}, u32[]{:S(2)}) collective-permute-start(bf16[4,96,1536]{2,1,0:T(8,128)(2,1)} %pad_maximum_fusion.7.refs_0_), channel_id=1, source_target_pairs={{0,1},{1,0},{2,3},{3,2},{4,5},{5,4},{6,7},{7,6},{8,9},{9,8},{10,11... | collective-permute-start | bytes 3538952 | tf_op jit(solution)/shard_map/ppermute | solution.py:92
  234.6 52.8 %collective-permute-start.29 = (bf16[4,384,384]{2,1,0:T(8,128)(2,1)}, bf16[4,384,384]{2,1,0:T(8,128)(2,1)}, u32[]{:S(2)}, u32[]{:S(2)}) collective-permute-start(bf16[4,384,384]{2,1,0:T(8,128)(2,1)} %pad_maximum_fusion.8.refs_0_), channel_id=1, source_target_pairs={{0,1},{1,0},{2,3},{3,2},{4,5},{5,4},{6,7},{7,6},{8,9},{9,8},{10,11... | collective-permute-start | bytes 3538952 | tf_op jit(solution)/shard_map/ppermute | solution.py:92
  235.0 96.9 %collective-permute-start.64 = (bf16[4,96,2304]{2,1,0:T(8,128)(2,1)}, bf16[4,96,2304]{2,1,0:T(8,128)(2,1)}, u32[]{:S(2)}, u32[]{:S(2)}) collective-permute-start(bf16[4,96,2304]{2,1,0:T(8,128)(2,1)} %pad_maximum_fusion.5.refs_0_), channel_id=1, source_target_pairs={{0,16},{8,24},{16,0},{24,8},{1,17},{9,25},{17,1},{25,9},{2,18},{10... | collective-permute-start | bytes 5308424 | tf_op jit(solution)/shard_map/ppermute | solution.py:84
  236.6 87.8 %collective-permute-start.63 = (bf16[4,96,2304]{2,1,0:T(8,128)(2,1)}, bf16[4,96,2304]{2,1,0:T(8,128)(2,1)}, u32[]{:S(2)}, u32[]{:S(2)}) collective-permute-start(bf16[4,96,2304]{2,1,0:T(8,128)(2,1)} %pad_maximum_fusion.5.refs_0_), channel_id=1, source_target_pairs={{0,1},{1,0},{2,3},{3,2},{4,5},{5,4},{6,7},{7,6},{8,9},{9,8},{10,11... | collective-permute-start | bytes 5308424 | tf_op jit(solution)/shard_map/ppermute | solution.py:92
  282.4 47.8 %collective-permute-start.30 = (bf16[4,384,384]{2,1,0:T(8,128)(2,1)}, bf16[4,384,384]{2,1,0:T(8,128)(2,1)}, u32[]{:S(2)}, u32[]{:S(2)}) collective-permute-start(bf16[4,384,384]{2,1,0:T(8,128)(2,1)} %pad_maximum_fusion.8.refs_0_), channel_id=1, source_target_pairs={{0,8},{8,0},{16,24},{24,16},{1,9},{9,1},{17,25},{25,17},{2,10},{10... | collective-permute-start | bytes 3538952 | tf_op jit(solution)/shard_map/ppermute | solution.py:81
  282.4 42.0 %collective-permute-start.25 = (bf16[4,96,1536]{2,1,0:T(8,128)(2,1)}, bf16[4,96,1536]{2,1,0:T(8,128)(2,1)}, u32[]{:S(2)}, u32[]{:S(2)}) collective-permute-start(bf16[4,96,1536]{2,1,0:T(8,128)(2,1)} %collective-permute-done.23.refs_1_), channel_id=1, source_target_pairs={{0,8},{8,0},{16,24},{24,16},{1,9},{9,1},{17,25},{25,17},{2,10},{10... | collective-permute-start | bytes 3538952 | tf_op jit(solution)/shard_map/ppermute | solution.py:81
  287.4 44.5 %collective-permute-start.31 = (bf16[4,384,384]{2,1,0:T(8,128)(2,1)}, bf16[4,384,384]{2,1,0:T(8,128)(2,1)}, u32[]{:S(2)}, u32[]{:S(2)}) collective-permute-start(bf16[4,384,384]{2,1,0:T(8,128)(2,1)} %collective-permute-done.29.refs_1_), channel_id=1, source_target_pairs={{0,8},{8,0},{16,24},{24,16},{1,9},{9,1},{17,25},{25,17},{2,10},{10... | collective-permute-start | bytes 3538952 | tf_op jit(solution)/shard_map/ppermute | solution.py:81
  324.4 51.8 %collective-permute-start.66 = (bf16[4,96,2304]{2,1,0:T(8,128)(2,1)}, bf16[4,96,2304]{2,1,0:T(8,128)(2,1)}, u32[]{:S(2)}, u32[]{:S(2)}) collective-permute-start(bf16[4,96,2304]{2,1,0:T(8,128)(2,1)} %pad_maximum_fusion.5.refs_0_), channel_id=1, source_target_pairs={{0,8},{8,0},{16,24},{24,16},{1,9},{9,1},{17,25},{25,17},{2,10},{10... | collective-permute-start | bytes 5308424 | tf_op jit(solution)/shard_map/ppermute | solution.py:81
  324.4 51.8 %collective-permute-start.67 = (bf16[4,96,2304]{2,1,0:T(8,128)(2,1)}, bf16[4,96,2304]{2,1,0:T(8,128)(2,1)}, u32[]{:S(2)}, u32[]{:S(2)}) collective-permute-start(bf16[4,96,2304]{2,1,0:T(8,128)(2,1)} %collective-permute-done.63.refs_1_), channel_id=1, source_target_pairs={{0,8},{8,0},{16,24},{24,16},{1,9},{9,1},{17,25},{25,17},{2,10},{10... | collective-permute-start | bytes 5308424 | tf_op jit(solution)/shard_map/ppermute | solution.py:81
  330.2 41.0 %collective-permute-start.65 = (bf16[4,96,2304]{2,1,0:T(8,128)(2,1)}, bf16[4,96,2304]{2,1,0:T(8,128)(2,1)}, u32[]{:S(2)}, u32[]{:S(2)}) collective-permute-start(bf16[4,96,2304]{2,1,0:T(8,128)(2,1)} %collective-permute-done.63.refs_1_), channel_id=1, source_target_pairs={{0,16},{8,24},{16,0},{24,8},{1,17},{9,25},{17,1},{25,9},{2,18},{10... | collective-permute-start | bytes 5308424 | tf_op jit(solution)/shard_map/ppermute | solution.py:84
  331.9 44.3 %collective-permute-start.68 = (bf16[4,96,2304]{2,1,0:T(8,128)(2,1)}, bf16[4,96,2304]{2,1,0:T(8,128)(2,1)}, u32[]{:S(2)}, u32[]{:S(2)}) collective-permute-start(bf16[4,96,2304]{2,1,0:T(8,128)(2,1)} %collective-permute-done.64.refs_2_), channel_id=1, source_target_pairs={{0,8},{8,0},{16,24},{24,16},{1,9},{9,1},{17,25},{25,17},{2,10},{10... | collective-permute-start | bytes 5308424 | tf_op jit(solution)/shard_map/ppermute | solution.py:81
  546.5 31.2 %collective-permute-start.119 = (bf16[768,384]{1,0:T(8,128)(2,1)}, bf16[768,384]{1,0:T(8,128)(2,1)}, u32[]{:S(2)}, u32[]{:S(2)}) collective-permute-start(bf16[768,384]{1,0:T(8,128)(2,1)} %convolution_convert_fusion.5), channel_id=1, source_target_pairs={{0,8},{8,0},{16,24},{24,16},{1,9},{9,1},{17,25},{25,17},{2,10},{10... | collective-permute-start | bytes 1769480 | tf_op jit(solution)/shard_map/ppermute | solution.py:81
  551.1 28.8 %collective-permute-start.126 = (bf16[768,384]{1,0:T(8,128)(2,1)}, bf16[768,384]{1,0:T(8,128)(2,1)}, u32[]{:S(2)}, u32[]{:S(2)}) collective-permute-start(bf16[768,384]{1,0:T(8,128)(2,1)} %convolution_convert_fusion.4), channel_id=1, source_target_pairs={{0,8},{8,0},{16,24},{24,16},{1,9},{9,1},{17,25},{25,17},{2,10},{10... | collective-permute-start | bytes 1769480 | tf_op jit(solution)/shard_map/ppermute | solution.py:81
  551.1 32.8 %collective-permute-start.83 = (bf16[768,384]{1,0:T(8,128)(2,1)}, bf16[768,384]{1,0:T(8,128)(2,1)}, u32[]{:S(2)}, u32[]{:S(2)}) collective-permute-start(bf16[768,384]{1,0:T(8,128)(2,1)} %convolution_convert_fusion.6), channel_id=1, source_target_pairs={{0,8},{8,0},{16,24},{24,16},{1,9},{9,1},{17,25},{25,17},{2,10},{10... | collective-permute-start | bytes 1769480 | tf_op jit(solution)/shard_map/ppermute | solution.py:81
  564.1 105.2 %collective-permute-start.90 = (bf16[768,1536]{1,0:T(8,128)(2,1)}, bf16[768,1536]{1,0:T(8,128)(2,1)}, u32[]{:S(2)}, u32[]{:S(2)}) collective-permute-start(bf16[768,1536]{1,0:T(8,128)(2,1)} %convolution_convert_fusion.2), channel_id=1, source_target_pairs={{0,8},{8,0},{16,24},{24,16},{1,9},{9,1},{17,25},{25,17},{2,10},{10... | collective-permute-start | bytes 7077896 | tf_op jit(solution)/shard_map/ppermute | solution.py:81
  574.4 99.6 %collective-permute-start.97 = (bf16[3072,384]{1,0:T(8,128)(2,1)}, bf16[3072,384]{1,0:T(8,128)(2,1)}, u32[]{:S(2)}, u32[]{:S(2)}) collective-permute-start(bf16[3072,384]{1,0:T(8,128)(2,1)} %convolution_convert_fusion.1), channel_id=1, source_target_pairs={{0,8},{8,0},{16,24},{24,16},{1,9},{9,1},{17,25},{25,17},{2,10},{10... | collective-permute-start | bytes 7077896 | tf_op jit(solution)/shard_map/ppermute | solution.py:81
  641.7 84.5 %collective-permute-start.133 = (bf16[1536,2304]{1,0:T(8,128)(2,1)S(1)}, bf16[1536,2304]{1,0:T(8,128)(2,1)S(1)}, u32[]{:S(2)}, u32[]{:S(2)}) collective-permute-start(bf16[1536,2304]{1,0:T(8,128)(2,1)S(1)} %bitcast.446), channel_id=1, source_target_pairs={{0,8},{8,0},{16,24},{24,16},{1,9},{9,1},{17,25},{25,17},{2,10},{10... | collective-permute-start | bytes 21233672 | tf_op jit(solution)/shard_map/ppermute | solution.py:81
  656.0 22.8 %collective-permute-start.71 = (bf16[8,48,1152]{2,1,0:T(8,128)(2,1)}, bf16[8,48,1152]{2,1,0:T(8,128)(2,1)}, u32[]{:S(2)}, u32[]{:S(2)}) collective-permute-start(bf16[8,48,1152]{2,1,0:T(8,128)(2,1)} %dynamic-slice_bitcast_fusion.5), channel_id=1, source_target_pairs={{0,16},{8,24},{16,0},{24,8},{1,17},{9,25},{17,1},{25,9},{2,18},{10... | collective-permute-start | bytes 2654216 | tf_op jit(solution)/shard_map/ppermute | solution.py:84
  668.3 28.8 %collective-permute-start.105 = (bf16[8,48,1152]{2,1,0:T(8,128)(2,1)S(1)}, bf16[8,48,1152]{2,1,0:T(8,128)(2,1)S(1)}, u32[]{:S(2)}, u32[]{:S(2)}) collective-permute-start(bf16[8,48,1152]{2,1,0:T(8,128)(2,1)S(1)} %dynamic-slice_bitcast_fusion.4), channel_id=1, source_target_pairs={{0,16},{8,24},{16,0},{24,8},{1,17},{9,25},{17,1},{25,9},{2,18},{10... | collective-permute-start | bytes 2654216 | tf_op jit(solution)/shard_map/ppermute | solution.py:84
  673.3 137.5 %collective-permute-start.91 = (bf16[4,96,1536]{2,1,0:T(8,128)(2,1)}, bf16[4,96,1536]{2,1,0:T(8,128)(2,1)}, u32[]{:S(2)}, u32[]{:S(2)}) collective-permute-start(bf16[4,96,1536]{2,1,0:T(8,128)(2,1)} %dynamic-slice_bitcast_fusion.3), channel_id=1, source_target_pairs={{0,1},{1,0},{2,3},{3,2},{4,5},{5,4},{6,7},{7,6},{8,9},{9,8},{10,11... | collective-permute-start | bytes 3538952 | tf_op jit(solution)/shard_map/ppermute | solution.py:92
  680.3 31.6 %collective-permute-start.72 = (bf16[4,48,1152]{2,1,0:T(8,128)(2,1)S(1)}, bf16[4,48,1152]{2,1,0:T(8,128)(2,1)S(1)}, u32[]{:S(2)}, u32[]{:S(2)}) collective-permute-start(bf16[4,48,1152]{2,1,0:T(8,128)(2,1)S(1)} %dynamic-slice_bitcast_fusion.11), channel_id=1, source_target_pairs={{0,1},{1,0},{2,3},{3,2},{4,5},{5,4},{6,7},{7,6},{8,9},{9,8},{10,11... | collective-permute-start | bytes 1327112 | tf_op jit(solution)/shard_map/ppermute | solution.py:92
  697.4 21.5 %collective-permute-start.106 = (bf16[4,48,1152]{2,1,0:T(8,128)(2,1)S(1)}, bf16[4,48,1152]{2,1,0:T(8,128)(2,1)S(1)}, u32[]{:S(2)}, u32[]{:S(2)}) collective-permute-start(bf16[4,48,1152]{2,1,0:T(8,128)(2,1)S(1)} %dynamic-slice_bitcast_fusion.10), channel_id=1, source_target_pairs={{0,1},{1,0},{2,3},{3,2},{4,5},{5,4},{6,7},{7,6},{8,9},{9,8},{10,11... | collective-permute-start | bytes 1327112 | tf_op jit(solution)/shard_map/ppermute | solution.py:92
  722.3 92.1 %collective-permute-start.98 = (bf16[4,384,384]{2,1,0:T(8,128)(2,1)}, bf16[4,384,384]{2,1,0:T(8,128)(2,1)}, u32[]{:S(2)}, u32[]{:S(2)}) collective-permute-start(bf16[4,384,384]{2,1,0:T(8,128)(2,1)} %dynamic-slice_bitcast_fusion.2), channel_id=1, source_target_pairs={{0,1},{1,0},{2,3},{3,2},{4,5},{5,4},{6,7},{7,6},{8,9},{9,8},{10,11... | collective-permute-start | bytes 3538952 | tf_op jit(solution)/shard_map/ppermute | solution.py:92
  732.1 87.1 %collective-permute-start.134 = (bf16[8,96,2304]{2,1,0:T(8,128)(2,1)S(1)}, bf16[8,96,2304]{2,1,0:T(8,128)(2,1)S(1)}, u32[]{:S(2)}, u32[]{:S(2)}) collective-permute-start(bf16[8,96,2304]{2,1,0:T(8,128)(2,1)S(1)} %dynamic-slice_bitcast_fusion), channel_id=1, source_target_pairs={{0,16},{8,24},{16,0},{24,8},{1,17},{9,25},{17,1},{25,9},{2,18},{10... | collective-permute-start | bytes 10616840 | tf_op jit(solution)/shard_map/ppermute | solution.py:84
  736.8 73.9 %collective-permute-start.110 = (bf16[48,1152]{1,0:T(8,128)(2,1)S(1)}, bf16[48,1152]{1,0:T(8,128)(2,1)S(1)}, u32[]{:S(2)}, u32[]{:S(2)}) collective-permute-start(bf16[48,1152]{1,0:T(8,128)(2,1)S(1)} %fusion.389), channel_id=1, source_target_pairs={{0,16},{8,24},{16,0},{24,8},{1,17},{9,25},{17,1},{25,9},{2,18},{10... | collective-permute-start | bytes 331784 | tf_op jit(solution)/shard_map/ppermute | solution.py:84
  738.0 78.3 %collective-permute-start.77 = (bf16[96,1152]{1,0:T(8,128)(2,1)S(1)}, bf16[96,1152]{1,0:T(8,128)(2,1)S(1)}, u32[]{:S(2)}, u32[]{:S(2)}) collective-permute-start(bf16[96,1152]{1,0:T(8,128)(2,1)S(1)} %pad_maximum_fusion.20), channel_id=1, source_target_pairs={{0,8},{8,0},{16,24},{24,16},{1,9},{9,1},{17,25},{25,17},{2,10},{10... | collective-permute-start | bytes 663560 | tf_op jit(solution)/shard_map/ppermute | solution.py:81
  812.5 50.7 %collective-permute-start.92 = (bf16[96,1536]{1,0:T(8,128)(2,1)S(1)}, bf16[96,1536]{1,0:T(8,128)(2,1)S(1)}, u32[]{:S(2)}, u32[]{:S(2)}) collective-permute-start(bf16[96,1536]{1,0:T(8,128)(2,1)S(1)} %get-tuple-element.234), channel_id=1, source_target_pairs={{0,2},{1,3},{2,0},{3,1},{4,6},{5,7},{6,4},{7,5},{8,10},{9,11},{10,... | collective-permute-start | bytes 884744 | tf_op jit(solution)/shard_map/ppermute | solution.py:95
  816.0 22.6 %collective-permute-start.99 = (bf16[384,384]{1,0:T(8,128)(2,1)S(1)}, bf16[384,384]{1,0:T(8,128)(2,1)S(1)}, u32[]{:S(2)}, u32[]{:S(2)}) collective-permute-start(bf16[384,384]{1,0:T(8,128)(2,1)S(1)} %get-tuple-element.231), channel_id=1, source_target_pairs={{0,2},{1,3},{2,0},{3,1},{4,6},{5,7},{6,4},{7,5},{8,10},{9,11},{10,... | collective-permute-start | bytes 884744 | tf_op jit(solution)/shard_map/ppermute | solution.py:95
  816.3 24.3 %collective-permute-start.101 = (bf16[384,384]{1,0:T(8,128)(2,1)S(1)}, bf16[384,384]{1,0:T(8,128)(2,1)S(1)}, u32[]{:S(2)}, u32[]{:S(2)}) collective-permute-start(bf16[384,384]{1,0:T(8,128)(2,1)S(1)} %get-tuple-element.232), channel_id=1, source_target_pairs={{0,6},{1,7},{2,4},{3,5},{4,2},{5,3},{6,0},{7,1},{8,14},{9,15},{10,... | collective-permute-start | bytes 884744 | tf_op jit(solution)/shard_map/ppermute | solution.py:95
  819.2 39.9 %collective-permute-start.100 = (bf16[384,384]{1,0:T(8,128)(2,1)S(1)}, bf16[384,384]{1,0:T(8,128)(2,1)S(1)}, u32[]{:S(2)}, u32[]{:S(2)}) collective-permute-start(bf16[384,384]{1,0:T(8,128)(2,1)S(1)} %get-tuple-element.233), channel_id=1, source_target_pairs={{0,4},{1,5},{2,6},{3,7},{4,0},{5,1},{6,2},{7,3},{8,12},{9,13},{10,... | collective-permute-start | bytes 884744 | tf_op jit(solution)/shard_map/ppermute | solution.py:95
  820.7 40.5 %collective-permute-start.135 = (bf16[4,96,2304]{2,1,0:T(8,128)(2,1)S(1)}, bf16[4,96,2304]{2,1,0:T(8,128)(2,1)S(1)}, u32[]{:S(2)}, u32[]{:S(2)}) collective-permute-start(bf16[4,96,2304]{2,1,0:T(8,128)(2,1)S(1)} %dynamic-slice_bitcast_fusion.1), channel_id=1, source_target_pairs={{0,1},{1,0},{2,3},{3,2},{4,5},{5,4},{6,7},{7,6},{8,9},{9,8},{10,11... | collective-permute-start | bytes 5308424 | tf_op jit(solution)/shard_map/ppermute | solution.py:92
  838.6 26.6 %collective-permute-start.94 = (bf16[96,1536]{1,0:T(8,128)(2,1)S(1)}, bf16[96,1536]{1,0:T(8,128)(2,1)S(1)}, u32[]{:S(2)}, u32[]{:S(2)}) collective-permute-start(bf16[96,1536]{1,0:T(8,128)(2,1)S(1)} %get-tuple-element.235), channel_id=1, source_target_pairs={{0,6},{1,7},{2,4},{3,5},{4,2},{5,3},{6,0},{7,1},{8,14},{9,15},{10,... | collective-permute-start | bytes 884744 | tf_op jit(solution)/shard_map/ppermute | solution.py:95
  840.7 31.6 %collective-permute-start.93 = (bf16[96,1536]{1,0:T(8,128)(2,1)S(1)}, bf16[96,1536]{1,0:T(8,128)(2,1)S(1)}, u32[]{:S(2)}, u32[]{:S(2)}) collective-permute-start(bf16[96,1536]{1,0:T(8,128)(2,1)S(1)} %get-tuple-element.236), channel_id=1, source_target_pairs={{0,4},{1,5},{2,6},{3,7},{4,0},{5,1},{6,2},{7,3},{8,12},{9,13},{10,... | collective-permute-start | bytes 884744 | tf_op jit(solution)/shard_map/ppermute | solution.py:95
  861.8 26.7 %collective-permute-start.136 = (bf16[96,2304]{1,0:T(8,128)(2,1)S(1)}, bf16[96,2304]{1,0:T(8,128)(2,1)S(1)}, u32[]{:S(2)}, u32[]{:S(2)}) collective-permute-start(bf16[96,2304]{1,0:T(8,128)(2,1)S(1)} %get-tuple-element.209), channel_id=1, source_target_pairs={{0,2},{1,3},{2,0},{3,1},{4,6},{5,7},{6,4},{7,5},{8,10},{9,11},{10,... | collective-permute-start | bytes 1327112 | tf_op jit(solution)/shard_map/ppermute | solution.py:95
  863.1 25.4 %collective-permute-start.138 = (bf16[96,2304]{1,0:T(8,128)(2,1)S(1)}, bf16[96,2304]{1,0:T(8,128)(2,1)S(1)}, u32[]{:S(2)}, u32[]{:S(2)}) collective-permute-start(bf16[96,2304]{1,0:T(8,128)(2,1)S(1)} %get-tuple-element.210), channel_id=1, source_target_pairs={{0,6},{1,7},{2,4},{3,5},{4,2},{5,3},{6,0},{7,1},{8,14},{9,15},{10,... | collective-permute-start | bytes 1327112 | tf_op jit(solution)/shard_map/ppermute | solution.py:95
  865.2 43.4 %collective-permute-start.137 = (bf16[96,2304]{1,0:T(8,128)(2,1)S(1)}, bf16[96,2304]{1,0:T(8,128)(2,1)S(1)}, u32[]{:S(2)}, u32[]{:S(2)}) collective-permute-start(bf16[96,2304]{1,0:T(8,128)(2,1)S(1)} %get-tuple-element.211), channel_id=1, source_target_pairs={{0,4},{1,5},{2,6},{3,7},{4,0},{5,1},{6,2},{7,3},{8,12},{9,13},{10,... | collective-permute-start | bytes 1327112 | tf_op jit(solution)/shard_map/ppermute | solution.py:95
  872.4 37.6 %collective-permute-start.95 = (bf16[96,1536]{1,0:T(8,128)(2,1)S(1)}, bf16[96,1536]{1,0:T(8,128)(2,1)S(1)}, u32[]{:S(2)}, u32[]{:S(2)}) collective-permute-start(bf16[96,1536]{1,0:T(8,128)(2,1)S(1)} %fusion.152), channel_id=1, source_target_pairs={{0,16},{8,24},{16,0},{24,8},{1,17},{9,25},{17,1},{25,9},{2,18},{10... | collective-permute-start | bytes 884744 | tf_op jit(solution)/shard_map/ppermute | solution.py:84
  873.5 36.6 %collective-permute-start.103 = (bf16[384,384]{1,0:T(8,128)(2,1)S(1)}, bf16[384,384]{1,0:T(8,128)(2,1)S(1)}, u32[]{:S(2)}, u32[]{:S(2)}) collective-permute-start(bf16[384,384]{1,0:T(8,128)(2,1)S(1)} %add_convert_fusion.13), channel_id=1, source_target_pairs={{0,8},{8,0},{16,24},{24,16},{1,9},{9,1},{17,25},{25,17},{2,10},{10... | collective-permute-start | bytes 884744 | tf_op jit(solution)/shard_map/ppermute | solution.py:81
  (404 other events, 3363.9 us)
